TPU v7x, 512 devices: a whole 4x8x8 slice. The times are simulated.
512 devices in a mesh: pa: 8 (over y), pb: 64 (over z, x, core).
Axes of the slice: x: 4, y: 8, z: 8, core: 2. Of those that a mesh axis runs over, the one named last changes fastest.
Arguments:
- matrix: bfloat16 [12288, 24576], P('pa', 'pb'), may hold values from -6 to 6
- panels: bfloat16 [6, 12288, 128], P(None, ('pa', 'pb')), may hold values from -0.25 to 0.25
- inverses: float32 [6, 128, 128], replicated, as said below
- pivots: int32 [6, 128], replicated, may hold values from 128 to 12287, as said below
Outputs:
- factored: bfloat16 [12288, 24576], P('pa', 'pb')
Inputs may be any that keep to these rules, and one draw needn't show every extreme that they name: `pivots`: row k lists 128 different row numbers, each at least (k + 1) * 128. `inverses`: each block is unit lower triangular.
All inputs are finite; a program needn't handle non-finite values.
Results may differ from a plain program's by a relative error of at most 0.0082.
Values may be sent and summed in bfloat16 or wider, within the bound.
No kernel may reach another device: no remote copies, remote signals or barrier semaphores. Data moves between devices by JAX's collectives and lax.ppermute only.
A program may use at most 64 MiB of HBM per device.

v0:
```python
import jax
import jax.numpy as jnp
from jax import lax
from jax.sharding import PartitionSpec as P

NB = 128
STEPS = 6


def broadcast(x, axis, root):
    mine = lax.axis_index(axis) == root
    return lax.psum(jnp.where(mine, x, jnp.zeros_like(x)), axis)


def per_device(matrix, panels, inverses, pivots):
    local_rows = matrix.shape[0]
    proc_row = lax.axis_index("pa")
    first_row = proc_row * local_rows
    is_owner = proc_row == 0
    global_rows = first_row + jnp.arange(local_rows, dtype=jnp.int32)
    for step in range(STEPS):
        lo = step * NB
        hi = lo + NB
        chosen = pivots[step]
        local_idx = chosen - first_row
        owned = (local_idx >= 0) & (local_idx < local_rows)
        safe_idx = jnp.clip(local_idx, 0, local_rows - 1)
        candidates = jnp.where(
            owned[:, None], jnp.take(matrix, safe_idx, axis=0), jnp.zeros((), jnp.bfloat16)
        )
        top_local = matrix[lo:hi]
        new_top = lax.psum(candidates, "pa").astype(jnp.float32).astype(jnp.bfloat16)
        upper_here = jnp.dot(
            inverses[step],
            new_top.astype(jnp.float32),
            precision=lax.Precision.HIGHEST,
            preferred_element_type=jnp.float32,
        ).astype(jnp.bfloat16)
        upper, old_top = (broadcast(upper_here, "pa", 0), broadcast(top_local, "pa", 0))
        target = jnp.where(owned, local_idx, local_rows)
        matrix = matrix.at[target].set(old_top, mode="drop")
        product = jnp.dot(
            lax.all_gather(panels[step], "pb", axis=0, tiled=True),
            upper,
            preferred_element_type=jnp.float32,
        )
        updated = (matrix.astype(jnp.float32) - product).astype(jnp.bfloat16)
        matrix = jnp.where((global_rows >= hi)[:, None], updated, matrix)
        matrix = matrix.at[lo:hi].set(jnp.where(is_owner, upper, matrix[lo:hi]))
    return matrix


def solution(mesh):
    in_specs = (P("pa", "pb"), P(None, ("pa", "pb"), None), P(), P())
    out_specs = P("pa", "pb")
    return jax.shard_map(
        per_device, mesh=mesh, in_specs=in_specs, out_specs=out_specs, check_vma=False
    )
```

profile of v0, /device:TPU:6, one launch (start us, length us, event | category | flops | bytes accessed | tf_op | source)
XLA Modules:
  0.0 992.0 jit_solution(16481884863507782826)
XLA Ops:
  15.7 57.2 %all-gather = bf16[1,1536,128]{2,1,0:T(8,128)(2,1)} all-gather(bf16[1,24,128]{2,1,0:T(8,128)(2,1)S(1)} %get-tuple-element.106), channel_id=2, replica_groups=mesh['pa'=8,'pb'=64] {'pb'}, dimensions={1}, use_global_device_ids=true | all-gather | bytes 399360 | tf_op jit(solution)/shard_map/all_gather | solution.py:43
  72.9 19.5 %all-reduce.19.cloned.1.call-done = bf16[128,384]{0,1:T(8,128)(2,1)} async-done(((bf16[128,384]{0,1:T(8,128)(2,1)}), bf16[128,384]{0,1:T(8,128)(2,1)}) %all-reduce.19.cloned.1.call-update) | async-done | bytes 98320 | tf_op jit(solution)/shard_map/psum | solution.py:32
  92.5 1.8 fusion.19
  94.9 75.9 %all-reduce.41.cloned.1.call-done = (bf16[128,384]{0,1:T(8,128)(2,1)}, bf16[128,384]{0,1:T(8,128)(2,1)}) async-done(((bf16[128,384]{0,1:T(8,128)(2,1)}, bf16[128,384]{0,1:T(8,128)(2,1)}), (bf16[128,384]{0,1:T(8,128)(2,1)}, bf16[128,384]{0,1:T(8,128)(2,1)})) %all-reduce.41.cloned.1.call-update) | async-done | bytes 196624 | tf_op jit(solution)/shard_map/psum | solution.py:12
  179.2 75.1 %all-reduce.21.cloned.1.call-done = bf16[128,384]{0,1:T(8,128)(2,1)} async-done(((bf16[128,384]{0,1:T(8,128)(2,1)}), bf16[128,384]{0,1:T(8,128)(2,1)}) %all-reduce.21.cloned.1.call-update) | async-done | bytes 98320 | tf_op jit(solution)/shard_map/psum | solution.py:32
  254.3 1.8 fusion.21
  256.2 53.7 %all-gather.1 = bf16[1,1536,128]{2,1,0:T(8,128)(2,1)} all-gather(bf16[1,24,128]{2,1,0:T(8,128)(2,1)S(1)} %copy-done.9), channel_id=3, replica_groups=mesh['pa'=8,'pb'=64] {'pb'}, dimensions={1}, use_global_device_ids=true | all-gather | bytes 399360 | tf_op jit(solution)/shard_map/all_gather | solution.py:43
  310.5 22.1 %all-reduce.39.cloned.1.call-done = (bf16[128,384]{0,1:T(8,128)(2,1)}, bf16[128,384]{0,1:T(8,128)(2,1)}) async-done(((bf16[128,384]{0,1:T(8,128)(2,1)}, bf16[128,384]{0,1:T(8,128)(2,1)}), (bf16[128,384]{0,1:T(8,128)(2,1)}, bf16[128,384]{0,1:T(8,128)(2,1)})) %all-reduce.39.cloned.1.call-update) | async-done | bytes 196624 | tf_op jit(solution)/shard_map/psum | solution.py:12
  340.9 75.2 %all-reduce.23.cloned.1.call-done = bf16[128,384]{0,1:T(8,128)(2,1)} async-done(((bf16[128,384]{0,1:T(8,128)(2,1)}), bf16[128,384]{0,1:T(8,128)(2,1)}) %all-reduce.23.cloned.1.call-update) | async-done | bytes 98320 | tf_op jit(solution)/shard_map/psum | solution.py:32
  416.1 1.8 fusion.23
  417.9 53.8 %all-gather.2 = bf16[1,1536,128]{2,1,0:T(8,128)(2,1)} all-gather(bf16[1,24,128]{2,1,0:T(8,128)(2,1)S(1)} %copy-done.8), channel_id=4, replica_groups=mesh['pa'=8,'pb'=64] {'pb'}, dimensions={1}, use_global_device_ids=true | all-gather | bytes 399360 | tf_op jit(solution)/shard_map/all_gather | solution.py:43
  472.4 21.9 %all-reduce.37.cloned.1.call-done = (bf16[128,384]{0,1:T(8,128)(2,1)}, bf16[128,384]{0,1:T(8,128)(2,1)}) async-done(((bf16[128,384]{0,1:T(8,128)(2,1)}, bf16[128,384]{0,1:T(8,128)(2,1)}), (bf16[128,384]{0,1:T(8,128)(2,1)}, bf16[128,384]{0,1:T(8,128)(2,1)})) %all-reduce.37.cloned.1.call-update) | async-done | bytes 196624 | tf_op jit(solution)/shard_map/psum | solution.py:12
  502.7 75.2 %all-reduce.25.cloned.1.call-done = bf16[128,384]{0,1:T(8,128)(2,1)} async-done(((bf16[128,384]{0,1:T(8,128)(2,1)}), bf16[128,384]{0,1:T(8,128)(2,1)}) %all-reduce.25.cloned.1.call-update) | async-done | bytes 98320 | tf_op jit(solution)/shard_map/psum | solution.py:32
  577.8 1.8 fusion.25
  579.7 53.7 %all-gather.3 = bf16[1,1536,128]{2,1,0:T(8,128)(2,1)} all-gather(bf16[1,24,128]{2,1,0:T(8,128)(2,1)S(1)} %copy-done.7), channel_id=5, replica_groups=mesh['pa'=8,'pb'=64] {'pb'}, dimensions={1}, use_global_device_ids=true | all-gather | bytes 399360 | tf_op jit(solution)/shard_map/all_gather | solution.py:43
  633.9 22.3 %all-reduce.35.cloned.1.call-done = (bf16[128,384]{0,1:T(8,128)(2,1)}, bf16[128,384]{0,1:T(8,128)(2,1)}) async-done(((bf16[128,384]{0,1:T(8,128)(2,1)}, bf16[128,384]{0,1:T(8,128)(2,1)}), (bf16[128,384]{0,1:T(8,128)(2,1)}, bf16[128,384]{0,1:T(8,128)(2,1)})) %all-reduce.35.cloned.1.call-update) | async-done | bytes 196624 | tf_op jit(solution)/shard_map/psum | solution.py:12
  664.5 75.2 %all-reduce.27.cloned.1.call-done = bf16[128,384]{0,1:T(8,128)(2,1)} async-done(((bf16[128,384]{0,1:T(8,128)(2,1)}), bf16[128,384]{0,1:T(8,128)(2,1)}) %all-reduce.27.cloned.1.call-update) | async-done | bytes 98320 | tf_op jit(solution)/shard_map/psum | solution.py:32
  739.7 1.8 fusion.27
  741.5 53.9 %all-gather.4 = bf16[1,1536,128]{2,1,0:T(8,128)(2,1)} all-gather(bf16[1,24,128]{2,1,0:T(8,128)(2,1)S(1)} %get-tuple-element.107), channel_id=6, replica_groups=mesh['pa'=8,'pb'=64] {'pb'}, dimensions={1}, use_global_device_ids=true | all-gather | bytes 399360 | tf_op jit(solution)/shard_map/all_gather | solution.py:43
  795.4 22.5 %all-reduce.33.cloned.1.call-done = (bf16[128,384]{0,1:T(8,128)(2,1)}, bf16[128,384]{0,1:T(8,128)(2,1)}) async-done(((bf16[128,384]{0,1:T(8,128)(2,1)}, bf16[128,384]{0,1:T(8,128)(2,1)}), (bf16[128,384]{0,1:T(8,128)(2,1)}, bf16[128,384]{0,1:T(8,128)(2,1)})) %all-reduce.33.cloned.1.call-update) | async-done | bytes 196624 | tf_op jit(solution)/shard_map/psum | solution.py:12
  826.2 75.2 %all-reduce.29.cloned.1.call-done = bf16[128,384]{0,1:T(8,128)(2,1)} async-done(((bf16[128,384]{0,1:T(8,128)(2,1)}), bf16[128,384]{0,1:T(8,128)(2,1)}) %all-reduce.29.cloned.1.call-update) | async-done | bytes 98320 | tf_op jit(solution)/shard_map/psum | solution.py:32
  901.3 1.8 fusion.29
  903.1 49.0 %all-gather.5 = bf16[1,1536,128]{2,1,0:T(8,128)(2,1)S(1)} all-gather(bf16[1,24,128]{2,1,0:T(8,128)(2,1)S(1)} %get-tuple-element.102), channel_id=7, replica_groups=mesh['pa'=8,'pb'=64] {'pb'}, dimensions={1}, use_global_device_ids=true | all-gather | bytes 399360 | tf_op jit(solution)/shard_map/all_gather | solution.py:43
  952.2 27.4 %all-reduce.31.cloned.1.call-done = (bf16[128,384]{0,1:T(8,128)(2,1)}, bf16[128,384]{0,1:T(8,128)(2,1)}) async-done(((bf16[128,384]{0,1:T(8,128)(2,1)}, bf16[128,384]{0,1:T(8,128)(2,1)}), (bf16[128,384]{0,1:T(8,128)(2,1)}, bf16[128,384]{0,1:T(8,128)(2,1)})) %all-reduce.31.cloned.1.call-update) | async-done | bytes 196624 | tf_op jit(solution)/shard_map/psum | solution.py:12
  (165 shorter events, 58.4 us)
Async XLA Ops:
  6.5 85.9 %all-reduce.19.cloned.1.call-start = ((), (), s32[]{:S(2)}) async-start(), calls=%async_computation | async-start | bytes 196608 | tf_op jit(solution)/shard_map/psum | solution.py:32
  10.7 160.1 %all-reduce.41.cloned.1.call-start = ((), (), s32[]{:S(2)}) async-start(), calls=%async_computation.11 | async-start | bytes 393216 | tf_op jit(solution)/shard_map/psum | solution.py:12
  94.3 160.1 %all-reduce.21.cloned.1.call-start = ((), (), s32[]{:S(2)}) async-start(), calls=%async_computation.1 | async-start | bytes 196608 | tf_op jit(solution)/shard_map/psum | solution.py:32
  176.7 79.5 %copy-start.9 = (bf16[1,24,128]{2,1,0:T(8,128)(2,1)S(1)}, bf16[1,24,128]{2,1,0:T(8,128)(2,1)}, u32[]{:S(2)}) copy-start(bf16[1,24,128]{2,1,0:T(8,128)(2,1)} %get-tuple-element.105) | copy-start | bytes 18436
  176.7 133.2 %copy-start.30 = (s32[128]{0:T(128)S(1)}, s32[128]{0:T(128)}, u32[]{:S(2)}) copy-start(s32[128]{0:T(128)} %get-tuple-element.119) | copy-start | bytes 1540
  176.7 156.9 %copy-start.26 = (s32[128]{0:T(128)S(1)}, s32[128]{0:T(128)}, u32[]{:S(2)}) copy-start(s32[128]{0:T(128)} %get-tuple-element.125) | copy-start | bytes 1540
  178.5 154.1 %all-reduce.39.cloned.1.call-start = ((), (), s32[]{:S(2)}) async-start(), calls=%async_computation.10 | async-start | bytes 393216 | tf_op jit(solution)/shard_map/psum | solution.py:12
  256.1 159.9 %all-reduce.23.cloned.1.call-start = ((), (), s32[]{:S(2)}) async-start(), calls=%async_computation.2 | async-start | bytes 196608 | tf_op jit(solution)/shard_map/psum | solution.py:32
  338.4 79.5 %copy-start.8 = (bf16[1,24,128]{2,1,0:T(8,128)(2,1)S(1)}, bf16[1,24,128]{2,1,0:T(8,128)(2,1)}, u32[]{:S(2)}) copy-start(bf16[1,24,128]{2,1,0:T(8,128)(2,1)} %get-tuple-element.104) | copy-start | bytes 18436
  338.4 133.4 %copy-start.29 = (s32[128]{0:T(128)S(1)}, s32[128]{0:T(128)}, u32[]{:S(2)}) copy-start(s32[128]{0:T(128)} %get-tuple-element.117) | copy-start | bytes 1540
  338.4 156.9 %copy-start.24 = (s32[128]{0:T(128)S(1)}, s32[128]{0:T(128)}, u32[]{:S(2)}) copy-start(s32[128]{0:T(128)} %get-tuple-element.126) | copy-start | bytes 1540
  340.2 154.1 %all-reduce.37.cloned.1.call-start = ((), (), s32[]{:S(2)}) async-start(), calls=%async_computation.9 | async-start | bytes 393216 | tf_op jit(solution)/shard_map/psum | solution.py:12
  417.9 159.9 %all-reduce.25.cloned.1.call-start = ((), (), s32[]{:S(2)}) async-start(), calls=%async_computation.3 | async-start | bytes 196608 | tf_op jit(solution)/shard_map/psum | solution.py:32
  500.1 79.5 %copy-start.7 = (bf16[1,24,128]{2,1,0:T(8,128)(2,1)S(1)}, bf16[1,24,128]{2,1,0:T(8,128)(2,1)}, u32[]{:S(2)}) copy-start(bf16[1,24,128]{2,1,0:T(8,128)(2,1)} %get-tuple-element.103) | copy-start | bytes 18436
  500.1 133.2 %copy-start.28 = (s32[128]{0:T(128)S(1)}, s32[128]{0:T(128)}, u32[]{:S(2)}) copy-start(s32[128]{0:T(128)} %get-tuple-element.115) | copy-start | bytes 1540
  500.1 157.1 %copy-start.22 = (s32[128]{0:T(128)S(1)}, s32[128]{0:T(128)}, u32[]{:S(2)}) copy-start(s32[128]{0:T(128)} %get-tuple-element.127) | copy-start | bytes 1540
  502.0 154.2 %all-reduce.35.cloned.1.call-start = ((), (), s32[]{:S(2)}) async-start(), calls=%async_computation.8 | async-start | bytes 393216 | tf_op jit(solution)/shard_map/psum | solution.py:12
  579.6 160.1 %all-reduce.27.cloned.1.call-start = ((), (), s32[]{:S(2)}) async-start(), calls=%async_computation.4 | async-start | bytes 196608 | tf_op jit(solution)/shard_map/psum | solution.py:32
  662.0 133.4 %copy-start.27 = (s32[128]{0:T(128)S(1)}, s32[128]{0:T(128)}, u32[]{:S(2)}) copy-start(s32[128]{0:T(128)} %get-tuple-element.91) | copy-start | bytes 1540
  662.0 156.9 %copy-start.20 = (s32[128]{0:T(128)S(1)}, s32[128]{0:T(128)}, u32[]{:S(2)}) copy-start(s32[128]{0:T(128)} %get-tuple-element.128) | copy-start | bytes 1540
  663.8 154.1 %all-reduce.33.cloned.1.call-start = ((), (), s32[]{:S(2)}) async-start(), calls=%async_computation.7 | async-start | bytes 393216 | tf_op jit(solution)/shard_map/psum | solution.py:12
  741.5 159.8 %all-reduce.29.cloned.1.call-start = ((), (), s32[]{:S(2)}) async-start(), calls=%async_computation.5 | async-start | bytes 196608 | tf_op jit(solution)/shard_map/psum | solution.py:32
  823.8 156.8 %copy-start.18 = (s32[128]{0:T(128)S(1)}, s32[128]{0:T(128)}, u32[]{:S(2)}) copy-start(s32[128]{0:T(128)} %get-tuple-element.124) | copy-start | bytes 1540
  825.5 154.1 %all-reduce.31.cloned.1.call-start = ((), (), s32[]{:S(2)}) async-start(), calls=%async_computation.6 | async-start | bytes 393216 | tf_op jit(solution)/shard_map/psum | solution.py:12
  (19 other events, 34.8 us)
Sparse Core Ops, SparseCore 0:
  10.8 81.5 all-reduce.18
  94.9 75.9 all-reduce.40
  178.6 75.6 all-reduce.20
  256.6 75.9 all-reduce.38
  340.3 75.6 all-reduce.22
  418.4 75.9 all-reduce.36
  502.1 75.6 all-reduce.24
  580.3 75.9 all-reduce.34
  664.0 75.6 all-reduce.26
  742.0 75.9 all-reduce.32
  825.6 75.6 all-reduce.28
  903.6 75.9 all-reduce.30
where the time goes:
time: 993 us; the launch traced here: 992 us
  waiting for transfers between devices  588 us (59%)
  blocking collectives  321 us (32%)
  local copies, waits for them, and re-layouts  34.2 us (3%)
  matrix products  18.7 us (2%)
  other arithmetic  15.4 us (2%)
  between operations  14.3 us (1%)
    psum x6, waiting for transfers between devices, per_device(): lax.psum(candidates, 'pa').astype(jnp.float32).astype(jnp.bfloat16)  395 us
    all_gather x6, blocking collectives, per_device(): lax.all_gather(panels[step], 'pb', axis=0, tiled=True)  321 us
    psum x6, waiting for transfers between devices, broadcast(): return lax.psum(jnp.where(mine, x, jnp.zeros_like(x)), axis)  192 us
  transfers between devices with their start and end apart: 12, of which 12 were waited for; matrix products, arithmetic and copies ran while one was open for 1% of the time, Pallas kernels for 0%

commit v1 on v0

v1 whole, which is shorter than its diff:
```python
import functools

import jax
import jax.numpy as jnp
from jax import lax
from jax.experimental import pallas as pl
from jax.experimental.pallas import tpu as pltpu
from jax.sharding import Mesh
from jax.sharding import PartitionSpec as P

NB = 128
STEPS = 6
TOP = NB * STEPS
PAIRS = [(k, j) for k in range(1, STEPS) for j in range(k)]
CHUNK = 64
BF = jnp.bfloat16
F32 = jnp.float32
VM = pl.BlockSpec(memory_space=pltpu.VMEM)
SM = pl.BlockSpec(memory_space=pltpu.SMEM)
ANY = pl.BlockSpec(memory_space=pl.ANY)


def start_of(k):
    return 2 * NB * (k * (k - 1) // 2)


def iota(shape, dim):
    return lax.broadcasted_iota(jnp.int32, shape, dim)


def prep_kernel(first_ref, rows_ref, cols_ref, matrix_ref, picked_ref, tops_ref, select_ref):
    first = first_ref[0]
    ones = jnp.ones((NB, NB), BF)
    local = matrix_ref.shape[0]
    for k in range(STEPS):
        ids = jnp.concatenate([iota((NB, NB), 0) + k * NB, jnp.broadcast_to(cols_ref[k * NB:(k + 1) * NB, :], (NB, NB))])
        found = jnp.zeros((2 * NB, NB), F32)
        for j in reversed(range(k)):
            at = start_of(k) + 2 * NB * j
            same = jnp.where(ids == rows_ref[j:j + 1, :], 1.0, 0.0).astype(F32)
            live = 1.0 - found
            select_ref[:, at:at + NB] = (same * live).astype(BF)
            select_ref[:, at + NB:at + 2 * NB] = (-live).astype(BF)
            hit = jnp.dot(same.astype(BF), ones, preferred_element_type=F32)
            found = jnp.maximum(found, hit)
        fresh = found < 0.5
        where = cols_ref[k * NB:(k + 1) * NB, :] - first
        hot = jnp.where(iota((NB, local), 1) == where, 1.0, 0.0).astype(BF)
        row = jnp.dot(hot, matrix_ref[...], preferred_element_type=F32)
        for c in range(0, row.shape[1], NB):
            picked_ref[k * NB:(k + 1) * NB, c:c + NB] = jnp.where(fresh[NB:], row[:, c:c + NB], 0.0).astype(BF)
            mine = fresh[:NB] & (iota((NB, NB), 0) + first < TOP)
            top = matrix_ref[k * NB:(k + 1) * NB, c:c + NB].astype(F32)
            tops_ref[k * NB:(k + 1) * NB, c:c + NB] = jnp.where(mine, top, 0.0).astype(BF)


def rows_kernel(first_ref, rows_ref, panels_ref, matrix_ref, factor_ref, kept_ref):
    ones = jnp.ones((NB, NB), BF)
    height = 2 * NB

    def one(step, carry):
        at = pl.multiple_of(step * height, height)
        ids = iota((height, NB), 0) + first_ref[0] + at
        is_top = ids < TOP
        found = jnp.zeros((height, NB), F32)
        for j in reversed(range(STEPS)):
            same = jnp.where((ids == rows_ref[j:j + 1, :]) & ~is_top, 1.0, 0.0).astype(F32)
            live = 1.0 - found
            factor_ref[pl.ds(at, height), 2 * NB * j:2 * NB * j + NB] = (same * live).astype(BF)
            diag = jnp.where(ids - NB * j == iota((height, NB), 1), 1.0, 0.0).astype(F32)
            lower = -live * panels_ref[j, pl.ds(at, height), :].astype(F32)
            factor_ref[pl.ds(at, height), 2 * NB * j + NB:2 * NB * (j + 1)] = jnp.where(is_top, diag, lower).astype(BF)
            hit = jnp.dot(same.astype(BF), ones, preferred_element_type=F32)
            found = jnp.maximum(found, hit)
        fresh = (found < 0.5) & ~is_top
        for c in range(0, matrix_ref.shape[1], NB):
            old = matrix_ref[pl.ds(at, height), c:c + NB].astype(F32)
            kept_ref[pl.ds(at, height), c:c + NB] = jnp.where(fresh, old, 0.0).astype(BF)
        return carry

    lax.fori_loop(0, matrix_ref.shape[0] // height, one, 0)


def solve_kernel(core_ref, content_ref, mine_ref, other_ref, inverses_ref, select_ref, factor_hbm, kept_hbm, out_ref,
                 low, coef, state, factor, kept, sems):
    loads = [pltpu.make_async_copy(factor_hbm, factor, sems.at[0]), pltpu.make_async_copy(kept_hbm, kept, sems.at[1])]
    for load in loads:
        load.start()
    half = low.shape[1]
    core = core_ref[0]
    low[core] = mine_ref[...].reshape(half, NB)
    low[1 - core] = other_ref[...].reshape(half, NB)
    parts, each = content_ref.shape[0], content_ref.shape[1] // 2
    width = content_ref.shape[2]
    picked, tops = [], []
    contents = content_ref[:, :each, :].reshape(parts * each, width)
    displaced = content_ref[:, each:, :].reshape(parts * each, width)
    for k in range(STEPS):
        x = jnp.concatenate([displaced[k * NB:(k + 1) * NB], contents[k * NB:(k + 1) * NB]]).astype(F32)
        if k:
            for j in range(k):
                at = start_of(k) + 2 * NB * j
                t = 2 * PAIRS.index((k, j))
                b0, b1 = t * NB, (t + 1) * NB
                block = jnp.concatenate([low[b1 // half, b1 % half:b1 % half + NB, :], low[b0 // half, b0 % half:b0 % half + NB, :]])
                coef[:, 2 * NB * j:2 * NB * j + NB] = select_ref[:, at:at + NB]
                coef[:, 2 * NB * j + NB:2 * NB * (j + 1)] = select_ref[:, at + NB:at + 2 * NB] * block
            x = x + jnp.dot(coef[:, :2 * NB * k], state[:2 * NB * k, :], preferred_element_type=F32)
        y = x.astype(BF)
        state[2 * NB * k:2 * NB * k + NB, :] = y[:NB]
        inv = inverses_ref[k]
        hi = inv.astype(BF)
        rest = inv - hi.astype(F32)
        mid = rest.astype(BF)
        lo = (rest - mid.astype(F32)).astype(BF)
        v = y[NB:]
        upper = jnp.dot(hi, v, preferred_element_type=F32) + (
            jnp.dot(mid, v, preferred_element_type=F32) + jnp.dot(lo, v, preferred_element_type=F32))
        state[2 * NB * k + NB:2 * NB * (k + 1), :] = upper.astype(BF)
    for load in loads:
        load.wait()

    def one(step, carry):
        at = pl.multiple_of(step * 2 * NB, 2 * NB)
        new = jnp.dot(factor[pl.ds(at, 2 * NB), :], state[...], preferred_element_type=F32)
        out_ref[pl.ds(at, 2 * NB), :] = (kept[pl.ds(at, 2 * NB), :].astype(F32) + new).astype(BF)
        return carry

    lax.fori_loop(0, out_ref.shape[0] // (2 * NB), one, 0)


def cost(flops, nbytes):
    return pl.CostEstimate(flops=flops, bytes_accessed=nbytes, transcendentals=0)


def spread(x, axes, parts):
    return lax.all_to_all(jnp.broadcast_to(x[None], (parts,) + x.shape), axes, 0, 0, tiled=True)


def per_device(ny, nzx, nc, matrix, panels, inverses, pivots):
    local, width = matrix.shape
    held = panels.shape[1]
    y, core = lax.axis_index("y"), lax.axis_index("c")
    zx = lax.axis_index(("z", "x"))
    first = y * local
    swap = [(0, 1), (1, 0)]
    first1 = first.reshape(1).astype(jnp.int32)
    core1 = core.reshape(1).astype(jnp.int32)

    mine = spread(panels.reshape(STEPS * held, NB), ("z", "x"), nzx)
    other = lax.ppermute(mine, "c", swap)
    mine, other = (a.reshape(nzx, STEPS, held, NB) for a in (mine, other))
    both = jnp.stack([jnp.where(core == 0, mine, other), jnp.where(core == 0, other, mine)], axis=1)
    full = both.transpose(2, 0, 1, 3, 4).reshape(STEPS, local, NB)

    picked, tops, select = pl.pallas_call(
        prep_kernel,
        out_shape=(
            jax.ShapeDtypeStruct((TOP, width), BF),
            jax.ShapeDtypeStruct((TOP, width), BF),
            jax.ShapeDtypeStruct((2 * NB, start_of(STEPS)), BF),
        ),
        in_specs=[SM, VM, VM, VM],
        out_specs=(VM, VM, VM),
        cost_estimate=cost(2 * TOP * local * width, 8 << 20),
    )(first1, pivots, pivots.reshape(TOP, 1), matrix)
    share = jnp.concatenate([picked.reshape(ny, TOP // ny, width), tops.reshape(ny, TOP // ny, width)], axis=1)
    got = lax.all_to_all(share, "y", 0, 0, tiled=True)
    content = spread(got.astype(F32).sum(0).astype(BF), "y", ny)

    idx = []
    for k, j in PAIRS:
        for rows in (pivots[k], k * NB + jnp.arange(NB, dtype=jnp.int32)):
            here = rows - first
            idx.append(jnp.where((here >= 0) & (here < local), here + j * local, -1))
    per_dev = len(idx) * NB // (nzx * nc)
    chunk = -(-per_dev // CHUNK) * CHUNK
    idx = jnp.concatenate(idx + [jnp.full((chunk * nzx * nc - len(idx) * NB,), -1, jnp.int32)])
    idx = lax.dynamic_slice(idx, ((core * nzx + zx) * chunk,), (chunk,))
    part = jnp.take(full.reshape(STEPS * local, NB), jnp.maximum(idx, 0), axis=0)
    part = jnp.where((idx >= 0)[:, None], part, jnp.zeros((), BF))
    part = spread(part, "y", ny).astype(F32).reshape(ny, chunk, NB).sum(0).astype(BF)
    low_mine = spread(part, ("z", "x"), nzx)
    low_other = lax.ppermute(low_mine, "c", swap)

    factor, kept = pl.pallas_call(
        rows_kernel,
        out_shape=(jax.ShapeDtypeStruct((local, 2 * TOP), BF), jax.ShapeDtypeStruct((local, width), BF)),
        in_specs=[SM, VM, VM, VM],
        out_specs=(VM, VM),
        cost_estimate=cost(2 * TOP * local * NB, 12 << 20),
    )(first1, pivots, full, matrix)

    return pl.pallas_call(
        solve_kernel,
        out_shape=jax.ShapeDtypeStruct((local, width), BF),
        in_specs=[SM, VM, VM, VM, VM, VM, ANY, ANY],
        out_specs=VM,
        scratch_shapes=[
            pltpu.VMEM((2, nzx * chunk, NB), BF),
            pltpu.VMEM((2 * NB, 2 * NB * (STEPS - 1)), BF),
            pltpu.VMEM((2 * TOP, width), BF),
            pltpu.VMEM((local, 2 * TOP), BF),
            pltpu.VMEM((local, width), BF),
            pltpu.SemaphoreType.DMA((2,)),
        ],
        cost_estimate=cost(4 * TOP * local * width, 16 << 20),
    )(core1, content.reshape(ny, 2 * TOP // ny, width), low_mine.reshape(nzx, chunk, NB), low_other.reshape(nzx, chunk, NB),
      inverses, select, factor, kept)


def solution(mesh):
    ny, npb = mesh.devices.shape
    nz, nx, nc = (8, 4, 2) if npb == 64 else (1, npb // 2, 2)
    fine = Mesh(mesh.devices.reshape(ny, nz, nx, nc), ("y", "z", "x", "c"))
    cols = ("z", "x", "c")
    in_specs = (P("y", cols), P(None, ("y",) + cols, None), P(), P())
    return jax.shard_map(
        functools.partial(per_device, ny, nz * nx, nc), mesh=fine, in_specs=in_specs, out_specs=P("y", cols), check_vma=False
    )
```

time: 993 us -> 179 us (0.18)
  waiting for transfers between devices: 588 us -> 103 us
  blocking collectives: 321 us -> 0 us
  starting transfers between devices: 0.46 us -> 39.8 us
  local copies, waits for them, and re-layouts: 34.2 us -> 7.99 us
  Pallas kernels: 0 us -> 22.1 us
  matrix products: 18.7 us -> 0 us
  between operations: 14.3 us -> 0.35 us
  other arithmetic: 15.4 us -> 3.4 us
    psum x12 -> x0, waiting for transfers between devices: 587 us -> none  [the longest x6 395 us: per_device(): lax.psum(candidates, 'pa').astype(jnp.float32).astype(jnp.bfloat16)]
    all_gather x6 -> x0, blocking collectives: 321 us -> none  [per_device(): lax.all_gather(panels[step], 'pb', axis=0, tiled=True)]
    all_to_all x0 -> x5, waiting for transfers between devices: none -> 101 us  [the longest x4 69.3 us: spread(): lax.all_to_all(jnp.broadcast_to(x[None], (parts,) + x.shape), axes, 0, 0,...]
    all_to_all x0 -> x5, starting transfers between devices: none -> 36 us  [the longest x4 29.8 us: spread(): lax.all_to_all(jnp.broadcast_to(x[None], (parts,) + x.shape), axes, 0, 0,...]
    pallas_call x0 -> x3, Pallas kernels: none -> 22.1 us  [the longest x1 9.52 us: per_device(): pl.pallas_call(solve_kernel, out_shape=jax.ShapeDtypeStruct((local, width...]
    scatter x18 -> x0, local copies, waits for them, and re-layouts: 19.4 us -> none  [the longest x12 14.3 us: per_device(): matrix = matrix.at[target].set(old_top, mode='drop')]
    dot_general x12 -> x0, matrix products: 18.7 us -> none  [the longest x6 10.7 us: per_device(): jnp.dot(inverses[step], new_top.astype(jnp.float32), precision=lax.Precis...]
  transfers between devices with their start and end apart: 12 -> 7, of which waited for: 12 -> 6; matrix products, arithmetic and copies ran while one was open for 1% -> 2% of each run, Pallas kernels for 0% -> 7%
where the time goes in v1:
time: 179 us; the launch traced here: 177 us
  waiting for transfers between devices  103 us (58%)
  starting transfers between devices  39.8 us (22%)
  Pallas kernels  22.1 us (12%)
  local copies, waits for them, and re-layouts  7.99 us (4%)
  other arithmetic  3.4 us (2%)
    all_to_all x4, waiting for transfers between devices, spread(): lax.all_to_all(jnp.broadcast_to(x[None], (parts,) + x.shape), axes, 0, 0,...  69.3 us
    all_to_all x1, waiting for transfers between devices, per_device(): got = lax.all_to_all(share, 'y', 0, 0, tiled=True)  31.3 us
    all_to_all x4, starting transfers between devices, spread(): lax.all_to_all(jnp.broadcast_to(x[None], (parts,) + x.shape), axes, 0, 0,...  29.8 us
    pallas_call x1, Pallas kernels, per_device(): pl.pallas_call(solve_kernel, out_shape=jax.ShapeDtypeStruct((local, width...  9.52 us
    pallas_call x1, Pallas kernels, per_device(): pl.pallas_call(rows_kernel, out_shape=(jax.ShapeDtypeStruct((local, 2 * T...  7.55 us
    all_to_all x1, starting transfers between devices, per_device(): got = lax.all_to_all(share, 'y', 0, 0, tiled=True)  6.22 us
    pallas_call x1, Pallas kernels, per_device(): pl.pallas_call(prep_kernel, out_shape=(jax.ShapeDtypeStruct((TOP, width),...  5.05 us
    broadcast_in_dim x4, local copies, waits for them, and re-layouts, spread(): jnp.broadcast_to(x[None], (parts,) + x.shape)  4.76 us
  transfers between devices with their start and end apart: 7, of which 6 were waited for; matrix products, arithmetic and copies ran while one was open for 2% of the time, Pallas kernels for 7%

profile of v1, /device:TPU:6, one launch (start us, length us, event | category | flops | bytes accessed | tf_op | source)
XLA Modules:
  0.0 176.8 jit_solution(11960135938346587165)
XLA Ops:
  0.0 1.9 %broadcast_in_dim.92 = bf16[32,144,128]{2,1,0:T(8,128)(2,1)} broadcast(bf16[144,128]{1,0:T(8,128)(2,1)} %bitcast.124), dimensions={1,2} | broadcast | bytes 1216512 | tf_op jit(solution)/shard_map/broadcast_in_dim | solution.py:137
  1.9 13.5 %all-to-all-start.2 = ((bf16[32,144,128]{2,1,0:T(8,128)(2,1)}), bf16[32,144,128]{2,1,0:T(8,128)(2,1)S(1)}, u32[]{:S(2)}, u32[]{:S(2)}) async-start(bf16[32,144,128]{2,1,0:T(8,128)(2,1)} %broadcast_in_dim.92), calls=%async_computation.2 | async-start | bytes 2359296 | tf_op jit(solution)/shard_map/all_to_all | solution.py:137
  15.9 30.5 %all-to-all-done.2 = bf16[32,144,128]{2,1,0:T(8,128)(2,1)S(1)} async-done(((bf16[32,144,128]{2,1,0:T(8,128)(2,1)}), bf16[32,144,128]{2,1,0:T(8,128)(2,1)S(1)}, u32[]{:S(2)}, u32[]{:S(2)}) %all-to-all-start.2) | async-done | bytes 1179680 | tf_op jit(solution)/shard_map/all_to_all | solution.py:137
  46.4 1.9 %collective-permute-start = (bf16[32,144,128]{2,1,0:T(8,128)(2,1)S(1)}, bf16[32,144,128]{2,1,0:T(8,128)(2,1)S(1)}, u32[]{:S(2)}, u32[]{:S(2)}) collective-permute-start(bf16[32,144,128]{2,1,0:T(8,128)(2,1)S(1)} %all-to-all-done.2), channel_id=1, source_target_pairs={{0,1},{1,0},{2,3},{3,2},{4,5},{5,4},{6,7},{7,6},{8,9},{9,8},{10,11... | collective-permute-start | bytes 3538952 | tf_op jit(solution)/shard_map/ppermute | solution.py:151
  48.5 2.6 %collective-permute-done = bf16[32,144,128]{2,1,0:T(8,128)(2,1)S(1)} collective-permute-done((bf16[32,144,128]{2,1,0:T(8,128)(2,1)S(1)}, bf16[32,144,128]{2,1,0:T(8,128)(2,1)S(1)}, u32[]{:S(2)}, u32[]{:S(2)}) %collective-permute-start) | collective-permute-done | bytes 1179680 | tf_op jit(solution)/shard_map/ppermute | solution.py:151
  51.9 0.6 gather_fusion
  52.6 0.7 broadcast_in_dim.96
  53.4 7.1 %all-to-all-start.3 = ((bf16[8,64,128]{2,1,0:T(8,128)(2,1)}), bf16[8,64,128]{2,1,0:T(8,128)(2,1)S(1)}, u32[]{:S(2)}, u32[]{:S(2)}) async-start(bf16[8,64,128]{2,1,0:T(8,128)(2,1)} %broadcast_in_dim.96), calls=%async_computation.3 | async-start | bytes 262144 | tf_op jit(solution)/shard_map/all_to_all | solution.py:137
  60.5 0.9 copy.12
  61.4 5.0 %shard_map.46 = (bf16[768,384]{1,0:T(8,128)(2,1)}, bf16[768,384]{1,0:T(8,128)(2,1)}, bf16[256,3840]{1,0:T(8,128)(2,1)}) custom-call(s32[1]{0:T(128)} %bitcast.1.first_ref, s32[6,128]{1,0:T(8,128)} %rows_ref.3, s32[768,1]{1,0:T(8,128)} %bitcast.123, bf16[1536,384]{1,0:T(8,128)(2,1)} %matrix_ref.3), custom_call_target="tpu_custom_call" | custom-call | flops 905969664 | bytes 8388608 | tf_op jit(solution)/shard_map/pallas_call | solution.py:156
  66.5 2.4 %pad_maximum_fusion = bf16[8,192,384]{2,1,0:T(8,128)(2,1)} fusion(bf16[8,96,384]{2,1,0:T(8,128)(2,1)} %bitcast.122, bf16[8,96,384]{2,1,0:T(8,128)(2,1)} %bitcast.121), kind=kLoop, calls=%fused_computation.2 | loop fusion | flops 2359296 | bytes 2359296 | tf_op jit(solution)/shard_map/concatenate | solution.py:167
  68.8 1.0 all-to-all-done.3
  69.8 6.2 %all-to-all-start = ((bf16[8,192,384]{2,1,0:T(8,128)(2,1)}), bf16[8,192,384]{2,1,0:T(8,128)(2,1)S(1)}, u32[]{:S(2)}, u32[]{:S(2)}) async-start(bf16[8,192,384]{2,1,0:T(8,128)(2,1)} %pad_maximum_fusion), calls=%async_computation | async-start | bytes 2359296 | tf_op jit(solution)/shard_map/all_to_all | solution.py:168
  76.1 31.3 %all-to-all-done = bf16[8,192,384]{2,1,0:T(8,128)(2,1)S(1)} async-done(((bf16[8,192,384]{2,1,0:T(8,128)(2,1)}), bf16[8,192,384]{2,1,0:T(8,128)(2,1)S(1)}, u32[]{:S(2)}, u32[]{:S(2)}) %all-to-all-start) | async-done | bytes 1179680 | tf_op jit(solution)/shard_map/all_to_all | solution.py:168
  107.3 0.9 broadcast_in_dim.97
  108.2 5.6 %all-to-all-start.4 = ((bf16[32,64,128]{2,1,0:T(8,128)(2,1)}), bf16[32,64,128]{2,1,0:T(8,128)(2,1)S(1)}, u32[]{:S(2)}, u32[]{:S(2)}) async-start(bf16[32,64,128]{2,1,0:T(8,128)(2,1)} %broadcast_in_dim.97), calls=%async_computation.4 | async-start | bytes 1048576 | tf_op jit(solution)/shard_map/all_to_all | solution.py:137
  114.0 16.8 %all-to-all-done.4.mine_ref = bf16[32,64,128]{2,1,0:T(8,128)(2,1)S(1)} async-done(((bf16[32,64,128]{2,1,0:T(8,128)(2,1)}), bf16[32,64,128]{2,1,0:T(8,128)(2,1)S(1)}, u32[]{:S(2)}, u32[]{:S(2)}) %all-to-all-start.4) | async-done | bytes 524320 | tf_op jit(solution)/shard_map/all_to_all | solution.py:137
  130.8 1.2 broadcast_in_dim.86
  132.0 3.6 %all-to-all-start.1 = ((bf16[8,192,384]{2,1,0:T(8,128)(2,1)}), bf16[8,192,384]{2,1,0:T(8,128)(2,1)S(1)}, u32[]{:S(2)}, u32[]{:S(2)}) async-start(bf16[8,192,384]{2,1,0:T(8,128)(2,1)} %broadcast_in_dim.86), calls=%async_computation.1 | async-start | bytes 2359296 | tf_op jit(solution)/shard_map/all_to_all | solution.py:137
  135.6 1.9 %collective-permute-start.1 = (bf16[32,64,128]{2,1,0:T(8,128)(2,1)S(1)}, bf16[32,64,128]{2,1,0:T(8,128)(2,1)S(1)}, u32[]{:S(2)}, u32[]{:S(2)}) collective-permute-start(bf16[32,64,128]{2,1,0:T(8,128)(2,1)S(1)} %all-to-all-done.4.mine_ref), channel_id=1, source_target_pairs={{0,1},{1,0},{2,3},{3,2},{4,5},{5,4},{6,7},{7,6},{8,9},{9,8},{10,11... | collective-permute-start | bytes 1572872 | tf_op jit(solution)/shard_map/ppermute | solution.py:184
  137.5 7.5 %shard_map.47 = (bf16[1536,1536]{1,0:T(8,128)(2,1)}, bf16[1536,384]{1,0:T(8,128)(2,1)}) custom-call(s32[1]{0:T(128)} %bitcast.1.first_ref, s32[6,128]{1,0:T(8,128)} %rows_ref.3, bf16[6,1536,128]{2,1,0:T(8,128)(2,1)} %bitcast.118, bf16[1536,384]{1,0:T(8,128)(2,1)} %matrix_ref.3), custom_call_target="tpu_custom_call" | custom-call | flops 301989888 | bytes 12582912 | tf_op jit(solution)/shard_map/pallas_call | solution.py:186
  145.1 21.0 %all-to-all-done.1.content_ref = bf16[8,192,384]{2,1,0:T(8,128)(2,1)S(1)} async-done(((bf16[8,192,384]{2,1,0:T(8,128)(2,1)}), bf16[8,192,384]{2,1,0:T(8,128)(2,1)S(1)}, u32[]{:S(2)}, u32[]{:S(2)}) %all-to-all-start.1) | async-done | bytes 1179680 | tf_op jit(solution)/shard_map/all_to_all | solution.py:137
  166.1 1.0 copy-done.1
  167.3 9.5 %shard_map.48 = bf16[1536,384]{1,0:T(8,128)(2,1)} custom-call(s32[1]{0:T(128)} %bitcast.core_ref, bf16[8,192,384]{2,1,0:T(8,128)(2,1)} %copy-done.1, bf16[32,64,128]{2,1,0:T(8,128)(2,1)} %copy-done.2, bf16[32,64,128]{2,1,0:T(8,128)(2,1)} %copy-done.3, f32[6,128,128]{2,1,0:T(8,128)} %inverses_ref.1, bf16[256,3840]{1,0:T(8,128)(2,1)} %get-tuple-element.12.select_ref, ...), custom_call_target="tpu_custom_call" | custom-call | flops 1811939328 | bytes 16777216 | tf_op jit(solution)/shard_map/pallas_call | solution.py:194
  (51 shorter events, 1.7 us)
Async XLA Ops:
  1.9 13.6 %copy-start.4 = (s32[6,128]{1,0:T(8,128)S(1)}, s32[6,128]{1,0:T(8,128)}, u32[]{:S(2)}) copy-start(s32[6,128]{1,0:T(8,128)} %rows_ref.3) | copy-start | bytes 9220
  1.9 44.4 %all-to-all-start.2 = ((bf16[32,144,128]{2,1,0:T(8,128)(2,1)}), bf16[32,144,128]{2,1,0:T(8,128)(2,1)S(1)}, u32[]{:S(2)}, u32[]{:S(2)}) async-start(bf16[32,144,128]{2,1,0:T(8,128)(2,1)} %broadcast_in_dim.92), calls=%async_computation.2 | async-start | bytes 2359296 | tf_op jit(solution)/shard_map/all_to_all | solution.py:137
  46.4 4.7 %collective-permute-start = (bf16[32,144,128]{2,1,0:T(8,128)(2,1)S(1)}, bf16[32,144,128]{2,1,0:T(8,128)(2,1)S(1)}, u32[]{:S(2)}, u32[]{:S(2)}) collective-permute-start(bf16[32,144,128]{2,1,0:T(8,128)(2,1)S(1)} %all-to-all-done.2), channel_id=1, source_target_pairs={{0,1},{1,0},{2,3},{3,2},{4,5},{5,4},{6,7},{7,6},{8,9},{9,8},{10,11... | collective-permute-start | bytes 3538952 | tf_op jit(solution)/shard_map/ppermute | solution.py:151
  51.9 14.6 %copy-start = (bf16[6,32,2,24,128]{4,3,2,1,0:T(8,128)(2,1)}, bf16[6,32,2,24,128]{4,3,2,1,0:T(8,128)(2,1)S(1)}, u32[]{:S(2)}) copy-start(bf16[6,32,2,24,128]{4,3,2,1,0:T(8,128)(2,1)S(1)} %copy.9) | copy-start | bytes 7077892
  53.4 16.5 %all-to-all-start.3 = ((bf16[8,64,128]{2,1,0:T(8,128)(2,1)}), bf16[8,64,128]{2,1,0:T(8,128)(2,1)S(1)}, u32[]{:S(2)}, u32[]{:S(2)}) async-start(bf16[8,64,128]{2,1,0:T(8,128)(2,1)} %broadcast_in_dim.96), calls=%async_computation.3 | async-start | bytes 262144 | tf_op jit(solution)/shard_map/all_to_all | solution.py:137
  69.8 37.5 %all-to-all-start = ((bf16[8,192,384]{2,1,0:T(8,128)(2,1)}), bf16[8,192,384]{2,1,0:T(8,128)(2,1)S(1)}, u32[]{:S(2)}, u32[]{:S(2)}) async-start(bf16[8,192,384]{2,1,0:T(8,128)(2,1)} %pad_maximum_fusion), calls=%async_computation | async-start | bytes 2359296 | tf_op jit(solution)/shard_map/all_to_all | solution.py:168
  108.2 22.6 %all-to-all-start.4 = ((bf16[32,64,128]{2,1,0:T(8,128)(2,1)}), bf16[32,64,128]{2,1,0:T(8,128)(2,1)S(1)}, u32[]{:S(2)}, u32[]{:S(2)}) async-start(bf16[32,64,128]{2,1,0:T(8,128)(2,1)} %broadcast_in_dim.97), calls=%async_computation.4 | async-start | bytes 1048576 | tf_op jit(solution)/shard_map/all_to_all | solution.py:137
  130.8 4.8 %copy-start.2 = (bf16[32,64,128]{2,1,0:T(8,128)(2,1)}, bf16[32,64,128]{2,1,0:T(8,128)(2,1)S(1)}, u32[]{:S(2)}) copy-start(bf16[32,64,128]{2,1,0:T(8,128)(2,1)S(1)} %all-to-all-done.4.mine_ref) | copy-start | bytes 1572868
  132.0 34.0 %all-to-all-start.1 = ((bf16[8,192,384]{2,1,0:T(8,128)(2,1)}), bf16[8,192,384]{2,1,0:T(8,128)(2,1)S(1)}, u32[]{:S(2)}, u32[]{:S(2)}) async-start(bf16[8,192,384]{2,1,0:T(8,128)(2,1)} %broadcast_in_dim.86), calls=%async_computation.1 | async-start | bytes 2359296 | tf_op jit(solution)/shard_map/all_to_all | solution.py:137
  135.6 30.5 %collective-permute-start.1 = (bf16[32,64,128]{2,1,0:T(8,128)(2,1)S(1)}, bf16[32,64,128]{2,1,0:T(8,128)(2,1)S(1)}, u32[]{:S(2)}, u32[]{:S(2)}) collective-permute-start(bf16[32,64,128]{2,1,0:T(8,128)(2,1)S(1)} %all-to-all-done.4.mine_ref), channel_id=1, source_target_pairs={{0,1},{1,0},{2,3},{3,2},{4,5},{5,4},{6,7},{7,6},{8,9},{9,8},{10,11... | collective-permute-start | bytes 1572872 | tf_op jit(solution)/shard_map/ppermute | solution.py:184
  166.1 1.0 copy-start.1
  166.1 1.2 copy-start.3

commit v2 on v1

--- a/solution.py
+++ b/solution.py
@@ -28,10 +28,13 @@
     return lax.broadcasted_iota(jnp.int32, shape, dim)
 
 
-def prep_kernel(first_ref, rows_ref, cols_ref, matrix_ref, picked_ref, tops_ref, select_ref):
-    first = first_ref[0]
+def prep_kernel(first_ref, me_ref, rows_ref, cols_ref, matrix_ref, select_ref, *rest):
+    piece_refs, fresh_ref = rest[:-1], rest[-1]
+    parts = len(piece_refs)
+    first, me = first_ref[0], me_ref[0]
     ones = jnp.ones((NB, NB), BF)
-    local = matrix_ref.shape[0]
+    local, width = matrix_ref.shape
+    each = TOP // parts
     for k in range(STEPS):
         ids = jnp.concatenate([iota((NB, NB), 0) + k * NB, jnp.broadcast_to(cols_ref[k * NB:(k + 1) * NB, :], (NB, NB))])
         found = jnp.zeros((2 * NB, NB), F32)
@@ -43,15 +46,19 @@
             select_ref[:, at + NB:at + 2 * NB] = (-live).astype(BF)
             hit = jnp.dot(same.astype(BF), ones, preferred_element_type=F32)
             found = jnp.maximum(found, hit)
-        fresh = found < 0.5
-        where = cols_ref[k * NB:(k + 1) * NB, :] - first
-        hot = jnp.where(iota((NB, local), 1) == where, 1.0, 0.0).astype(BF)
+        fresh_ref[0, k * NB:(k + 1) * NB, :] = found[:NB]
+        fresh_ref[1, k * NB:(k + 1) * NB, :] = found[NB:]
+    for s in range(parts):
+        at = pl.multiple_of(lax.rem(me + s, parts) * each, each)
+        where = cols_ref[pl.ds(at, each), :] - first
+        hot = jnp.where(iota((each, local), 1) == where, 1.0, 0.0).astype(BF)
         row = jnp.dot(hot, matrix_ref[...], preferred_element_type=F32)
-        for c in range(0, row.shape[1], NB):
-            picked_ref[k * NB:(k + 1) * NB, c:c + NB] = jnp.where(fresh[NB:], row[:, c:c + NB], 0.0).astype(BF)
-            mine = fresh[:NB] & (iota((NB, NB), 0) + first < TOP)
-            top = matrix_ref[k * NB:(k + 1) * NB, c:c + NB].astype(F32)
-            tops_ref[k * NB:(k + 1) * NB, c:c + NB] = jnp.where(mine, top, 0.0).astype(BF)
+        fresh = fresh_ref[1, pl.ds(at, each), :] < 0.5
+        mine = (fresh_ref[0, pl.ds(at, each), :] < 0.5) & (first == 0)
+        for c in range(0, width, NB):
+            piece_refs[s][:each, c:c + NB] = jnp.where(fresh, row[:, c:c + NB], 0.0).astype(BF)
+            top = matrix_ref[pl.ds(at, each), c:c + NB].astype(F32)
+            piece_refs[s][each:, c:c + NB] = jnp.where(mine, top, 0.0).astype(BF)
 
 
 def rows_kernel(first_ref, rows_ref, panels_ref, matrix_ref, factor_ref, kept_ref):
@@ -81,8 +88,8 @@
     lax.fori_loop(0, matrix_ref.shape[0] // height, one, 0)
 
 
-def solve_kernel(core_ref, content_ref, mine_ref, other_ref, inverses_ref, select_ref, factor_hbm, kept_hbm, out_ref,
-                 low, coef, state, factor, kept, sems):
+def solve_kernel(core_ref, me_ref, mine_ref, other_ref, inverses_ref, select_ref, factor_hbm, kept_hbm, *rest):
+    content_refs, (out_ref, low, coef, state, factor, kept, content, sems) = rest[:-8], rest[-8:]
     loads = [pltpu.make_async_copy(factor_hbm, factor, sems.at[0]), pltpu.make_async_copy(kept_hbm, kept, sems.at[1])]
     for load in loads:
         load.start()
@@ -90,13 +97,14 @@
     core = core_ref[0]
     low[core] = mine_ref[...].reshape(half, NB)
     low[1 - core] = other_ref[...].reshape(half, NB)
-    parts, each = content_ref.shape[0], content_ref.shape[1] // 2
-    width = content_ref.shape[2]
-    picked, tops = [], []
-    contents = content_ref[:, :each, :].reshape(parts * each, width)
-    displaced = content_ref[:, each:, :].reshape(parts * each, width)
+    parts = len(content_refs)
+    each = TOP // parts
+    for i, ref in enumerate(content_refs):
+        at = pl.multiple_of(lax.rem(me_ref[0] + parts - i, parts) * each, each)
+        content[1, pl.ds(at, each), :] = ref[:each]
+        content[0, pl.ds(at, each), :] = ref[each:]
     for k in range(STEPS):
-        x = jnp.concatenate([displaced[k * NB:(k + 1) * NB], contents[k * NB:(k + 1) * NB]]).astype(F32)
+        x = content[:, k * NB:(k + 1) * NB, :].reshape(2 * NB, -1).astype(F32)
         if k:
             for j in range(k):
                 at = start_of(k) + 2 * NB * j
@@ -137,7 +145,12 @@
     return lax.all_to_all(jnp.broadcast_to(x[None], (parts,) + x.shape), axes, 0, 0, tiled=True)
 
 
-def per_device(ny, nzx, nc, matrix, panels, inverses, pivots):
+def shift(x, n, s):
+    return lax.ppermute(x, "y", [(i, (i + s) % n) for i in range(n)])
+
+
+def per_device(ny, nz, nx, nc, matrix, panels, inverses, pivots):
+    nzx = nz * nx
     local, width = matrix.shape
     held = panels.shape[1]
     y, core = lax.axis_index("y"), lax.axis_index("c")
@@ -145,28 +158,28 @@
     first = y * local
     swap = [(0, 1), (1, 0)]
     first1 = first.reshape(1).astype(jnp.int32)
-    core1 = core.reshape(1).astype(jnp.int32)
-
-    mine = spread(panels.reshape(STEPS * held, NB), ("z", "x"), nzx)
+    me1, core1 = (a.reshape(1).astype(jnp.int32) for a in (y, core))
+
+    each = TOP // ny
+    select, *pieces = pl.pallas_call(
+        prep_kernel,
+        out_shape=(jax.ShapeDtypeStruct((2 * NB, start_of(STEPS)), BF),) + (jax.ShapeDtypeStruct((2 * each, width), BF),) * ny,
+        in_specs=[SM, SM, VM, VM, VM],
+        out_specs=(VM,) * (ny + 1),
+        scratch_shapes=[pltpu.VMEM((2, TOP, NB), F32)],
+        cost_estimate=cost(2 * TOP * local * width, 8 << 20),
+    )(first1, me1, pivots, pivots.reshape(TOP, 1), matrix)
+
+    mine = spread(panels.reshape(STEPS * held, NB), "z", nz)
+    mine, *pieces = lax.optimization_barrier((mine, *pieces))
+    mine = spread(mine, "x", nx)
+    content = sum(pieces[:1] + [shift(pieces[s], ny, s) for s in range(1, ny)])
+    mine, content = lax.optimization_barrier((mine, content))
+    contents = [content] + [shift(content, ny, s) for s in range(1, ny)]
     other = lax.ppermute(mine, "c", swap)
-    mine, other = (a.reshape(nzx, STEPS, held, NB) for a in (mine, other))
-    both = jnp.stack([jnp.where(core == 0, mine, other), jnp.where(core == 0, other, mine)], axis=1)
-    full = both.transpose(2, 0, 1, 3, 4).reshape(STEPS, local, NB)
-
-    picked, tops, select = pl.pallas_call(
-        prep_kernel,
-        out_shape=(
-            jax.ShapeDtypeStruct((TOP, width), BF),
-            jax.ShapeDtypeStruct((TOP, width), BF),
-            jax.ShapeDtypeStruct((2 * NB, start_of(STEPS)), BF),
-        ),
-        in_specs=[SM, VM, VM, VM],
-        out_specs=(VM, VM, VM),
-        cost_estimate=cost(2 * TOP * local * width, 8 << 20),
-    )(first1, pivots, pivots.reshape(TOP, 1), matrix)
-    share = jnp.concatenate([picked.reshape(ny, TOP // ny, width), tops.reshape(ny, TOP // ny, width)], axis=1)
-    got = lax.all_to_all(share, "y", 0, 0, tiled=True)
-    content = spread(got.astype(F32).sum(0).astype(BF), "y", ny)
+    mine, other = (a.reshape(nx, nz, STEPS, held, NB) for a in (mine, other))
+    both = jnp.stack([jnp.where(core == 0, mine, other), jnp.where(core == 0, other, mine)])
+    full = both.transpose(3, 2, 1, 0, 4, 5).reshape(STEPS, local, NB)
 
     idx = []
     for k, j in PAIRS:
@@ -179,8 +192,10 @@
     idx = lax.dynamic_slice(idx, ((core * nzx + zx) * chunk,), (chunk,))
     part = jnp.take(full.reshape(STEPS * local, NB), jnp.maximum(idx, 0), axis=0)
     part = jnp.where((idx >= 0)[:, None], part, jnp.zeros((), BF))
-    part = spread(part, "y", ny).astype(F32).reshape(ny, chunk, NB).sum(0).astype(BF)
+    part = spread(part, "y", ny).reshape(ny, chunk, NB).astype(F32).sum(0).astype(BF)
+    part, *contents[1:4] = lax.optimization_barrier((part, *contents[1:4]))
     low_mine = spread(part, ("z", "x"), nzx)
+    low_mine, *contents[4:] = lax.optimization_barrier((low_mine, *contents[4:]))
     low_other = lax.ppermute(low_mine, "c", swap)
 
     factor, kept = pl.pallas_call(
@@ -194,7 +209,7 @@
     return pl.pallas_call(
         solve_kernel,
         out_shape=jax.ShapeDtypeStruct((local, width), BF),
-        in_specs=[SM, VM, VM, VM, VM, VM, ANY, ANY],
+        in_specs=[SM, SM, VM, VM, VM, VM, ANY, ANY] + [VM] * ny,
         out_specs=VM,
         scratch_shapes=[
             pltpu.VMEM((2, nzx * chunk, NB), BF),
@@ -202,11 +217,12 @@
             pltpu.VMEM((2 * TOP, width), BF),
             pltpu.VMEM((local, 2 * TOP), BF),
             pltpu.VMEM((local, width), BF),
+            pltpu.VMEM((2, TOP, width), BF),
             pltpu.SemaphoreType.DMA((2,)),
         ],
         cost_estimate=cost(4 * TOP * local * width, 16 << 20),
-    )(core1, content.reshape(ny, 2 * TOP // ny, width), low_mine.reshape(nzx, chunk, NB), low_other.reshape(nzx, chunk, NB),
-      inverses, select, factor, kept)
+    )(core1, me1, low_mine.reshape(nzx, chunk, NB), low_other.reshape(nzx, chunk, NB),
+      inverses, select, factor, kept, *contents)
 
 
 def solution(mesh):
@@ -216,5 +232,5 @@
     cols = ("z", "x", "c")
     in_specs = (P("y", cols), P(None, ("y",) + cols, None), P(), P())
     return jax.shard_map(
-        functools.partial(per_device, ny, nz * nx, nc), mesh=fine, in_specs=in_specs, out_specs=P("y", cols), check_vma=False
+        functools.partial(per_device, ny, nz, nx, nc), mesh=fine, in_specs=in_specs, out_specs=P("y", cols), check_vma=False
     )

time: 179 us -> 171 us (0.955)
  waiting for transfers between devices: 103 us -> 46.8 us
  starting transfers between devices: 39.8 us -> 88.8 us
  other arithmetic: 3.4 us -> 1.6 us
    all_to_all x4, waiting for transfers between devices: 69.3 us -> 5.53 us  [spread(): lax.all_to_all(jnp.broadcast_to(x[None], (parts,) + x.shape), axes, 0, 0,...]
    ppermute x0 -> x14, starting transfers between devices: none -> 59.8 us  [shift(): return lax.ppermute(x, 'y', [(i, (i + s) % n) for i in range(n)])]
    ppermute x0 -> x14, waiting for transfers between devices: none -> 38.7 us  [shift(): return lax.ppermute(x, 'y', [(i, (i + s) % n) for i in range(n)])]
    all_to_all x1 -> x0, waiting for transfers between devices: 31.3 us -> none  [per_device(): got = lax.all_to_all(share, 'y', 0, 0, tiled=True)]
    all_to_all x1 -> x0, starting transfers between devices: 6.22 us -> none  [per_device(): got = lax.all_to_all(share, 'y', 0, 0, tiled=True)]
    all_to_all x4, starting transfers between devices: 29.8 us -> 25.2 us  [spread(): lax.all_to_all(jnp.broadcast_to(x[None], (parts,) + x.shape), axes, 0, 0,...]
    concatenate x1 -> x0, other arithmetic: 2.38 us -> none  [per_device(): jnp.concatenate([picked.reshape(ny, TOP // ny, width), tops.reshape(ny, T...]
  transfers between devices with their start and end apart: 7 -> 20, of which waited for: 6 -> 11; matrix products, arithmetic and copies ran while one was open for 2% -> 2% of each run, Pallas kernels for 7% -> 8%
where the time goes in v2:
time: 171 us; the launch traced here: 169 us
  starting transfers between devices  88.8 us (52%)
  waiting for transfers between devices  46.8 us (27%)
  Pallas kernels  22.2 us (13%)
  local copies, waits for them, and re-layouts  8.8 us (5%)
    ppermute x14, starting transfers between devices, shift(): return lax.ppermute(x, 'y', [(i, (i + s) % n) for i in range(n)])  59.8 us
    ppermute x14, waiting for transfers between devices, shift(): return lax.ppermute(x, 'y', [(i, (i + s) % n) for i in range(n)])  38.7 us
    all_to_all x4, starting transfers between devices, spread(): lax.all_to_all(jnp.broadcast_to(x[None], (parts,) + x.shape), axes, 0, 0,...  25.2 us
    pallas_call x1, Pallas kernels, per_device(): pl.pallas_call(solve_kernel, out_shape=jax.ShapeDtypeStruct((local, width...  9.53 us
    pallas_call x1, Pallas kernels, per_device(): pl.pallas_call(rows_kernel, out_shape=(jax.ShapeDtypeStruct((local, 2 * T...  7.56 us
    all_to_all x4, waiting for transfers between devices, spread(): lax.all_to_all(jnp.broadcast_to(x[None], (parts,) + x.shape), axes, 0, 0,...  5.53 us
    pallas_call x1, Pallas kernels, per_device(): pl.pallas_call(prep_kernel, out_shape=(jax.ShapeDtypeStruct((2 * NB, star...  5.11 us
    broadcast_in_dim x4, local copies, waits for them, and re-layouts, spread(): jnp.broadcast_to(x[None], (parts,) + x.shape)  4.32 us
  transfers between devices with their start and end apart: 20, of which 11 were waited for; matrix products, arithmetic and copies ran while one was open for 2% of the time, Pallas kernels for 8%

profile of v2, /device:TPU:6, one launch (start us, length us, event | category | flops | bytes accessed | tf_op | source)
XLA Modules:
  0.0 168.8 jit_solution(9907861912310495683)
XLA Ops:
  1.5 10.3 %all-to-all-start = ((bf16[8,144,128]{2,1,0:T(8,128)(2,1)}), bf16[8,144,128]{2,1,0:T(8,128)(2,1)S(1)}, u32[]{:S(2)}, u32[]{:S(2)}) async-start(bf16[8,144,128]{2,1,0:T(8,128)(2,1)} %broadcast_in_dim.91), calls=%async_computation | async-start | bytes 589824 | tf_op jit(solution)/shard_map/all_to_all | solution.py:145
  13.8 5.1 %shard_map.46 = (bf16[256,3840]{1,0:T(8,128)(2,1)}, bf16[192,384]{1,0:T(8,128)(2,1)}, bf16[192,384]{1,0:T(8,128)(2,1)}, bf16[192,384]{1,0:T(8,128)(2,1)}, bf16[1...) custom-call(s32[1]{0:T(128)} %bitcast.8.first_ref, ...), custom_call_target="tpu_custom_call" | custom-call | flops 905969664 | bytes 8388608 | tf_op jit(solution)/shard_map/pallas_call | solution.py:164
  18.9 5.5 %all-to-all-done = bf16[8,144,128]{2,1,0:T(8,128)(2,1)S(1)} async-done(((bf16[8,144,128]{2,1,0:T(8,128)(2,1)}), bf16[8,144,128]{2,1,0:T(8,128)(2,1)S(1)}, u32[]{:S(2)}, u32[]{:S(2)}) %all-to-all-start) | async-done | bytes 294944 | tf_op jit(solution)/shard_map/all_to_all | solution.py:145
  27.9 4.5 %collective-permute-start.1 = (bf16[192,384]{1,0:T(8,128)(2,1)}, bf16[192,384]{1,0:T(8,128)(2,1)S(1)}, u32[]{:S(2)}, u32[]{:S(2)}) collective-permute-start(bf16[192,384]{1,0:T(8,128)(2,1)} %get-tuple-element.47), channel_id=1, source_target_pairs={{0,128},{64,192},{128,256},{192,320},{256,384},{320,448},{384,0},{... | collective-permute-start | bytes 442376 | tf_op jit(solution)/shard_map/ppermute | solution.py:149
  33.6 4.9 %all-to-all-start.1 = ((bf16[4,8,144,128]{3,2,1,0:T(8,128)(2,1)}), bf16[4,8,144,128]{3,2,1,0:T(8,128)(2,1)S(1)}, u32[]{:S(2)}, u32[]{:S(2)}) async-start(bf16[4,8,144,128]{3,2,1,0:T(8,128)(2,1)} %broadcast_in_dim.92), calls=%async_computation.1 | async-start | bytes 2359296 | tf_op jit(solution)/shard_map/all_to_all | solution.py:145
  39.3 4.9 %collective-permute-start.2 = (bf16[192,384]{1,0:T(8,128)(2,1)S(1)}, bf16[192,384]{1,0:T(8,128)(2,1)S(1)}, u32[]{:S(2)}, u32[]{:S(2)}) collective-permute-start(bf16[192,384]{1,0:T(8,128)(2,1)S(1)} %copy-done.16), channel_id=1, source_target_pairs={{0,192},{64,256},{128,320},{192,384},{256,448},{320,0},{384,64},{4... | collective-permute-start | bytes 442376 | tf_op jit(solution)/shard_map/ppermute | solution.py:149
  44.2 3.8 %collective-permute-start.3 = (bf16[192,384]{1,0:T(8,128)(2,1)S(1)}, bf16[192,384]{1,0:T(8,128)(2,1)S(1)}, u32[]{:S(2)}, u32[]{:S(2)}) collective-permute-start(bf16[192,384]{1,0:T(8,128)(2,1)S(1)} %copy-done.15), channel_id=1, source_target_pairs={{0,256},{64,320},{128,384},{192,448},{256,0},{320,64},{384,128},{4... | collective-permute-start | bytes 442376 | tf_op jit(solution)/shard_map/ppermute | solution.py:149
  48.0 5.2 %collective-permute-start.4 = (bf16[192,384]{1,0:T(8,128)(2,1)S(1)}, bf16[192,384]{1,0:T(8,128)(2,1)S(1)}, u32[]{:S(2)}, u32[]{:S(2)}) collective-permute-start(bf16[192,384]{1,0:T(8,128)(2,1)S(1)} %copy-done.14), channel_id=1, source_target_pairs={{0,320},{64,384},{128,448},{192,0},{256,64},{320,128},{384,192},{4... | collective-permute-start | bytes 442376 | tf_op jit(solution)/shard_map/ppermute | solution.py:149
  53.2 5.3 %collective-permute-start.5 = (bf16[192,384]{1,0:T(8,128)(2,1)S(1)}, bf16[192,384]{1,0:T(8,128)(2,1)S(1)}, u32[]{:S(2)}, u32[]{:S(2)}) collective-permute-start(bf16[192,384]{1,0:T(8,128)(2,1)S(1)} %copy-done.13), channel_id=1, source_target_pairs={{0,384},{64,448},{128,0},{192,64},{256,128},{320,192},{384,256},{4... | collective-permute-start | bytes 442376 | tf_op jit(solution)/shard_map/ppermute | solution.py:149
  61.8 7.1 %collective-permute-done.4 = bf16[192,384]{1,0:T(8,128)(2,1)S(1)} collective-permute-done((bf16[192,384]{1,0:T(8,128)(2,1)S(1)}, bf16[192,384]{1,0:T(8,128)(2,1)S(1)}, u32[]{:S(2)}, u32[]{:S(2)}) %collective-permute-start.4) | collective-permute-done | bytes 147488 | tf_op jit(solution)/shard_map/ppermute | solution.py:149
  80.6 4.4 %all-to-all-start.2 = ((bf16[8,64,128]{2,1,0:T(8,128)(2,1)}), bf16[8,64,128]{2,1,0:T(8,128)(2,1)S(1)}, u32[]{:S(2)}, u32[]{:S(2)}) async-start(bf16[8,64,128]{2,1,0:T(8,128)(2,1)} %broadcast_in_dim.96), calls=%async_computation.2 | async-start | bytes 262144 | tf_op jit(solution)/shard_map/all_to_all | solution.py:145
  85.0 5.7 %collective-permute-start.10 = (bf16[192,384]{1,0:T(8,128)(2,1)S(1)}, bf16[192,384]{1,0:T(8,128)(2,1)S(1)}, u32[]{:S(2)}, u32[]{:S(2)}) collective-permute-start(bf16[192,384]{1,0:T(8,128)(2,1)S(1)} %add_add_fusion.rest_0_), channel_id=1, source_target_pairs={{0,192},{64,256},{128,320},{192,384},{256,448},{320,0},{384,64},{4... | collective-permute-start | bytes 442376 | tf_op jit(solution)/shard_map/ppermute | solution.py:149
  90.7 4.6 %collective-permute-start.8 = (bf16[192,384]{1,0:T(8,128)(2,1)S(1)}, bf16[192,384]{1,0:T(8,128)(2,1)S(1)}, u32[]{:S(2)}, u32[]{:S(2)}) collective-permute-start(bf16[192,384]{1,0:T(8,128)(2,1)S(1)} %add_add_fusion.rest_0_), channel_id=1, source_target_pairs={{0,64},{64,128},{128,192},{192,256},{256,320},{320,384},{384,448},... | collective-permute-start | bytes 442376 | tf_op jit(solution)/shard_map/ppermute | solution.py:149
  97.8 5.2 %collective-permute-done.10.rest_3_ = bf16[192,384]{1,0:T(8,128)(2,1)S(1)} collective-permute-done((bf16[192,384]{1,0:T(8,128)(2,1)S(1)}, bf16[192,384]{1,0:T(8,128)(2,1)S(1)}, u32[]{:S(2)}, u32[]{:S(2)}) %collective-permute-start.10) | collective-permute-done | bytes 147488 | tf_op jit(solution)/shard_map/ppermute | solution.py:149
  103.0 3.6 %collective-permute-done.8.rest_1_ = bf16[192,384]{1,0:T(8,128)(2,1)S(1)} collective-permute-done((bf16[192,384]{1,0:T(8,128)(2,1)S(1)}, bf16[192,384]{1,0:T(8,128)(2,1)S(1)}, u32[]{:S(2)}, u32[]{:S(2)}) %collective-permute-start.8) | collective-permute-done | bytes 147488 | tf_op jit(solution)/shard_map/ppermute | solution.py:149
  106.6 3.8 %collective-permute-done.9.rest_2_ = bf16[192,384]{1,0:T(8,128)(2,1)S(1)} collective-permute-done((bf16[192,384]{1,0:T(8,128)(2,1)S(1)}, bf16[192,384]{1,0:T(8,128)(2,1)S(1)}, u32[]{:S(2)}, u32[]{:S(2)}) %collective-permute-start.9) | collective-permute-done | bytes 147488 | tf_op jit(solution)/shard_map/ppermute | solution.py:149
  111.3 5.5 %all-to-all-start.3 = ((bf16[32,64,128]{2,1,0:T(8,128)(2,1)}), bf16[32,64,128]{2,1,0:T(8,128)(2,1)S(1)}, u32[]{:S(2)}, u32[]{:S(2)}) async-start(bf16[32,64,128]{2,1,0:T(8,128)(2,1)} %broadcast_in_dim.97), calls=%async_computation.3 | async-start | bytes 1048576 | tf_op jit(solution)/shard_map/all_to_all | solution.py:145
  116.8 5.6 %collective-permute-start.11 = (bf16[192,384]{1,0:T(8,128)(2,1)S(1)}, bf16[192,384]{1,0:T(8,128)(2,1)S(1)}, u32[]{:S(2)}, u32[]{:S(2)}) collective-permute-start(bf16[192,384]{1,0:T(8,128)(2,1)S(1)} %add_add_fusion.rest_0_), channel_id=1, source_target_pairs={{0,256},{64,320},{128,384},{192,448},{256,0},{320,64},{384,128},{4... | collective-permute-start | bytes 442376 | tf_op jit(solution)/shard_map/ppermute | solution.py:149
  122.4 5.5 %collective-permute-start.12 = (bf16[192,384]{1,0:T(8,128)(2,1)S(1)}, bf16[192,384]{1,0:T(8,128)(2,1)S(1)}, u32[]{:S(2)}, u32[]{:S(2)}) collective-permute-start(bf16[192,384]{1,0:T(8,128)(2,1)S(1)} %add_add_fusion.rest_0_), channel_id=1, source_target_pairs={{0,320},{64,384},{128,448},{192,0},{256,64},{320,128},{384,192},{4... | collective-permute-start | bytes 442376 | tf_op jit(solution)/shard_map/ppermute | solution.py:149
  128.0 3.6 %collective-permute-start.13 = (bf16[192,384]{1,0:T(8,128)(2,1)S(1)}, bf16[192,384]{1,0:T(8,128)(2,1)S(1)}, u32[]{:S(2)}, u32[]{:S(2)}) collective-permute-start(bf16[192,384]{1,0:T(8,128)(2,1)S(1)} %add_add_fusion.rest_0_), channel_id=1, source_target_pairs={{0,384},{64,448},{128,0},{192,64},{256,128},{320,192},{384,256},{4... | collective-permute-start | bytes 442376 | tf_op jit(solution)/shard_map/ppermute | solution.py:149
  133.6 7.8 %collective-permute-done.12.rest_5_ = bf16[192,384]{1,0:T(8,128)(2,1)S(1)} collective-permute-done((bf16[192,384]{1,0:T(8,128)(2,1)S(1)}, bf16[192,384]{1,0:T(8,128)(2,1)S(1)}, u32[]{:S(2)}, u32[]{:S(2)}) %collective-permute-start.12) | collective-permute-done | bytes 147488 | tf_op jit(solution)/shard_map/ppermute | solution.py:149
  141.4 5.8 %collective-permute-done.13.rest_6_ = bf16[192,384]{1,0:T(8,128)(2,1)S(1)} collective-permute-done((bf16[192,384]{1,0:T(8,128)(2,1)S(1)}, bf16[192,384]{1,0:T(8,128)(2,1)S(1)}, u32[]{:S(2)}, u32[]{:S(2)}) %collective-permute-start.13) | collective-permute-done | bytes 147488 | tf_op jit(solution)/shard_map/ppermute | solution.py:149
  150.8 7.6 %shard_map.47 = (bf16[1536,1536]{1,0:T(8,128)(2,1)}, bf16[1536,384]{1,0:T(8,128)(2,1)}) custom-call(s32[1]{0:T(128)} %bitcast.8.first_ref, s32[6,128]{1,0:T(8,128)} %rows_ref.3, bf16[6,1536,128]{2,1,0:T(8,128)(2,1)} %bitcast.117, bf16[1536,384]{1,0:T(8,128)(2,1)} %matrix_ref.3), custom_call_target="tpu_custom_call" | custom-call | flops 301989888 | bytes 12582912 | tf_op jit(solution)/shard_map/pallas_call | solution.py:201
  159.3 9.5 %shard_map.48 = bf16[1536,384]{1,0:T(8,128)(2,1)} custom-call(s32[1]{0:T(128)} %bitcast.core_ref, s32[1]{0:T(128)} %bitcast.1.me_ref, bf16[32,64,128]{2,1,0:T(8,128)(2,1)} %copy-done.1, bf16[32,64,128]{2,1,0:T(8,128)(2,1)} %copy-done.3, f32[6,128,128]{2,1,0:T(8,128)} %inverses_ref.1, bf16[256,3840]{1,0:T(8,128)(2,1)} %get-tuple-element.57.select_ref, ...), custom_call_target="tpu_custom_call" | custom-call | flops 1811939328 | bytes 16777216 | tf_op jit(solution)/shard_map/pallas_call | solution.py:209
  (100 shorter events, 33.3 us)
Async XLA Ops:
  1.5 22.9 %all-to-all-start = ((bf16[8,144,128]{2,1,0:T(8,128)(2,1)}), bf16[8,144,128]{2,1,0:T(8,128)(2,1)S(1)}, u32[]{:S(2)}, u32[]{:S(2)}) async-start(bf16[8,144,128]{2,1,0:T(8,128)(2,1)} %broadcast_in_dim.91), calls=%async_computation | async-start | bytes 589824 | tf_op jit(solution)/shard_map/all_to_all | solution.py:145
  24.4 28.7 %collective-permute-start = (bf16[192,384]{1,0:T(8,128)(2,1)}, bf16[192,384]{1,0:T(8,128)(2,1)S(1)}, u32[]{:S(2)}, u32[]{:S(2)}) collective-permute-start(bf16[192,384]{1,0:T(8,128)(2,1)} %get-tuple-element.46), channel_id=1, source_target_pairs={{0,64},{64,128},{128,192},{192,256},{256,320},{320,384},{384,448},... | collective-permute-start | bytes 442376 | tf_op jit(solution)/shard_map/ppermute | solution.py:149
  27.9 30.5 %collective-permute-start.1 = (bf16[192,384]{1,0:T(8,128)(2,1)}, bf16[192,384]{1,0:T(8,128)(2,1)S(1)}, u32[]{:S(2)}, u32[]{:S(2)}) collective-permute-start(bf16[192,384]{1,0:T(8,128)(2,1)} %get-tuple-element.47), channel_id=1, source_target_pairs={{0,128},{64,192},{128,256},{192,320},{256,384},{320,448},{384,0},{... | collective-permute-start | bytes 442376 | tf_op jit(solution)/shard_map/ppermute | solution.py:149
  33.6 39.7 %all-to-all-start.1 = ((bf16[4,8,144,128]{3,2,1,0:T(8,128)(2,1)}), bf16[4,8,144,128]{3,2,1,0:T(8,128)(2,1)S(1)}, u32[]{:S(2)}, u32[]{:S(2)}) async-start(bf16[4,8,144,128]{3,2,1,0:T(8,128)(2,1)} %broadcast_in_dim.92), calls=%async_computation.1 | async-start | bytes 2359296 | tf_op jit(solution)/shard_map/all_to_all | solution.py:145
  39.3 22.5 %collective-permute-start.2 = (bf16[192,384]{1,0:T(8,128)(2,1)S(1)}, bf16[192,384]{1,0:T(8,128)(2,1)S(1)}, u32[]{:S(2)}, u32[]{:S(2)}) collective-permute-start(bf16[192,384]{1,0:T(8,128)(2,1)S(1)} %copy-done.16), channel_id=1, source_target_pairs={{0,192},{64,256},{128,320},{192,384},{256,448},{320,0},{384,64},{4... | collective-permute-start | bytes 442376 | tf_op jit(solution)/shard_map/ppermute | solution.py:149
  44.2 17.6 %collective-permute-start.3 = (bf16[192,384]{1,0:T(8,128)(2,1)S(1)}, bf16[192,384]{1,0:T(8,128)(2,1)S(1)}, u32[]{:S(2)}, u32[]{:S(2)}) collective-permute-start(bf16[192,384]{1,0:T(8,128)(2,1)S(1)} %copy-done.15), channel_id=1, source_target_pairs={{0,256},{64,320},{128,384},{192,448},{256,0},{320,64},{384,128},{4... | collective-permute-start | bytes 442376 | tf_op jit(solution)/shard_map/ppermute | solution.py:149
  48.0 20.9 %collective-permute-start.4 = (bf16[192,384]{1,0:T(8,128)(2,1)S(1)}, bf16[192,384]{1,0:T(8,128)(2,1)S(1)}, u32[]{:S(2)}, u32[]{:S(2)}) collective-permute-start(bf16[192,384]{1,0:T(8,128)(2,1)S(1)} %copy-done.14), channel_id=1, source_target_pairs={{0,320},{64,384},{128,448},{192,0},{256,64},{320,128},{384,192},{4... | collective-permute-start | bytes 442376 | tf_op jit(solution)/shard_map/ppermute | solution.py:149
  53.2 17.2 %collective-permute-start.5 = (bf16[192,384]{1,0:T(8,128)(2,1)S(1)}, bf16[192,384]{1,0:T(8,128)(2,1)S(1)}, u32[]{:S(2)}, u32[]{:S(2)}) collective-permute-start(bf16[192,384]{1,0:T(8,128)(2,1)S(1)} %copy-done.13), channel_id=1, source_target_pairs={{0,384},{64,448},{128,0},{192,64},{256,128},{320,192},{384,256},{4... | collective-permute-start | bytes 442376 | tf_op jit(solution)/shard_map/ppermute | solution.py:149
  58.5 14.7 %collective-permute-start.6 = (bf16[192,384]{1,0:T(8,128)(2,1)S(1)}, bf16[192,384]{1,0:T(8,128)(2,1)S(1)}, u32[]{:S(2)}, u32[]{:S(2)}) collective-permute-start(bf16[192,384]{1,0:T(8,128)(2,1)S(1)} %copy-done.12), channel_id=1, source_target_pairs={{0,448},{64,0},{128,64},{192,128},{256,192},{320,256},{384,320},{4... | collective-permute-start | bytes 442376 | tf_op jit(solution)/shard_map/ppermute | solution.py:149
  73.3 58.3 %copy-start.2 = (bf16[192,384]{1,0:T(8,128)(2,1)}, bf16[192,384]{1,0:T(8,128)(2,1)S(1)}, u32[]{:S(2)}) copy-start(bf16[192,384]{1,0:T(8,128)(2,1)S(1)} %add_add_fusion.rest_0_) | copy-start | bytes 442372
  73.3 4.7 %collective-permute-start.7 = (bf16[4,8,144,128]{3,2,1,0:T(8,128)(2,1)S(1)}, bf16[4,8,144,128]{3,2,1,0:T(8,128)(2,1)S(1)}, u32[]{:S(2)}, u32[]{:S(2)}) collective-permute-start(bf16[4,8,144,128]{3,2,1,0:T(8,128)(2,1)S(1)} %all-to-all-done.1), channel_id=1, source_target_pairs={{0,1},{1,0},{2,3},{3,2},{4,5},{5,4},{6,7},{7,6},{8,9},{9,8},{10,11... | collective-permute-start | bytes 3538952 | tf_op jit(solution)/shard_map/ppermute | solution.py:179
  79.1 71.7 %copy-start = (bf16[6,8,4,2,24,128]{5,4,3,2,1,0:T(8,128)(2,1)}, bf16[6,8,4,2,24,128]{5,4,3,2,1,0:T(8,128)(2,1)S(1)}, u32[]{:S(2)}) copy-start(bf16[6,8,4,2,24,128]{5,4,3,2,1,0:T(8,128)(2,1)S(1)} %copy.9) | copy-start | bytes 7077892
  80.6 17.2 %all-to-all-start.2 = ((bf16[8,64,128]{2,1,0:T(8,128)(2,1)}), bf16[8,64,128]{2,1,0:T(8,128)(2,1)S(1)}, u32[]{:S(2)}, u32[]{:S(2)}) async-start(bf16[8,64,128]{2,1,0:T(8,128)(2,1)} %broadcast_in_dim.96), calls=%async_computation.2 | async-start | bytes 262144 | tf_op jit(solution)/shard_map/all_to_all | solution.py:145
  85.0 18.0 %collective-permute-start.10 = (bf16[192,384]{1,0:T(8,128)(2,1)S(1)}, bf16[192,384]{1,0:T(8,128)(2,1)S(1)}, u32[]{:S(2)}, u32[]{:S(2)}) collective-permute-start(bf16[192,384]{1,0:T(8,128)(2,1)S(1)} %add_add_fusion.rest_0_), channel_id=1, source_target_pairs={{0,192},{64,256},{128,320},{192,384},{256,448},{320,0},{384,64},{4... | collective-permute-start | bytes 442376 | tf_op jit(solution)/shard_map/ppermute | solution.py:149
  90.7 15.9 %collective-permute-start.8 = (bf16[192,384]{1,0:T(8,128)(2,1)S(1)}, bf16[192,384]{1,0:T(8,128)(2,1)S(1)}, u32[]{:S(2)}, u32[]{:S(2)}) collective-permute-start(bf16[192,384]{1,0:T(8,128)(2,1)S(1)} %add_add_fusion.rest_0_), channel_id=1, source_target_pairs={{0,64},{64,128},{128,192},{192,256},{256,320},{320,384},{384,448},... | collective-permute-start | bytes 442376 | tf_op jit(solution)/shard_map/ppermute | solution.py:149
  95.3 15.1 %collective-permute-start.9 = (bf16[192,384]{1,0:T(8,128)(2,1)S(1)}, bf16[192,384]{1,0:T(8,128)(2,1)S(1)}, u32[]{:S(2)}, u32[]{:S(2)}) collective-permute-start(bf16[192,384]{1,0:T(8,128)(2,1)S(1)} %add_add_fusion.rest_0_), channel_id=1, source_target_pairs={{0,128},{64,192},{128,256},{192,320},{256,384},{320,448},{384,0},{... | collective-permute-start | bytes 442376 | tf_op jit(solution)/shard_map/ppermute | solution.py:149
  103.0 55.4 %copy-start.5 = (bf16[192,384]{1,0:T(8,128)(2,1)}, bf16[192,384]{1,0:T(8,128)(2,1)S(1)}, u32[]{:S(2)}) copy-start(bf16[192,384]{1,0:T(8,128)(2,1)S(1)} %collective-permute-done.10.rest_3_) | copy-start | bytes 442372
  106.6 42.3 %copy-start.6 = (bf16[192,384]{1,0:T(8,128)(2,1)}, bf16[192,384]{1,0:T(8,128)(2,1)S(1)}, u32[]{:S(2)}) copy-start(bf16[192,384]{1,0:T(8,128)(2,1)S(1)} %collective-permute-done.8.rest_1_) | copy-start | bytes 442372
  111.3 37.6 %all-to-all-start.3 = ((bf16[32,64,128]{2,1,0:T(8,128)(2,1)}), bf16[32,64,128]{2,1,0:T(8,128)(2,1)S(1)}, u32[]{:S(2)}, u32[]{:S(2)}) async-start(bf16[32,64,128]{2,1,0:T(8,128)(2,1)} %broadcast_in_dim.97), calls=%async_computation.3 | async-start | bytes 1048576 | tf_op jit(solution)/shard_map/all_to_all | solution.py:145
  116.8 16.7 %collective-permute-start.11 = (bf16[192,384]{1,0:T(8,128)(2,1)S(1)}, bf16[192,384]{1,0:T(8,128)(2,1)S(1)}, u32[]{:S(2)}, u32[]{:S(2)}) collective-permute-start(bf16[192,384]{1,0:T(8,128)(2,1)S(1)} %add_add_fusion.rest_0_), channel_id=1, source_target_pairs={{0,256},{64,320},{128,384},{192,448},{256,0},{320,64},{384,128},{4... | collective-permute-start | bytes 442376 | tf_op jit(solution)/shard_map/ppermute | solution.py:149
  122.4 19.0 %collective-permute-start.12 = (bf16[192,384]{1,0:T(8,128)(2,1)S(1)}, bf16[192,384]{1,0:T(8,128)(2,1)S(1)}, u32[]{:S(2)}, u32[]{:S(2)}) collective-permute-start(bf16[192,384]{1,0:T(8,128)(2,1)S(1)} %add_add_fusion.rest_0_), channel_id=1, source_target_pairs={{0,320},{64,384},{128,448},{192,0},{256,64},{320,128},{384,192},{4... | collective-permute-start | bytes 442376 | tf_op jit(solution)/shard_map/ppermute | solution.py:149
  128.0 19.3 %collective-permute-start.13 = (bf16[192,384]{1,0:T(8,128)(2,1)S(1)}, bf16[192,384]{1,0:T(8,128)(2,1)S(1)}, u32[]{:S(2)}, u32[]{:S(2)}) collective-permute-start(bf16[192,384]{1,0:T(8,128)(2,1)S(1)} %add_add_fusion.rest_0_), channel_id=1, source_target_pairs={{0,384},{64,448},{128,0},{192,64},{256,128},{320,192},{384,256},{4... | collective-permute-start | bytes 442376 | tf_op jit(solution)/shard_map/ppermute | solution.py:149
  131.6 17.2 %collective-permute-start.14 = (bf16[192,384]{1,0:T(8,128)(2,1)S(1)}, bf16[192,384]{1,0:T(8,128)(2,1)}, u32[]{:S(2)}, u32[]{:S(2)}) collective-permute-start(bf16[192,384]{1,0:T(8,128)(2,1)S(1)} %add_add_fusion.rest_0_), channel_id=1, source_target_pairs={{0,448},{64,0},{128,64},{192,128},{256,192},{320,256},{384,320},{4... | collective-permute-start | bytes 442376 | tf_op jit(solution)/shard_map/ppermute | solution.py:149
  148.9 9.5 %collective-permute-start.15 = (bf16[32,64,128]{2,1,0:T(8,128)(2,1)S(1)}, bf16[32,64,128]{2,1,0:T(8,128)(2,1)S(1)}, u32[]{:S(2)}, u32[]{:S(2)}) collective-permute-start(bf16[32,64,128]{2,1,0:T(8,128)(2,1)S(1)} %all-to-all-done.3.mine_ref), channel_id=1, source_target_pairs={{0,1},{1,0},{2,3},{3,2},{4,5},{5,4},{6,7},{7,6},{8,9},{9,8},{10,11... | collective-permute-start | bytes 1572872 | tf_op jit(solution)/shard_map/ppermute | solution.py:199
  (13 other events, 197.3 us)

commit v3 on v1

--- a/solution.py
+++ b/solution.py
@@ -28,10 +28,10 @@
     return lax.broadcasted_iota(jnp.int32, shape, dim)
 
 
-def prep_kernel(first_ref, rows_ref, cols_ref, matrix_ref, picked_ref, tops_ref, select_ref):
+def prep_kernel(first_ref, rows_ref, cols_ref, matrix_ref, share_ref, select_ref):
     first = first_ref[0]
     ones = jnp.ones((NB, NB), BF)
-    local = matrix_ref.shape[0]
+    local, width = matrix_ref.shape
     for k in range(STEPS):
         ids = jnp.concatenate([iota((NB, NB), 0) + k * NB, jnp.broadcast_to(cols_ref[k * NB:(k + 1) * NB, :], (NB, NB))])
         found = jnp.zeros((2 * NB, NB), F32)
@@ -44,14 +44,14 @@
             hit = jnp.dot(same.astype(BF), ones, preferred_element_type=F32)
             found = jnp.maximum(found, hit)
         fresh = found < 0.5
-        where = cols_ref[k * NB:(k + 1) * NB, :] - first
-        hot = jnp.where(iota((NB, local), 1) == where, 1.0, 0.0).astype(BF)
+        at = k * NB
+        hot = jnp.where(iota((NB, local), 1) == cols_ref[at:at + NB, :] - first, 1.0, 0.0).astype(BF)
         row = jnp.dot(hot, matrix_ref[...], preferred_element_type=F32)
-        for c in range(0, row.shape[1], NB):
-            picked_ref[k * NB:(k + 1) * NB, c:c + NB] = jnp.where(fresh[NB:], row[:, c:c + NB], 0.0).astype(BF)
-            mine = fresh[:NB] & (iota((NB, NB), 0) + first < TOP)
-            top = matrix_ref[k * NB:(k + 1) * NB, c:c + NB].astype(F32)
-            tops_ref[k * NB:(k + 1) * NB, c:c + NB] = jnp.where(mine, top, 0.0).astype(BF)
+        mine = fresh[:NB] & (first == 0)
+        for c in range(0, width, NB):
+            top = matrix_ref[at:at + NB, c:c + NB].astype(F32)
+            share_ref[0, at:at + NB, c:c + NB] = jnp.where(mine, top, 0.0).astype(BF)
+            share_ref[1, at:at + NB, c:c + NB] = jnp.where(fresh[NB:], row[:, c:c + NB], 0.0).astype(BF)
 
 
 def rows_kernel(first_ref, rows_ref, panels_ref, matrix_ref, factor_ref, kept_ref):
@@ -81,7 +81,7 @@
     lax.fori_loop(0, matrix_ref.shape[0] // height, one, 0)
 
 
-def solve_kernel(core_ref, content_ref, mine_ref, other_ref, inverses_ref, select_ref, factor_hbm, kept_hbm, out_ref,
+def solve_kernel(core_ref, content, mine_ref, other_ref, inverses_ref, select_ref, factor_hbm, kept_hbm, out_ref,
                  low, coef, state, factor, kept, sems):
     loads = [pltpu.make_async_copy(factor_hbm, factor, sems.at[0]), pltpu.make_async_copy(kept_hbm, kept, sems.at[1])]
     for load in loads:
@@ -90,13 +90,8 @@
     core = core_ref[0]
     low[core] = mine_ref[...].reshape(half, NB)
     low[1 - core] = other_ref[...].reshape(half, NB)
-    parts, each = content_ref.shape[0], content_ref.shape[1] // 2
-    width = content_ref.shape[2]
-    picked, tops = [], []
-    contents = content_ref[:, :each, :].reshape(parts * each, width)
-    displaced = content_ref[:, each:, :].reshape(parts * each, width)
     for k in range(STEPS):
-        x = jnp.concatenate([displaced[k * NB:(k + 1) * NB], contents[k * NB:(k + 1) * NB]]).astype(F32)
+        x = content[:, k * NB:(k + 1) * NB, :].reshape(2 * NB, -1).astype(F32)
         if k:
             for j in range(k):
                 at = start_of(k) + 2 * NB * j
@@ -137,7 +132,8 @@
     return lax.all_to_all(jnp.broadcast_to(x[None], (parts,) + x.shape), axes, 0, 0, tiled=True)
 
 
-def per_device(ny, nzx, nc, matrix, panels, inverses, pivots):
+def per_device(ny, nz, nx, nc, matrix, panels, inverses, pivots):
+    nzx = nz * nx
     local, width = matrix.shape
     held = panels.shape[1]
     y, core = lax.axis_index("y"), lax.axis_index("c")
@@ -147,50 +143,55 @@
     first1 = first.reshape(1).astype(jnp.int32)
     core1 = core.reshape(1).astype(jnp.int32)
 
-    mine = spread(panels.reshape(STEPS * held, NB), ("z", "x"), nzx)
-    other = lax.ppermute(mine, "c", swap)
-    mine, other = (a.reshape(nzx, STEPS, held, NB) for a in (mine, other))
-    both = jnp.stack([jnp.where(core == 0, mine, other), jnp.where(core == 0, other, mine)], axis=1)
-    full = both.transpose(2, 0, 1, 3, 4).reshape(STEPS, local, NB)
-
-    picked, tops, select = pl.pallas_call(
+    share, select = pl.pallas_call(
         prep_kernel,
-        out_shape=(
-            jax.ShapeDtypeStruct((TOP, width), BF),
-            jax.ShapeDtypeStruct((TOP, width), BF),
-            jax.ShapeDtypeStruct((2 * NB, start_of(STEPS)), BF),
-        ),
+        out_shape=(jax.ShapeDtypeStruct((2, TOP, width), BF), jax.ShapeDtypeStruct((2 * NB, start_of(STEPS)), BF)),
         in_specs=[SM, VM, VM, VM],
-        out_specs=(VM, VM, VM),
+        out_specs=(VM, VM),
         cost_estimate=cost(2 * TOP * local * width, 8 << 20),
     )(first1, pivots, pivots.reshape(TOP, 1), matrix)
-    share = jnp.concatenate([picked.reshape(ny, TOP // ny, width), tops.reshape(ny, TOP // ny, width)], axis=1)
-    got = lax.all_to_all(share, "y", 0, 0, tiled=True)
-    content = spread(got.astype(F32).sum(0).astype(BF), "y", ny)
-
-    idx = []
-    for k, j in PAIRS:
-        for rows in (pivots[k], k * NB + jnp.arange(NB, dtype=jnp.int32)):
-            here = rows - first
-            idx.append(jnp.where((here >= 0) & (here < local), here + j * local, -1))
-    per_dev = len(idx) * NB // (nzx * nc)
-    chunk = -(-per_dev // CHUNK) * CHUNK
-    idx = jnp.concatenate(idx + [jnp.full((chunk * nzx * nc - len(idx) * NB,), -1, jnp.int32)])
-    idx = lax.dynamic_slice(idx, ((core * nzx + zx) * chunk,), (chunk,))
-    part = jnp.take(full.reshape(STEPS * local, NB), jnp.maximum(idx, 0), axis=0)
-    part = jnp.where((idx >= 0)[:, None], part, jnp.zeros((), BF))
-    part = spread(part, "y", ny).astype(F32).reshape(ny, chunk, NB).sum(0).astype(BF)
-    low_mine = spread(part, ("z", "x"), nzx)
-    low_other = lax.ppermute(low_mine, "c", swap)
-
-    factor, kept = pl.pallas_call(
-        rows_kernel,
-        out_shape=(jax.ShapeDtypeStruct((local, 2 * TOP), BF), jax.ShapeDtypeStruct((local, width), BF)),
-        in_specs=[SM, VM, VM, VM],
-        out_specs=(VM, VM),
-        cost_estimate=cost(2 * TOP * local * NB, 12 << 20),
-    )(first1, pivots, full, matrix)
-
+    content = lax.psum(share, "y")
+
+    mine = spread(panels.reshape(STEPS * held, NB), "z", nz)
+    mine, pivots, _ = lax.optimization_barrier((mine, pivots, share))
+
+    def gather(mine, pivots):
+        mine = spread(mine, "x", nx)
+        other = lax.ppermute(mine, "c", swap)
+        mine, other = (a.reshape(nx, nz, STEPS, held, NB) for a in (mine, other))
+        both = jnp.stack([jnp.where(core == 0, mine, other), jnp.where(core == 0, other, mine)])
+        full = both.transpose(3, 2, 1, 0, 4, 5).reshape(STEPS, local, NB)
+
+        idx = []
+        for k, j in PAIRS:
+            for rows in (pivots[k], k * NB + jnp.arange(NB, dtype=jnp.int32)):
+                here = rows - first
+                idx.append(jnp.where((here >= 0) & (here < local), here + j * local, -1))
+        per_dev = len(idx) * NB // (nzx * nc)
+        chunk = -(-per_dev // CHUNK) * CHUNK
+        idx = jnp.concatenate(idx + [jnp.full((chunk * nzx * nc - len(idx) * NB,), -1, jnp.int32)])
+        idx = lax.dynamic_slice(idx, ((core * nzx + zx) * chunk,), (chunk,))
+        part = jnp.take(full.reshape(STEPS * local, NB), jnp.maximum(idx, 0), axis=0)
+        part = jnp.where((idx >= 0)[:, None], part, jnp.zeros((), BF))
+        part = spread(part, "y", ny).reshape(ny, chunk, NB).astype(F32).sum(0).astype(BF)
+        low_mine = spread(part, ("z", "x"), nzx)
+        low_other = lax.ppermute(low_mine, "c", swap)
+
+        factor, kept = pl.pallas_call(
+            rows_kernel,
+            out_shape=(jax.ShapeDtypeStruct((local, 2 * TOP), BF), jax.ShapeDtypeStruct((local, width), BF)),
+            in_specs=[SM, VM, VM, VM],
+            out_specs=(VM, VM),
+            cost_estimate=cost(2 * TOP * local * NB, 12 << 20),
+        )(first1, pivots, full, matrix)
+        return low_mine, low_other, factor, kept
+
+    def nothing(mine, pivots):
+        return tuple(jnp.zeros(o.shape, o.dtype) for o in jax.eval_shape(gather, mine, pivots))
+
+    low_mine, low_other, factor, kept = lax.cond(pivots[0, 0] > 0, gather, nothing, mine, pivots)
+
+    chunk = low_mine.size // (nzx * NB)
     return pl.pallas_call(
         solve_kernel,
         out_shape=jax.ShapeDtypeStruct((local, width), BF),
@@ -205,7 +206,7 @@
             pltpu.SemaphoreType.DMA((2,)),
         ],
         cost_estimate=cost(4 * TOP * local * width, 16 << 20),
-    )(core1, content.reshape(ny, 2 * TOP // ny, width), low_mine.reshape(nzx, chunk, NB), low_other.reshape(nzx, chunk, NB),
+    )(core1, content, low_mine.reshape(nzx, chunk, NB), low_other.reshape(nzx, chunk, NB),
       inverses, select, factor, kept)
 
 
@@ -216,5 +217,5 @@
     cols = ("z", "x", "c")
     in_specs = (P("y", cols), P(None, ("y",) + cols, None), P(), P())
     return jax.shard_map(
-        functools.partial(per_device, ny, nz * nx, nc), mesh=fine, in_specs=in_specs, out_specs=P("y", cols), check_vma=False
+        functools.partial(per_device, ny, nz, nx, nc), mesh=fine, in_specs=in_specs, out_specs=P("y", cols), check_vma=False
     )

time: 179 us -> 128 us (0.72); the launches traced: 177 us -> 128 us
  waiting for transfers between devices: 103 us -> 27 us
  blocking collectives: 0 us -> 38.3 us
  starting transfers between devices: 39.8 us -> 18.9 us
  between operations: 0.35 us -> 14.1 us
  other arithmetic: 3.4 us -> 0.86 us
    all_to_all x4 -> x2, waiting for transfers between devices: 69.3 us -> 18.5 us  [spread(): lax.all_to_all(jnp.broadcast_to(x[None], (parts,) + x.shape), axes, 0, 0,...]
    all_to_all x0 -> x2, blocking collectives: none -> 38.3 us  [spread(): lax.all_to_all(jnp.broadcast_to(x[None], (parts,) + x.shape), axes, 0, 0,...]
    all_to_all x1 -> x0, waiting for transfers between devices: 31.3 us -> none  [per_device(): got = lax.all_to_all(share, 'y', 0, 0, tiled=True)]
    all_to_all x4 -> x2, starting transfers between devices: 29.8 us -> 15.1 us  [spread(): lax.all_to_all(jnp.broadcast_to(x[None], (parts,) + x.shape), axes, 0, 0,...]
    all_to_all x1 -> x0, starting transfers between devices: 6.22 us -> none  [per_device(): got = lax.all_to_all(share, 'y', 0, 0, tiled=True)]
    psum x0 -> x1, waiting for transfers between devices: none -> 5.88 us  [per_device(): content = lax.psum(share, 'y')]
    concatenate x1 -> x0, other arithmetic: 2.38 us -> none  [per_device(): jnp.concatenate([picked.reshape(ny, TOP // ny, width), tops.reshape(ny, T...]
  transfers between devices with their start and end apart: 7 -> 5, of which waited for: 6 -> 4; matrix products, arithmetic and copies ran while one was open for 2% -> 5% of each run, Pallas kernels for 7% -> 9%
where the time goes in v3:
time: 128 us
  blocking collectives  38.3 us (30%)
  waiting for transfers between devices  27 us (21%)
  Pallas kernels  21.6 us (17%)
  starting transfers between devices  18.9 us (15%)
  between operations  14.1 us (11%)
  local copies, waits for them, and re-layouts  6.68 us (5%)
    all_to_all x2, blocking collectives, spread(): lax.all_to_all(jnp.broadcast_to(x[None], (parts,) + x.shape), axes, 0, 0,...  38.3 us
    all_to_all x2, waiting for transfers between devices, spread(): lax.all_to_all(jnp.broadcast_to(x[None], (parts,) + x.shape), axes, 0, 0,...  18.5 us
    all_to_all x2, starting transfers between devices, spread(): lax.all_to_all(jnp.broadcast_to(x[None], (parts,) + x.shape), axes, 0, 0,...  15.1 us
    pallas_call x1, Pallas kernels, per_device(): pl.pallas_call(solve_kernel, out_shape=jax.ShapeDtypeStruct((local, width...  9.75 us
    pallas_call x1, Pallas kernels, gather(): pl.pallas_call(rows_kernel, out_shape=(jax.ShapeDtypeStruct((local, 2 * T...  7.08 us
    psum x1, waiting for transfers between devices, per_device(): content = lax.psum(share, 'y')  5.88 us
    pallas_call x1, Pallas kernels, per_device(): pl.pallas_call(prep_kernel, out_shape=(jax.ShapeDtypeStruct((2, TOP, widt...  4.76 us
    broadcast_in_dim x4, local copies, waits for them, and re-layouts, spread(): jnp.broadcast_to(x[None], (parts,) + x.shape)  3.05 us
  transfers between devices with their start and end apart: 5, of which 4 were waited for; matrix products, arithmetic and copies ran while one was open for 5% of the time, Pallas kernels for 9%

profile of v3, /device:TPU:6, one launch (start us, length us, event | category | flops | bytes accessed | tf_op | source)
XLA Modules:
  0.0 127.8 jit_solution(12172757113987918624)
XLA Ops:
  6.5 1.6 %broadcast_in_dim.84 = bf16[8,144,128]{2,1,0:T(8,128)(2,1)} broadcast(bf16[144,128]{1,0:T(8,128)(2,1)} %bitcast.121), dimensions={1,2} | broadcast | bytes 331776 | tf_op jit(solution)/shard_map/broadcast_in_dim | solution.py:132
  8.2 10.3 %all-to-all-start.3 = ((bf16[8,144,128]{2,1,0:T(8,128)(2,1)}), bf16[8,144,128]{2,1,0:T(8,128)(2,1)S(1)}, u32[]{:S(2)}, u32[]{:S(2)}) async-start(bf16[8,144,128]{2,1,0:T(8,128)(2,1)} %broadcast_in_dim.84), calls=%async_computation.3 | async-start | bytes 589824 | tf_op jit(solution)/shard_map/all_to_all | solution.py:132
  18.5 0.7 copy.14
  19.2 0.9 copy.12
  20.2 4.8 %shard_map.46 = (bf16[2,768,384]{2,1,0:T(8,128)(2,1)}, bf16[256,3840]{1,0:T(8,128)(2,1)}) custom-call(s32[1]{0:T(128)} %bitcast.11.first_ref, s32[6,128]{1,0:T(8,128)S(1)} %copy-done.3, s32[768,1]{1,0:T(8,128)} %bitcast.120, bf16[1536,384]{1,0:T(8,128)(2,1)S(1)} %copy-done.1), custom_call_target="tpu_custom_call" | custom-call | flops 905969664 | bytes 8388608 | tf_op jit(solution)/shard_map/pallas_call | solution.py:146
  24.9 6.1 %all-to-all-done.3 = bf16[8,144,128]{2,1,0:T(8,128)(2,1)S(1)} async-done(((bf16[8,144,128]{2,1,0:T(8,128)(2,1)}), bf16[8,144,128]{2,1,0:T(8,128)(2,1)S(1)}, u32[]{:S(2)}, u32[]{:S(2)}) %all-to-all-start.3) | async-done | bytes 294944 | tf_op jit(solution)/shard_map/all_to_all | solution.py:132
  31.1 0.6 slice.12
  32.3 73.0 %conditional.1 = (bf16[32,64,128]{2,1,0:T(8,128)(2,1)}, bf16[32,64,128]{2,1,0:T(8,128)(2,1)}, bf16[1536,1536]{1,0:T(8,128)(2,1)}, bf16[1536,384]{1,0:T(8,128)(2,1)S(1)}) conditional(s32[]{:T(128)} %bitcast.13, () %tuple.16, (s32[6,128]{1,0:T(8,128)S(1)}, s32[]{:T(128)}, s32[]{:T(128)}, s32[]{:T(128)}, s32[]{:T(128)}, ...), branch_computations={%region_1.0_spmd, %region_2.4_spmd} | conditional | flops 304446912 | bytes 54966420 | solution.py:192
  32.4 1.3 %broadcast_in_dim.75 = bf16[4,8,144,128]{3,2,1,0:T(8,128)(2,1)} broadcast(bf16[8,144,128]{2,1,0:T(8,128)(2,1)S(1)} %get-tuple-element.29), dimensions={1,2,3} | broadcast | bytes 1474560 | tf_op jit(solution)/shard_map/cond/branch_1_fun/broadcast_in_dim | solution.py:132
  33.8 4.8 %all-to-all-start = ((bf16[4,8,144,128]{3,2,1,0:T(8,128)(2,1)}), bf16[4,8,144,128]{3,2,1,0:T(8,128)(2,1)S(1)}, u32[]{:S(2)}, u32[]{:S(2)}) async-start(bf16[4,8,144,128]{3,2,1,0:T(8,128)(2,1)} %broadcast_in_dim.75), calls=%async_computation | async-start | bytes 2359296 | tf_op jit(solution)/shard_map/cond/branch_1_fun/all_to_all | solution.py:132
  38.9 12.4 %all-to-all-done = bf16[4,8,144,128]{3,2,1,0:T(8,128)(2,1)S(1)} async-done(((bf16[4,8,144,128]{3,2,1,0:T(8,128)(2,1)}), bf16[4,8,144,128]{3,2,1,0:T(8,128)(2,1)S(1)}, u32[]{:S(2)}, u32[]{:S(2)}) %all-to-all-start) | async-done | bytes 1179680 | tf_op jit(solution)/shard_map/cond/branch_1_fun/all_to_all | solution.py:132
  51.3 1.9 %collective-permute-start = (bf16[4,8,144,128]{3,2,1,0:T(8,128)(2,1)S(1)}, bf16[4,8,144,128]{3,2,1,0:T(8,128)(2,1)S(1)}, u32[]{:S(2)}, u32[]{:S(2)}) collective-permute-start(bf16[4,8,144,128]{3,2,1,0:T(8,128)(2,1)S(1)} %all-to-all-done), channel_id=1, source_target_pairs={{0,1},{1,0},{2,3},{3,2},{4,5},{5,4},{6,7},{7,6},{8,9},{9,8},{10,11... | collective-permute-start | bytes 3538952 | tf_op jit(solution)/shard_map/cond/branch_1_fun/ppermute | solution.py:160
  53.4 2.6 %collective-permute-done = bf16[4,8,144,128]{3,2,1,0:T(8,128)(2,1)S(1)} collective-permute-done((bf16[4,8,144,128]{3,2,1,0:T(8,128)(2,1)S(1)}, bf16[4,8,144,128]{3,2,1,0:T(8,128)(2,1)S(1)}, u32[]{:S(2)}, u32[]{:S(2)}) %collective-permute-start) | collective-permute-done | bytes 1179680 | tf_op jit(solution)/shard_map/cond/branch_1_fun/ppermute | solution.py:160
  56.0 0.2 broadcast_select_fusion.1
  56.2 0.2 maximum_bitcast_fusion
  56.4 0.7 copy.8
  57.1 0.6 gather_fusion
  57.8 16.3 %all_to_all.17 = bf16[8,64,128]{2,1,0:T(8,128)(2,1)S(1)} all-to-all(bf16[8,64,128]{2,1,0:T(8,128)(2,1)S(1)} %broadcast_in_dim.79), channel_id=1, replica_groups=mesh['y'=8,'z'=8,'x'=4,'c'=2] {'y'}, dimensions={0} | all-to-all | bytes 262144 | tf_op jit(solution)/shard_map/cond/branch_1_fun/all_to_all | solution.py:132
  74.1 0.1 broadcast_in_dim.80
  74.2 22.0 %all_to_all.18 = bf16[32,64,128]{2,1,0:T(8,128)(2,1)} all-to-all(bf16[32,64,128]{2,1,0:T(8,128)(2,1)S(1)} %broadcast_in_dim.80), channel_id=1, replica_groups=mesh['y'=8,'z'=8,'x'=4,'c'=2] {'z','x'}, dimensions={0} | all-to-all | bytes 1048576 | tf_op jit(solution)/shard_map/cond/branch_1_fun/all_to_all | solution.py:132
  96.3 1.9 %collective-permute-start.1 = (bf16[32,64,128]{2,1,0:T(8,128)(2,1)}, bf16[32,64,128]{2,1,0:T(8,128)(2,1)}, u32[]{:S(2)}, u32[]{:S(2)}) collective-permute-start(bf16[32,64,128]{2,1,0:T(8,128)(2,1)} %all_to_all.18), channel_id=1, source_target_pairs={{0,1},{1,0},{2,3},{3,2},{4,5},{5,4},{6,7},{7,6},{8,9},{9,8},{10,11... | collective-permute-start | bytes 1572872 | tf_op jit(solution)/shard_map/cond/branch_1_fun/ppermute | solution.py:178
  98.2 7.1 %branch_1_fun.1 = (bf16[1536,1536]{1,0:T(8,128)(2,1)}, bf16[1536,384]{1,0:T(8,128)(2,1)S(1)}) custom-call(s32[1]{0:T(128)} %get-tuple-element.30.first_ref, s32[6,128]{1,0:T(8,128)S(1)} %get-tuple-element.24.rows_ref, bf16[6,1536,128]{2,1,0:T(8,128)(2,1)} %bitcast.117, bf16[1536,384]{1,0:T(8,128)(2,1)} %copy-done.2), custom_call_target="tpu_custom_call" | custom-call | flops 301989888 | bytes 12582912 | tf_op jit(solution)/shard_map/cond/branch_1_fun/pallas_call | solution.py:180
  105.3 5.9 %all-reduce.2.cloned.1.call-done.content = bf16[2,768,384]{2,1,0:T(8,128)(2,1)} async-done(((bf16[2,768,384]{2,1,0:T(8,128)(2,1)}), bf16[2,768,384]{2,1,0:T(8,128)(2,1)}) %all-reduce.2.cloned.1.call-update) | async-done | bytes 1179664 | tf_op jit(solution)/shard_map/psum | solution.py:153
  111.2 9.8 %shard_map.47 = bf16[1536,384]{1,0:T(8,128)(2,1)} custom-call(s32[1]{0:T(128)} %bitcast.10.core_ref, bf16[2,768,384]{2,1,0:T(8,128)(2,1)} %all-reduce.2.cloned.1.call-done.content, bf16[32,64,128]{2,1,0:T(8,128)(2,1)} %get-tuple-element.45.mine_ref, bf16[32,64,128]{2,1,0:T(8,128)(2,1)} %get-tuple-element.46.other_ref, f32[6,128,128]{2,1,0:T(8,128)} %inverses_ref.1, ...), custom_call_target="tpu_custom_call" | custom-call | flops 1811939328 | bytes 16777216 | tf_op jit(solution)/shard_map/pallas_call | solution.py:195
  (48 shorter events, 0.7 us)
Async XLA Ops:
  6.5 13.6 %copy-start.3 = (s32[6,128]{1,0:T(8,128)S(1)}, s32[6,128]{1,0:T(8,128)}, u32[]{:S(2)}) copy-start(s32[6,128]{1,0:T(8,128)} %rows_ref.1) | copy-start | bytes 9220
  6.5 13.6 %copy-start.1 = (bf16[1536,384]{1,0:T(8,128)(2,1)S(1)}, bf16[1536,384]{1,0:T(8,128)(2,1)}, u32[]{:S(2)}) copy-start(bf16[1536,384]{1,0:T(8,128)(2,1)} %matrix_ref.1) | copy-start | bytes 3538948
  8.2 22.9 %all-to-all-start.3 = ((bf16[8,144,128]{2,1,0:T(8,128)(2,1)}), bf16[8,144,128]{2,1,0:T(8,128)(2,1)S(1)}, u32[]{:S(2)}, u32[]{:S(2)}) async-start(bf16[8,144,128]{2,1,0:T(8,128)(2,1)} %broadcast_in_dim.84), calls=%async_computation.3 | async-start | bytes 589824 | tf_op jit(solution)/shard_map/all_to_all | solution.py:132
  18.5 92.7 %all-reduce.2.cloned.1.call-start = ((), (), s32[]{:S(2)}) async-start(), calls=%async_computation.4 | async-start | bytes 2359296 | tf_op jit(solution)/shard_map/psum | solution.py:153
  32.4 1.4 %copy-start.2 = (bf16[1536,384]{1,0:T(8,128)(2,1)}, bf16[1536,384]{1,0:T(8,128)(2,1)S(1)}, u32[]{:S(2)}) copy-start(bf16[1536,384]{1,0:T(8,128)(2,1)S(1)} %get-tuple-element.31.matrix_ref) | copy-start | bytes 3538948 | tf_op jit(solution)/shard_map/cond
  33.8 17.5 %all-to-all-start = ((bf16[4,8,144,128]{3,2,1,0:T(8,128)(2,1)}), bf16[4,8,144,128]{3,2,1,0:T(8,128)(2,1)S(1)}, u32[]{:S(2)}, u32[]{:S(2)}) async-start(bf16[4,8,144,128]{3,2,1,0:T(8,128)(2,1)} %broadcast_in_dim.75), calls=%async_computation | async-start | bytes 2359296 | tf_op jit(solution)/shard_map/cond/branch_1_fun/all_to_all | solution.py:132
  51.3 4.7 %collective-permute-start = (bf16[4,8,144,128]{3,2,1,0:T(8,128)(2,1)S(1)}, bf16[4,8,144,128]{3,2,1,0:T(8,128)(2,1)S(1)}, u32[]{:S(2)}, u32[]{:S(2)}) collective-permute-start(bf16[4,8,144,128]{3,2,1,0:T(8,128)(2,1)S(1)} %all-to-all-done), channel_id=1, source_target_pairs={{0,1},{1,0},{2,3},{3,2},{4,5},{5,4},{6,7},{7,6},{8,9},{9,8},{10,11... | collective-permute-start | bytes 3538952 | tf_op jit(solution)/shard_map/cond/branch_1_fun/ppermute | solution.py:160
  57.1 41.1 %copy-start = (bf16[6,8,4,2,24,128]{5,4,3,2,1,0:T(8,128)(2,1)}, bf16[6,8,4,2,24,128]{5,4,3,2,1,0:T(8,128)(2,1)S(1)}, u32[]{:S(2)}) copy-start(bf16[6,8,4,2,24,128]{5,4,3,2,1,0:T(8,128)(2,1)S(1)} %copy.8) | copy-start | bytes 7077892 | tf_op jit(solution)/shard_map/cond
  96.3 9.0 %collective-permute-start.1 = (bf16[32,64,128]{2,1,0:T(8,128)(2,1)}, bf16[32,64,128]{2,1,0:T(8,128)(2,1)}, u32[]{:S(2)}, u32[]{:S(2)}) collective-permute-start(bf16[32,64,128]{2,1,0:T(8,128)(2,1)} %all_to_all.18), channel_id=1, source_target_pairs={{0,1},{1,0},{2,3},{3,2},{4,5},{5,4},{6,7},{7,6},{8,9},{9,8},{10,11... | collective-permute-start | bytes 1572872 | tf_op jit(solution)/shard_map/cond/branch_1_fun/ppermute | solution.py:178
Sparse Core Ops, SparseCore 0:
  31.2 79.9 all-reduce.1

commit v4 on v3

--- a/solution.py
+++ b/solution.py
@@ -28,25 +28,34 @@
     return lax.broadcasted_iota(jnp.int32, shape, dim)
 
 
-def prep_kernel(first_ref, rows_ref, cols_ref, matrix_ref, share_ref, select_ref):
+def columns(row):
+    return jnp.broadcast_to(row.astype(F32), (NB, NB)).T.astype(jnp.int32)
+
+
+def masks(k, rows_ref):
+    ones = jnp.ones((NB, NB), BF)
+    ids = jnp.concatenate([iota((NB, NB), 0) + k * NB, columns(rows_ref[k:k + 1, :])])
+    found = jnp.zeros((2 * NB, NB), F32)
+    out = []
+    for j in reversed(range(k)):
+        same = jnp.where(ids == rows_ref[j:j + 1, :], 1.0, 0.0).astype(F32)
+        live = 1.0 - found
+        out.append((j, same * live, live))
+        hit = jnp.dot(same.astype(BF), ones, preferred_element_type=F32)
+        found = jnp.maximum(found, hit)
+    return ids, out, found < 0.5
+
+
+def share_kernel(first_ref, rows_ref, matrix_ref, share_ref, hot):
     first = first_ref[0]
-    ones = jnp.ones((NB, NB), BF)
     local, width = matrix_ref.shape
     for k in range(STEPS):
-        ids = jnp.concatenate([iota((NB, NB), 0) + k * NB, jnp.broadcast_to(cols_ref[k * NB:(k + 1) * NB, :], (NB, NB))])
-        found = jnp.zeros((2 * NB, NB), F32)
-        for j in reversed(range(k)):
-            at = start_of(k) + 2 * NB * j
-            same = jnp.where(ids == rows_ref[j:j + 1, :], 1.0, 0.0).astype(F32)
-            live = 1.0 - found
-            select_ref[:, at:at + NB] = (same * live).astype(BF)
-            select_ref[:, at + NB:at + 2 * NB] = (-live).astype(BF)
-            hit = jnp.dot(same.astype(BF), ones, preferred_element_type=F32)
-            found = jnp.maximum(found, hit)
-        fresh = found < 0.5
+        ids, _, fresh = masks(k, rows_ref)
         at = k * NB
-        hot = jnp.where(iota((NB, local), 1) == cols_ref[at:at + NB, :] - first, 1.0, 0.0).astype(BF)
-        row = jnp.dot(hot, matrix_ref[...], preferred_element_type=F32)
+        where = ids[NB:] - first
+        for c in range(0, local, NB):
+            hot[:, c:c + NB] = jnp.where(iota((NB, NB), 1) + c == where, 1.0, 0.0).astype(BF)
+        row = jnp.dot(hot[...], matrix_ref[...], preferred_element_type=F32)
         mine = fresh[:NB] & (first == 0)
         for c in range(0, width, NB):
             top = matrix_ref[at:at + NB, c:c + NB].astype(F32)
@@ -54,7 +63,12 @@
             share_ref[1, at:at + NB, c:c + NB] = jnp.where(fresh[NB:], row[:, c:c + NB], 0.0).astype(BF)
 
 
-def rows_kernel(first_ref, rows_ref, panels_ref, matrix_ref, factor_ref, kept_ref):
+def rows_kernel(first_ref, rows_ref, panels_ref, matrix_ref, factor_ref, kept_ref, select_ref):
+    for k in range(1, STEPS):
+        for j, same, live in masks(k, rows_ref)[1]:
+            at = start_of(k) + 2 * NB * j
+            select_ref[:, at:at + NB] = same.astype(BF)
+            select_ref[:, at + NB:at + 2 * NB] = (-live).astype(BF)
     ones = jnp.ones((NB, NB), BF)
     height = 2 * NB
 
@@ -143,53 +157,61 @@
     first1 = first.reshape(1).astype(jnp.int32)
     core1 = core.reshape(1).astype(jnp.int32)
 
-    share, select = pl.pallas_call(
-        prep_kernel,
-        out_shape=(jax.ShapeDtypeStruct((2, TOP, width), BF), jax.ShapeDtypeStruct((2 * NB, start_of(STEPS)), BF)),
-        in_specs=[SM, VM, VM, VM],
-        out_specs=(VM, VM),
-        cost_estimate=cost(2 * TOP * local * width, 8 << 20),
-    )(first1, pivots, pivots.reshape(TOP, 1), matrix)
+    share = pl.pallas_call(
+        share_kernel,
+        out_shape=jax.ShapeDtypeStruct((2, TOP, width), BF),
+        in_specs=[SM, VM, VM],
+        out_specs=VM,
+        scratch_shapes=[pltpu.VMEM((NB, local), BF)],
+        cost_estimate=cost(2 * TOP * local * width, 4 << 20),
+    )(first1, pivots, matrix)
     content = lax.psum(share, "y")
-
-    mine = spread(panels.reshape(STEPS * held, NB), "z", nz)
-    mine, pivots, _ = lax.optimization_barrier((mine, pivots, share))
-
-    def gather(mine, pivots):
+    panels, pivots, _ = lax.optimization_barrier((panels, pivots, share))
+
+    def gather(panels, pivots):
+        mine = spread(panels.reshape(STEPS * held, NB), "z", nz)
         mine = spread(mine, "x", nx)
-        other = lax.ppermute(mine, "c", swap)
-        mine, other = (a.reshape(nx, nz, STEPS, held, NB) for a in (mine, other))
-        both = jnp.stack([jnp.where(core == 0, mine, other), jnp.where(core == 0, other, mine)])
-        full = both.transpose(3, 2, 1, 0, 4, 5).reshape(STEPS, local, NB)
 
         idx = []
         for k, j in PAIRS:
             for rows in (pivots[k], k * NB + jnp.arange(NB, dtype=jnp.int32)):
                 here = rows - first
-                idx.append(jnp.where((here >= 0) & (here < local), here + j * local, -1))
-        per_dev = len(idx) * NB // (nzx * nc)
-        chunk = -(-per_dev // CHUNK) * CHUNK
+                pb = here // held
+                at = ((pb // nc % nx * nz + pb // nc // nx) * STEPS + j) * held + here % held
+                idx.append(jnp.where((here >= 0) & (here < local) & (pb % nc == core), at, -1))
+        chunk = -(-len(idx) * NB // (nzx * nc) // CHUNK) * CHUNK
         idx = jnp.concatenate(idx + [jnp.full((chunk * nzx * nc - len(idx) * NB,), -1, jnp.int32)])
-        idx = lax.dynamic_slice(idx, ((core * nzx + zx) * chunk,), (chunk,))
-        part = jnp.take(full.reshape(STEPS * local, NB), jnp.maximum(idx, 0), axis=0)
-        part = jnp.where((idx >= 0)[:, None], part, jnp.zeros((), BF))
-        part = spread(part, "y", ny).reshape(ny, chunk, NB).astype(F32).sum(0).astype(BF)
+        idx = lax.dynamic_slice(idx.reshape(nc, nzx, chunk), (0, zx, 0), (nc, 1, chunk)).reshape(nc * chunk)
+        part = jnp.take(mine.reshape(-1, NB), jnp.maximum(idx, 0), axis=0)
+        part = jnp.where((idx >= 0)[:, None], part, jnp.zeros((), BF)).reshape(1, nc, chunk, NB)
+        part = jnp.broadcast_to(part, (ny, nc, chunk, NB)).reshape(ny * nc, chunk, NB)
+        part = lax.all_to_all(part, ("y", "c"), 0, 0, tiled=True).astype(F32).sum(0).astype(BF)
+
+        other = lax.ppermute(mine, "c", swap)
+        part, other = lax.optimization_barrier((part, other))
         low_mine = spread(part, ("z", "x"), nzx)
-        low_other = lax.ppermute(low_mine, "c", swap)
-
-        factor, kept = pl.pallas_call(
+
+        both = [a.reshape(nx, nz, STEPS, held, NB) for a in (mine, other)]
+        both = jnp.stack([jnp.where(core == 0, both[0], both[1]), jnp.where(core == 0, both[1], both[0])])
+        full = both.transpose(3, 2, 1, 0, 4, 5).reshape(STEPS, local, NB)
+        factor, kept, select = pl.pallas_call(
             rows_kernel,
-            out_shape=(jax.ShapeDtypeStruct((local, 2 * TOP), BF), jax.ShapeDtypeStruct((local, width), BF)),
+            out_shape=(
+                jax.ShapeDtypeStruct((local, 2 * TOP), BF),
+                jax.ShapeDtypeStruct((local, width), BF),
+                jax.ShapeDtypeStruct((2 * NB, start_of(STEPS)), BF),
+            ),
             in_specs=[SM, VM, VM, VM],
-            out_specs=(VM, VM),
+            out_specs=(VM, VM, VM),
             cost_estimate=cost(2 * TOP * local * NB, 12 << 20),
         )(first1, pivots, full, matrix)
-        return low_mine, low_other, factor, kept
-
-    def nothing(mine, pivots):
-        return tuple(jnp.zeros(o.shape, o.dtype) for o in jax.eval_shape(gather, mine, pivots))
-
-    low_mine, low_other, factor, kept = lax.cond(pivots[0, 0] > 0, gather, nothing, mine, pivots)
+        low_mine, factor, kept, select = lax.optimization_barrier((low_mine, factor, kept, select))
+        return low_mine, lax.ppermute(low_mine, "c", swap), factor, kept, select
+
+    def nothing(panels, pivots):
+        return tuple(jnp.zeros(o.shape, o.dtype) for o in jax.eval_shape(gather, panels, pivots))
+
+    low_mine, low_other, factor, kept, select = lax.cond(pivots[0, 0] > 0, gather, nothing, panels, pivots)
 
     chunk = low_mine.size // (nzx * NB)
     return pl.pallas_call(

time: 128 us -> 125 us (0.977); the launches traced: 128 us -> 123 us
  blocking collectives: 38.3 us -> 18.6 us
  starting transfers between devices: 18.9 us -> 26.1 us
  waiting for transfers between devices: 27 us -> 33.1 us
  other arithmetic: 0.86 us -> 3.07 us
    all_to_all x2 -> x1, blocking collectives: 38.3 us -> 18.6 us  [gather(): lax.all_to_all(part, ('y', 'c'), 0, 0, tiled=True).astype(F32).sum(0)]
    all_to_all x2 -> x3, waiting for transfers between devices: 18.5 us -> 31 us  [spread(): lax.all_to_all(jnp.broadcast_to(x[None], (parts,) + x.shape), axes, 0, 0,...]
    all_to_all x2 -> x3, starting transfers between devices: 15.1 us -> 22.2 us  [spread(): lax.all_to_all(jnp.broadcast_to(x[None], (parts,) + x.shape), axes, 0, 0,...]
    psum x1, waiting for transfers between devices: 5.88 us -> 0.01 us  [per_device(): content = lax.psum(share, 'y')]
    ppermute x1, waiting for transfers between devices: 2.6 us -> 0.01 us  [gather(): other = lax.ppermute(mine, 'c', swap)]
    ppermute x1, waiting for transfers between devices: 0.01 us -> 2.11 us  [gather(): return (low_mine, lax.ppermute(low_mine, 'c', swap), factor, kept, select)]
    transpose x1, local copies, waits for them, and re-layouts: 0.66 us -> 2.1 us  [gather(): full = both.transpose(3, 2, 1, 0, 4, 5).reshape(STEPS, local, NB)]
    select_n x2, other arithmetic: 0.24 us -> 1.53 us  [the longest x1 1.43 us: gather(): jnp.where(core == 0, both[0], both[1])]
  transfers between devices with their start and end apart: 5 -> 6, of which waited for: 4 -> 4; matrix products, arithmetic and copies ran while one was open for 5% -> 8% of each run, Pallas kernels for 9% -> 6%
where the time goes in v4:
time: 125 us; the launch traced here: 123 us
  waiting for transfers between devices  33.1 us (26%)
  starting transfers between devices  26.1 us (21%)
  Pallas kernels  20.9 us (17%)
  blocking collectives  18.6 us (15%)
  between operations  14.1 us (11%)
  local copies, waits for them, and re-layouts  7.24 us (6%)
  other arithmetic  3.07 us (2%)
    all_to_all x3, waiting for transfers between devices, spread(): lax.all_to_all(jnp.broadcast_to(x[None], (parts,) + x.shape), axes, 0, 0,...  31 us
    all_to_all x3, starting transfers between devices, spread(): lax.all_to_all(jnp.broadcast_to(x[None], (parts,) + x.shape), axes, 0, 0,...  22.2 us
    all_to_all x1, blocking collectives, gather(): lax.all_to_all(part, ('y', 'c'), 0, 0, tiled=True).astype(F32).sum(0)  18.6 us
    pallas_call x1, Pallas kernels, per_device(): pl.pallas_call(solve_kernel, out_shape=jax.ShapeDtypeStruct((local, width...  9.04 us
    pallas_call x1, Pallas kernels, gather(): pl.pallas_call(rows_kernel, out_shape=(jax.ShapeDtypeStruct((local, 2 * T...  7.7 us
    pallas_call x1, Pallas kernels, per_device(): pl.pallas_call(share_kernel, out_shape=jax.ShapeDtypeStruct((2, TOP, widt...  4.19 us
    broadcast_in_dim x3, local copies, waits for them, and re-layouts, spread(): jnp.broadcast_to(x[None], (parts,) + x.shape)  2.99 us
  transfers between devices with their start and end apart: 6, of which 4 were waited for; matrix products, arithmetic and copies ran while one was open for 8% of the time, Pallas kernels for 6%

profile of v4, /device:TPU:6, one launch (start us, length us, event | category | flops | bytes accessed | tf_op | source)
XLA Modules:
  0.0 123.2 jit_solution(17147401794033341252)
XLA Ops:
  6.5 4.2 %shard_map.46 = bf16[2,768,384]{2,1,0:T(8,128)(2,1)} custom-call(s32[1]{0:T(128)} %bitcast.29.first_ref, s32[6,128]{1,0:T(8,128)} %rows_ref.1, bf16[1536,384]{1,0:T(8,128)(2,1)} %matrix_ref.1), custom_call_target="tpu_custom_call" | custom-call | flops 905969664 | bytes 4194304 | tf_op jit(solution)/shard_map/pallas_call | solution.py:160
  10.8 0.7 copy-done.2
  11.4 0.6 slice.12
  12.6 94.7 %conditional.1 = (bf16[32,64,128]{2,1,0:T(8,128)(2,1)}, bf16[32,64,128]{2,1,0:T(8,128)(2,1)}, bf16[1536,1536]{1,0:T(8,128)(2,1)}, bf16[1536,384]{1,0:T(8,128)(2,1)S(1)}, bf16[256,3840]{1,0:T(8,128)(2,1)S(1)}) conditional(s32[]{:T(128)} %bitcast.30, () %tuple.18, (s32[6,128]{1,0:T(8,128)S(1)}, s32[]{:T(128)}, s32[]{:T(128)}, s32[]{:T(128)}, s32[]{:T(128)}, ...), branch_computations={%region_1.0_spmd, %region_2.4_spmd} | conditional | flops 304739584 | bytes 47916052 | solution.py:214
  12.6 0.8 broadcast_in_dim.72
  13.4 10.3 %all-to-all-start = ((bf16[8,144,128]{2,1,0:T(8,128)(2,1)}), bf16[8,144,128]{2,1,0:T(8,128)(2,1)S(1)}, u32[]{:S(2)}, u32[]{:S(2)}) async-start(bf16[8,144,128]{2,1,0:T(8,128)(2,1)} %broadcast_in_dim.72), calls=%async_computation | async-start | bytes 589824 | tf_op jit(solution)/shard_map/cond/branch_1_fun/all_to_all | solution.py:146
  24.8 11.5 %all-to-all-done = bf16[8,144,128]{2,1,0:T(8,128)(2,1)S(1)} async-done(((bf16[8,144,128]{2,1,0:T(8,128)(2,1)}), bf16[8,144,128]{2,1,0:T(8,128)(2,1)S(1)}, u32[]{:S(2)}, u32[]{:S(2)}) %all-to-all-start) | async-done | bytes 294944 | tf_op jit(solution)/shard_map/cond/branch_1_fun/all_to_all | solution.py:146
  36.3 1.2 broadcast_in_dim.73
  37.5 4.8 %all-to-all-start.1 = ((bf16[4,8,144,128]{3,2,1,0:T(8,128)(2,1)}), bf16[4,8,144,128]{3,2,1,0:T(8,128)(2,1)S(1)}, u32[]{:S(2)}, u32[]{:S(2)}) async-start(bf16[4,8,144,128]{3,2,1,0:T(8,128)(2,1)} %broadcast_in_dim.73), calls=%async_computation.1 | async-start | bytes 2359296 | tf_op jit(solution)/shard_map/cond/branch_1_fun/all_to_all | solution.py:146
  42.4 12.6 %all-to-all-done.1 = bf16[4,8,144,128]{3,2,1,0:T(8,128)(2,1)S(1)} async-done(((bf16[4,8,144,128]{3,2,1,0:T(8,128)(2,1)}), bf16[4,8,144,128]{3,2,1,0:T(8,128)(2,1)S(1)}, u32[]{:S(2)}, u32[]{:S(2)}) %all-to-all-start.1) | async-done | bytes 1179680 | tf_op jit(solution)/shard_map/cond/branch_1_fun/all_to_all | solution.py:146
  55.0 1.9 %collective-permute-start = (bf16[4,8,144,128]{3,2,1,0:T(8,128)(2,1)S(1)}, bf16[4,8,144,128]{3,2,1,0:T(8,128)(2,1)S(1)}, u32[]{:S(2)}, u32[]{:S(2)}) collective-permute-start(bf16[4,8,144,128]{3,2,1,0:T(8,128)(2,1)S(1)} %all-to-all-done.1), channel_id=1, source_target_pairs={{0,1},{1,0},{2,3},{3,2},{4,5},{5,4},{6,7},{7,6},{8,9},{9,8},{10,11... | collective-permute-start | bytes 3538952 | tf_op jit(solution)/shard_map/cond/branch_1_fun/ppermute | solution.py:190
  57.1 0.7 gather_fusion
  57.9 0.1 select_select_fusion
  58.0 18.6 %all_to_all.16 = bf16[16,64,128]{2,1,0:T(8,128)(2,1)S(1)} all-to-all(bf16[16,64,128]{2,1,0:T(8,128)(2,1)S(1)} %bitcast.333), channel_id=1, replica_groups=mesh['y'=8,'z'=8,'x'=4,'c'=2] {'y','c'}, dimensions={0} | all-to-all | bytes 524288 | tf_op jit(solution)/shard_map/cond/branch_1_fun/all_to_all | solution.py:188
  76.6 1.1 broadcast_in_dim.77
  77.7 7.1 %all-to-all-start.3 = ((bf16[32,64,128]{2,1,0:T(8,128)(2,1)}), bf16[32,64,128]{2,1,0:T(8,128)(2,1)}, u32[]{:S(2)}, u32[]{:S(2)}) async-start(bf16[32,64,128]{2,1,0:T(8,128)(2,1)} %broadcast_in_dim.77), calls=%async_computation.3 | async-start | bytes 1048576 | tf_op jit(solution)/shard_map/cond/branch_1_fun/all_to_all | solution.py:146
  84.8 1.4 %broadcast_select_fusion.1 = (bf16[4,8,144,128]{3,2,1,0:T(8,128)(2,1)S(1)}, bf16[4,8,144,128]{3,2,1,0:T(8,128)(2,1)S(1)}) fusion(bf16[4,8,144,128]{3,2,1,0:T(8,128)(2,1)S(1)} %all-to-all-done.1, bf16[4,8,144,128]{3,2,1,0:T(8,128)(2,1)} %copy-done, pred[]{:T(512)S(6)} %eq.176), kind=kLoop, calls=%fused_computation.3 | loop fusion | flops 1179648 | bytes 4718593 | tf_op jit(solution)/shard_map/cond/branch_1_fun/jit(_where)/select_n | solution.py:195
  86.3 0.2 maximum_bitcast_fusion
  86.5 2.1 %copy.7 = bf16[6,8,4,2,24,128]{5,4,3,2,1,0:T(8,128)(2,1)} copy(bf16[6,8,4,2,24,128]{5,4,0,1,2,3:T(8,128)(2,1)S(1)} %maximum_bitcast_fusion) | data formatting | bytes 4718592 | tf_op jit(solution)/shard_map/cond/branch_1_fun/transpose | solution.py:196
  88.6 7.7 %branch_1_fun.1 = (bf16[1536,1536]{1,0:T(8,128)(2,1)}, bf16[1536,384]{1,0:T(8,128)(2,1)S(1)}, bf16[256,3840]{1,0:T(8,128)(2,1)S(1)}) custom-call(s32[1]{0:T(128)} %get-tuple-element.31.first_ref, s32[6,128]{1,0:T(8,128)S(1)} %get-tuple-element.24.rows_ref, bf16[6,1536,128]{2,1,0:T(8,128)(2,1)} %bitcast.329, bf16[1536,384]{1,0:T(8,128)(2,1)} %get-tuple-element.33.matrix_ref), custom_call_target="tpu_custom_call" | custom-call | flops 301989888 | bytes 12582912 | tf_op jit(solution)/shard_map/cond/branch_1_fun/pallas_call | solution.py:197
  96.3 6.9 %all-to-all-done.3 = bf16[32,64,128]{2,1,0:T(8,128)(2,1)} async-done(((bf16[32,64,128]{2,1,0:T(8,128)(2,1)}), bf16[32,64,128]{2,1,0:T(8,128)(2,1)}, u32[]{:S(2)}, u32[]{:S(2)}) %all-to-all-start.3) | async-done | bytes 524320 | tf_op jit(solution)/shard_map/cond/branch_1_fun/all_to_all | solution.py:146
  103.2 2.0 %collective-permute-start.1 = (bf16[32,64,128]{2,1,0:T(8,128)(2,1)}, bf16[32,64,128]{2,1,0:T(8,128)(2,1)}, u32[]{:S(2)}, u32[]{:S(2)}) collective-permute-start(bf16[32,64,128]{2,1,0:T(8,128)(2,1)} %all-to-all-done.3), channel_id=1, source_target_pairs={{0,1},{1,0},{2,3},{3,2},{4,5},{5,4},{6,7},{7,6},{8,9},{9,8},{10,11... | collective-permute-start | bytes 1572872 | tf_op jit(solution)/shard_map/cond/branch_1_fun/ppermute | solution.py:209
  105.2 2.1 %collective-permute-done.1 = bf16[32,64,128]{2,1,0:T(8,128)(2,1)} collective-permute-done((bf16[32,64,128]{2,1,0:T(8,128)(2,1)}, bf16[32,64,128]{2,1,0:T(8,128)(2,1)}, u32[]{:S(2)}, u32[]{:S(2)}) %collective-permute-start.1) | collective-permute-done | bytes 524320 | tf_op jit(solution)/shard_map/cond/branch_1_fun/ppermute | solution.py:209
  107.3 9.0 %shard_map.47 = bf16[1536,384]{1,0:T(8,128)(2,1)} custom-call(s32[1]{0:T(128)} %bitcast.28.core_ref, bf16[2,768,384]{2,1,0:T(8,128)(2,1)} %all-reduce.2.cloned.1.call-done.content, bf16[32,64,128]{2,1,0:T(8,128)(2,1)} %get-tuple-element.50.mine_ref, bf16[32,64,128]{2,1,0:T(8,128)(2,1)} %get-tuple-element.51.other_ref, f32[6,128,128]{2,1,0:T(8,128)} %inverses_ref.1, ...), custom_call_target="tpu_custom_call" | custom-call | flops 1811939328 | bytes 16777216 | tf_op jit(solution)/shard_map/pallas_call | solution.py:217
  (49 shorter events, 1.6 us)
Async XLA Ops:
  6.5 100.8 %all-reduce.2.cloned.1.call-start = ((), (), s32[]{:S(2)}) async-start(), calls=%async_computation.4 | async-start | bytes 2359296 | tf_op jit(solution)/shard_map/psum | solution.py:168
  10.7 0.7 copy-start.2
  10.7 1.9 %copy-start.1 = (bf16[6,24,128]{2,1,0:T(8,128)(2,1)S(1)}, bf16[6,24,128]{2,1,0:T(8,128)(2,1)}, u32[]{:S(2)}) copy-start(bf16[6,24,128]{2,1,0:T(8,128)(2,1)} %param.7) | copy-start | bytes 110596
  13.4 22.9 %all-to-all-start = ((bf16[8,144,128]{2,1,0:T(8,128)(2,1)}), bf16[8,144,128]{2,1,0:T(8,128)(2,1)S(1)}, u32[]{:S(2)}, u32[]{:S(2)}) async-start(bf16[8,144,128]{2,1,0:T(8,128)(2,1)} %broadcast_in_dim.72), calls=%async_computation | async-start | bytes 589824 | tf_op jit(solution)/shard_map/cond/branch_1_fun/all_to_all | solution.py:146
  37.5 17.5 %all-to-all-start.1 = ((bf16[4,8,144,128]{3,2,1,0:T(8,128)(2,1)}), bf16[4,8,144,128]{3,2,1,0:T(8,128)(2,1)S(1)}, u32[]{:S(2)}, u32[]{:S(2)}) async-start(bf16[4,8,144,128]{3,2,1,0:T(8,128)(2,1)} %broadcast_in_dim.73), calls=%async_computation.1 | async-start | bytes 2359296 | tf_op jit(solution)/shard_map/cond/branch_1_fun/all_to_all | solution.py:146
  55.0 21.6 %collective-permute-start = (bf16[4,8,144,128]{3,2,1,0:T(8,128)(2,1)S(1)}, bf16[4,8,144,128]{3,2,1,0:T(8,128)(2,1)S(1)}, u32[]{:S(2)}, u32[]{:S(2)}) collective-permute-start(bf16[4,8,144,128]{3,2,1,0:T(8,128)(2,1)S(1)} %all-to-all-done.1), channel_id=1, source_target_pairs={{0,1},{1,0},{2,3},{3,2},{4,5},{5,4},{6,7},{7,6},{8,9},{9,8},{10,11... | collective-permute-start | bytes 3538952 | tf_op jit(solution)/shard_map/cond/branch_1_fun/ppermute | solution.py:190
  76.6 8.2 %copy-start = (bf16[4,8,144,128]{3,2,1,0:T(8,128)(2,1)}, bf16[4,8,144,128]{3,2,1,0:T(8,128)(2,1)S(1)}, u32[]{:S(2)}) copy-start(bf16[4,8,144,128]{3,2,1,0:T(8,128)(2,1)S(1)} %collective-permute-done) | copy-start | bytes 3538948 | tf_op jit(solution)/shard_map/cond
  77.7 25.5 %all-to-all-start.3 = ((bf16[32,64,128]{2,1,0:T(8,128)(2,1)}), bf16[32,64,128]{2,1,0:T(8,128)(2,1)}, u32[]{:S(2)}, u32[]{:S(2)}) async-start(bf16[32,64,128]{2,1,0:T(8,128)(2,1)} %broadcast_in_dim.77), calls=%async_computation.3 | async-start | bytes 1048576 | tf_op jit(solution)/shard_map/cond/branch_1_fun/all_to_all | solution.py:146
  103.2 4.1 %collective-permute-start.1 = (bf16[32,64,128]{2,1,0:T(8,128)(2,1)}, bf16[32,64,128]{2,1,0:T(8,128)(2,1)}, u32[]{:S(2)}, u32[]{:S(2)}) collective-permute-start(bf16[32,64,128]{2,1,0:T(8,128)(2,1)} %all-to-all-done.3), channel_id=1, source_target_pairs={{0,1},{1,0},{2,3},{3,2},{4,5},{5,4},{6,7},{7,6},{8,9},{9,8},{10,11... | collective-permute-start | bytes 1572872 | tf_op jit(solution)/shard_map/cond/branch_1_fun/ppermute | solution.py:209
Sparse Core Ops, SparseCore 0:
  10.9 87.5 all-reduce.1

commit v5 on v4

--- a/solution.py
+++ b/solution.py
@@ -13,6 +13,7 @@
 TOP = NB * STEPS
 PAIRS = [(k, j) for k in range(1, STEPS) for j in range(k)]
 CHUNK = 64
+BLOCKS = 3
 BF = jnp.bfloat16
 F32 = jnp.float32
 VM = pl.BlockSpec(memory_space=pltpu.VMEM)
@@ -49,26 +50,34 @@
 def share_kernel(first_ref, rows_ref, matrix_ref, share_ref, hot):
     first = first_ref[0]
     local, width = matrix_ref.shape
+    fresh = []
     for k in range(STEPS):
-        ids, _, fresh = masks(k, rows_ref)
+        ids, _, new = masks(k, rows_ref)
+        fresh.append(new)
         at = k * NB
         where = ids[NB:] - first
         for c in range(0, local, NB):
-            hot[:, c:c + NB] = jnp.where(iota((NB, NB), 1) + c == where, 1.0, 0.0).astype(BF)
-        row = jnp.dot(hot[...], matrix_ref[...], preferred_element_type=F32)
-        mine = fresh[:NB] & (first == 0)
-        for c in range(0, width, NB):
+            hot[at:at + NB, c:c + NB] = jnp.where(iota((NB, NB), 1) + c == where, 1.0, 0.0).astype(BF)
+    for c in range(0, width, NB):
+        row = jnp.dot(hot[...], matrix_ref[:, c:c + NB], preferred_element_type=F32)
+        for k in range(STEPS):
+            at = k * NB
             top = matrix_ref[at:at + NB, c:c + NB].astype(F32)
-            share_ref[0, at:at + NB, c:c + NB] = jnp.where(mine, top, 0.0).astype(BF)
-            share_ref[1, at:at + NB, c:c + NB] = jnp.where(fresh[NB:], row[:, c:c + NB], 0.0).astype(BF)
-
-
-def rows_kernel(first_ref, rows_ref, panels_ref, matrix_ref, factor_ref, kept_ref, select_ref):
+            share_ref[0, at:at + NB, c:c + NB] = jnp.where(fresh[k][:NB] & (first == 0), top, 0.0).astype(BF)
+            share_ref[1, at:at + NB, c:c + NB] = jnp.where(fresh[k][NB:], row[at:at + NB], 0.0).astype(BF)
+
+
+def rows_kernel(first_ref, rows_ref, panels_ref, matrix_ref, inverses_ref, factor_ref, kept_ref, select_ref, parts_ref):
     for k in range(1, STEPS):
         for j, same, live in masks(k, rows_ref)[1]:
             at = start_of(k) + 2 * NB * j
             select_ref[:, at:at + NB] = same.astype(BF)
             select_ref[:, at + NB:at + 2 * NB] = (-live).astype(BF)
+    for k in range(STEPS):
+        rest = inverses_ref[k]
+        for i in range(3):
+            parts_ref[k, i * NB:(i + 1) * NB, :] = rest.astype(BF)
+            rest = rest - rest.astype(BF).astype(F32)
     ones = jnp.ones((NB, NB), BF)
     height = 2 * NB
 
@@ -95,47 +104,58 @@
     lax.fori_loop(0, matrix_ref.shape[0] // height, one, 0)
 
 
-def solve_kernel(core_ref, content, mine_ref, other_ref, inverses_ref, select_ref, factor_hbm, kept_hbm, out_ref,
-                 low, coef, state, factor, kept, sems):
-    loads = [pltpu.make_async_copy(factor_hbm, factor, sems.at[0]), pltpu.make_async_copy(kept_hbm, kept, sems.at[1])]
-    for load in loads:
-        load.start()
-    half = low.shape[1]
+def solve_kernel(core_ref, content_hbm, mine_hbm, other_hbm, parts_hbm, select_hbm, factor_hbm, kept_hbm, out_hbm,
+                 content, low, parts, coef, factor, kept, state, out, sems, out_sems):
     core = core_ref[0]
-    low[core] = mine_ref[...].reshape(half, NB)
-    low[1 - core] = other_ref[...].reshape(half, NB)
+    height = out.shape[0] // BLOCKS
+    copies = [
+        pltpu.make_async_copy(src, dst, sems.at[i])
+        for i, (src, dst) in enumerate((
+            (content_hbm, content),
+            (parts_hbm, parts),
+            (mine_hbm, low.at[core]),
+            (other_hbm, low.at[1 - core]),
+            (select_hbm, coef),
+            (factor_hbm, factor),
+            (kept_hbm, kept),
+        ))
+    ]
+    for copy in copies:
+        copy.start()
+    for copy in copies[:2]:
+        copy.wait()
+    each = CHUNK
     for k in range(STEPS):
         x = content[:, k * NB:(k + 1) * NB, :].reshape(2 * NB, -1).astype(F32)
+        if k == 1:
+            for copy in copies[2:5]:
+                copy.wait()
         if k:
             for j in range(k):
-                at = start_of(k) + 2 * NB * j
-                t = 2 * PAIRS.index((k, j))
-                b0, b1 = t * NB, (t + 1) * NB
-                block = jnp.concatenate([low[b1 // half, b1 % half:b1 % half + NB, :], low[b0 // half, b0 % half:b0 % half + NB, :]])
-                coef[:, 2 * NB * j:2 * NB * j + NB] = select_ref[:, at:at + NB]
-                coef[:, 2 * NB * j + NB:2 * NB * (j + 1)] = select_ref[:, at + NB:at + 2 * NB] * block
-            x = x + jnp.dot(coef[:, :2 * NB * k], state[:2 * NB * k, :], preferred_element_type=F32)
+                at = start_of(k) + 2 * NB * j + NB
+                for side in range(2):
+                    for r in range(0, NB, each):
+                        row = (2 * PAIRS.index((k, j)) + 1 - side) * NB + r
+                        held, inside = divmod(row // each, low.shape[1])
+                        here = side * NB + r
+                        coef[here:here + each, at:at + NB] = coef[here:here + each, at:at + NB] * low[held, inside]
+            at = start_of(k)
+            x = x + jnp.dot(coef[:, at:at + 2 * NB * k], state[:2 * NB * k, :], preferred_element_type=F32)
         y = x.astype(BF)
         state[2 * NB * k:2 * NB * k + NB, :] = y[:NB]
-        inv = inverses_ref[k]
-        hi = inv.astype(BF)
-        rest = inv - hi.astype(F32)
-        mid = rest.astype(BF)
-        lo = (rest - mid.astype(F32)).astype(BF)
-        v = y[NB:]
-        upper = jnp.dot(hi, v, preferred_element_type=F32) + (
-            jnp.dot(mid, v, preferred_element_type=F32) + jnp.dot(lo, v, preferred_element_type=F32))
-        state[2 * NB * k + NB:2 * NB * (k + 1), :] = upper.astype(BF)
-    for load in loads:
-        load.wait()
-
-    def one(step, carry):
-        at = pl.multiple_of(step * 2 * NB, 2 * NB)
-        new = jnp.dot(factor[pl.ds(at, 2 * NB), :], state[...], preferred_element_type=F32)
-        out_ref[pl.ds(at, 2 * NB), :] = (kept[pl.ds(at, 2 * NB), :].astype(F32) + new).astype(BF)
-        return carry
-
-    lax.fori_loop(0, out_ref.shape[0] // (2 * NB), one, 0)
+        u = jnp.dot(parts[k], y[NB:], preferred_element_type=F32)
+        state[2 * NB * k + NB:2 * NB * (k + 1), :] = (u[:NB] + (u[NB:2 * NB] + u[2 * NB:])).astype(BF)
+    for copy in copies[5:]:
+        copy.wait()
+    writes = []
+    for b in range(BLOCKS):
+        at = b * height
+        new = jnp.dot(factor[at:at + height, :], state[...], preferred_element_type=F32)
+        out[at:at + height, :] = (kept[at:at + height, :].astype(F32) + new).astype(BF)
+        writes.append(pltpu.make_async_copy(out.at[at:at + height], out_hbm.at[at:at + height], out_sems.at[b]))
+        writes[-1].start()
+    for write in writes:
+        write.wait()
 
 
 def cost(flops, nbytes):
@@ -162,7 +182,7 @@
         out_shape=jax.ShapeDtypeStruct((2, TOP, width), BF),
         in_specs=[SM, VM, VM],
         out_specs=VM,
-        scratch_shapes=[pltpu.VMEM((NB, local), BF)],
+        scratch_shapes=[pltpu.VMEM((TOP, local), BF)],
         cost_estimate=cost(2 * TOP * local * width, 4 << 20),
     )(first1, pivots, matrix)
     content = lax.psum(share, "y")
@@ -187,49 +207,54 @@
         part = jnp.broadcast_to(part, (ny, nc, chunk, NB)).reshape(ny * nc, chunk, NB)
         part = lax.all_to_all(part, ("y", "c"), 0, 0, tiled=True).astype(F32).sum(0).astype(BF)
 
+        part, mine = lax.optimization_barrier((part, mine))
         other = lax.ppermute(mine, "c", swap)
-        part, other = lax.optimization_barrier((part, other))
         low_mine = spread(part, ("z", "x"), nzx)
 
         both = [a.reshape(nx, nz, STEPS, held, NB) for a in (mine, other)]
         both = jnp.stack([jnp.where(core == 0, both[0], both[1]), jnp.where(core == 0, both[1], both[0])])
         full = both.transpose(3, 2, 1, 0, 4, 5).reshape(STEPS, local, NB)
-        factor, kept, select = pl.pallas_call(
+        factor, kept, select, parts = pl.pallas_call(
             rows_kernel,
             out_shape=(
                 jax.ShapeDtypeStruct((local, 2 * TOP), BF),
                 jax.ShapeDtypeStruct((local, width), BF),
                 jax.ShapeDtypeStruct((2 * NB, start_of(STEPS)), BF),
+                jax.ShapeDtypeStruct((STEPS, 3 * NB, NB), BF),
             ),
-            in_specs=[SM, VM, VM, VM],
-            out_specs=(VM, VM, VM),
+            in_specs=[SM, VM, VM, VM, VM],
+            out_specs=(VM, VM, VM, VM),
             cost_estimate=cost(2 * TOP * local * NB, 12 << 20),
-        )(first1, pivots, full, matrix)
-        low_mine, factor, kept, select = lax.optimization_barrier((low_mine, factor, kept, select))
-        return low_mine, lax.ppermute(low_mine, "c", swap), factor, kept, select
+        )(first1, pivots, full, matrix, inverses)
+        low_mine, factor, kept, select, parts = lax.optimization_barrier((low_mine, factor, kept, select, parts))
+        return low_mine, lax.ppermute(low_mine, "c", swap), factor, kept, select, parts
 
     def nothing(panels, pivots):
         return tuple(jnp.zeros(o.shape, o.dtype) for o in jax.eval_shape(gather, panels, pivots))
 
-    low_mine, low_other, factor, kept, select = lax.cond(pivots[0, 0] > 0, gather, nothing, panels, pivots)
+    low_mine, low_other, factor, kept, select, parts = lax.cond(y < ny, gather, nothing, panels, pivots)
 
     chunk = low_mine.size // (nzx * NB)
+    low_shape = (nzx * chunk // CHUNK, CHUNK, NB)
     return pl.pallas_call(
         solve_kernel,
         out_shape=jax.ShapeDtypeStruct((local, width), BF),
-        in_specs=[SM, VM, VM, VM, VM, VM, ANY, ANY],
-        out_specs=VM,
+        in_specs=[SM] + [ANY] * 7,
+        out_specs=ANY,
         scratch_shapes=[
-            pltpu.VMEM((2, nzx * chunk, NB), BF),
-            pltpu.VMEM((2 * NB, 2 * NB * (STEPS - 1)), BF),
+            pltpu.VMEM((2, TOP, width), BF),
+            pltpu.VMEM((2,) + low_shape, BF),
+            pltpu.VMEM(parts.shape, BF),
+            pltpu.VMEM(select.shape, BF),
+            pltpu.VMEM(factor.shape, BF),
+            pltpu.VMEM((local, width), BF),
             pltpu.VMEM((2 * TOP, width), BF),
-            pltpu.VMEM((local, 2 * TOP), BF),
             pltpu.VMEM((local, width), BF),
-            pltpu.SemaphoreType.DMA((2,)),
+            pltpu.SemaphoreType.DMA((7,)),
+            pltpu.SemaphoreType.DMA((BLOCKS,)),
         ],
         cost_estimate=cost(4 * TOP * local * width, 16 << 20),
-    )(core1, content, low_mine.reshape(nzx, chunk, NB), low_other.reshape(nzx, chunk, NB),
-      inverses, select, factor, kept)
+    )(core1, content, low_mine.reshape(low_shape), low_other.reshape(low_shape), parts, select, factor, kept)
 
 
 def solution(mesh):

time: 125 us -> 123 us (0.984)
  waiting for transfers between devices: 33.1 us -> 31.7 us
    pallas_call x1, Pallas kernels: 9.04 us -> 7.53 us  [per_device(): pl.pallas_call(solve_kernel, out_shape=jax.ShapeDtypeStruct((local, width...]
    all_to_all x3, waiting for transfers between devices: 31 us -> 29.7 us  [spread(): lax.all_to_all(jnp.broadcast_to(x[None], (parts,) + x.shape), axes, 0, 0,...]
where the time goes in v5:
time: 123 us; the launch traced here: 121 us
  waiting for transfers between devices  31.7 us (26%)
  starting transfers between devices  26.2 us (21%)
  Pallas kernels  20.1 us (16%)
  blocking collectives  18.2 us (15%)
  between operations  13.4 us (11%)
  local copies, waits for them, and re-layouts  7.67 us (6%)
  other arithmetic  3.07 us (2%)
    all_to_all x3, waiting for transfers between devices, spread(): lax.all_to_all(jnp.broadcast_to(x[None], (parts,) + x.shape), axes, 0, 0,...  29.7 us
    all_to_all x3, starting transfers between devices, spread(): lax.all_to_all(jnp.broadcast_to(x[None], (parts,) + x.shape), axes, 0, 0,...  21.2 us
    all_to_all x1, blocking collectives, gather(): lax.all_to_all(part, ('y', 'c'), 0, 0, tiled=True).astype(F32).sum(0)  18.2 us
    pallas_call x1, Pallas kernels, gather(): pl.pallas_call(rows_kernel, out_shape=(jax.ShapeDtypeStruct((local, 2 * T...  7.78 us
    pallas_call x1, Pallas kernels, per_device(): pl.pallas_call(solve_kernel, out_shape=jax.ShapeDtypeStruct((local, width...  7.53 us
    pallas_call x1, Pallas kernels, per_device(): pl.pallas_call(share_kernel, out_shape=jax.ShapeDtypeStruct((2, TOP, widt...  4.84 us
    broadcast_in_dim x3, local copies, waits for them, and re-layouts, spread(): jnp.broadcast_to(x[None], (parts,) + x.shape)  3.68 us
    ppermute x1, starting transfers between devices, gather(): other = lax.ppermute(mine, 'c', swap)  2.86 us
  transfers between devices with their start and end apart: 6, of which 4 were waited for; matrix products, arithmetic and copies ran while one was open for 8% of the time, Pallas kernels for 6%

profile of v5, /device:TPU:6, one launch (start us, length us, event | category | flops | bytes accessed | tf_op | source)
XLA Modules:
  0.0 120.5 jit_solution(3439519175094576329)
XLA Ops:
  6.5 4.8 %shard_map.47 = bf16[2,768,384]{2,1,0:T(8,128)(2,1)} custom-call(s32[1]{0:T(128)} %bitcast.29.first_ref, s32[6,128]{1,0:T(8,128)} %rows_ref.1, bf16[1536,384]{1,0:T(8,128)(2,1)} %matrix_ref.1), custom_call_target="tpu_custom_call" | custom-call | flops 905969664 | bytes 4194304 | tf_op jit(solution)/shard_map/pallas_call | solution.py:180
  11.4 1.0 copy-done
  12.4 93.8 %conditional.1 = (bf16[32,64,128]{2,1,0:T(8,128)(2,1)}, bf16[32,64,128]{2,1,0:T(8,128)(2,1)}, bf16[1536,1536]{1,0:T(8,128)(2,1)}, bf16[1536,384]{1,0:T(8,128)(2,...) conditional(s32[]{:T(128)} %convert_element_type.2, () %tuple.17, (s32[6,128]{1,0:T(8,128)S(1)}, ...), branch_computations={%region_1.0_spmd, %region_2.4_spmd} | conditional | flops 304739584 | bytes 43197440 | solution.py:235
  12.4 1.5 %broadcast_in_dim.72 = bf16[8,144,128]{2,1,0:T(8,128)(2,1)} broadcast(bf16[144,128]{1,0:T(8,128)(2,1)} %bitcast.334), dimensions={1,2} | broadcast | bytes 331776 | tf_op jit(solution)/shard_map/cond/branch_1_fun/broadcast_in_dim | solution.py:166
  13.9 10.3 %all-to-all-start = ((bf16[8,144,128]{2,1,0:T(8,128)(2,1)}), bf16[8,144,128]{2,1,0:T(8,128)(2,1)S(1)}, u32[]{:S(2)}, u32[]{:S(2)}) async-start(bf16[8,144,128]{2,1,0:T(8,128)(2,1)} %broadcast_in_dim.72), calls=%async_computation | async-start | bytes 589824 | tf_op jit(solution)/shard_map/cond/branch_1_fun/all_to_all | solution.py:166
  25.4 11.4 %all-to-all-done = bf16[8,144,128]{2,1,0:T(8,128)(2,1)S(1)} async-done(((bf16[8,144,128]{2,1,0:T(8,128)(2,1)}), bf16[8,144,128]{2,1,0:T(8,128)(2,1)S(1)}, u32[]{:S(2)}, u32[]{:S(2)}) %all-to-all-start) | async-done | bytes 294944 | tf_op jit(solution)/shard_map/cond/branch_1_fun/all_to_all | solution.py:166
  36.8 1.2 broadcast_in_dim.73
  38.0 4.8 %all-to-all-start.1 = ((bf16[4,8,144,128]{3,2,1,0:T(8,128)(2,1)}), bf16[4,8,144,128]{3,2,1,0:T(8,128)(2,1)S(1)}, u32[]{:S(2)}, u32[]{:S(2)}) async-start(bf16[4,8,144,128]{3,2,1,0:T(8,128)(2,1)} %broadcast_in_dim.73), calls=%async_computation.1 | async-start | bytes 2359296 | tf_op jit(solution)/shard_map/cond/branch_1_fun/all_to_all | solution.py:166
  43.0 0.1 reshape.187
  43.1 12.4 %all-to-all-done.1 = bf16[4,8,144,128]{3,2,1,0:T(8,128)(2,1)S(1)} async-done(((bf16[4,8,144,128]{3,2,1,0:T(8,128)(2,1)}), bf16[4,8,144,128]{3,2,1,0:T(8,128)(2,1)S(1)}, u32[]{:S(2)}, u32[]{:S(2)}) %all-to-all-start.1) | async-done | bytes 1179680 | tf_op jit(solution)/shard_map/cond/branch_1_fun/all_to_all | solution.py:166
  55.5 0.7 gather_fusion
  56.2 0.1 select_select_fusion
  56.4 18.2 %all_to_all.16 = bf16[16,64,128]{2,1,0:T(8,128)(2,1)S(1)} all-to-all(bf16[16,64,128]{2,1,0:T(8,128)(2,1)S(1)} %bitcast.332), channel_id=1, replica_groups=mesh['y'=8,'z'=8,'x'=4,'c'=2] {'y','c'}, dimensions={0} | all-to-all | bytes 524288 | tf_op jit(solution)/shard_map/cond/branch_1_fun/all_to_all | solution.py:208
  74.6 2.9 %collective-permute-start = (bf16[4,8,144,128]{3,2,1,0:T(8,128)(2,1)S(1)}, bf16[4,8,144,128]{3,2,1,0:T(8,128)(2,1)}, u32[]{:S(2)}, u32[]{:S(2)}) collective-permute-start(bf16[4,8,144,128]{3,2,1,0:T(8,128)(2,1)S(1)} %all-to-all-done.1), channel_id=1, source_target_pairs={{0,1},{1,0},{2,3},{3,2},{4,5},{5,4},{6,7},{7,6},{8,9},{9,8},{10,11... | collective-permute-start | bytes 3538952 | tf_op jit(solution)/shard_map/cond/branch_1_fun/ppermute | solution.py:211
  77.5 1.0 broadcast_in_dim.77
  78.4 6.2 %all-to-all-start.3 = ((bf16[32,64,128]{2,1,0:T(8,128)(2,1)}), bf16[32,64,128]{2,1,0:T(8,128)(2,1)}, u32[]{:S(2)}, u32[]{:S(2)}) async-start(bf16[32,64,128]{2,1,0:T(8,128)(2,1)} %broadcast_in_dim.77), calls=%async_computation.3 | async-start | bytes 1048576 | tf_op jit(solution)/shard_map/cond/branch_1_fun/all_to_all | solution.py:166
  84.6 1.4 %broadcast_select_fusion.1 = (bf16[4,8,144,128]{3,2,1,0:T(8,128)(2,1)S(1)}, bf16[4,8,144,128]{3,2,1,0:T(8,128)(2,1)S(1)}) fusion(bf16[4,8,144,128]{3,2,1,0:T(8,128)(2,1)S(1)} %all-to-all-done.1, bf16[4,8,144,128]{3,2,1,0:T(8,128)(2,1)} %collective-permute-done, pred[]{:T(512)S(6)} %eq.176), kind=kLoop, calls=%fused_computation.3 | loop fusion | flops 1179648 | bytes 4718593 | tf_op jit(solution)/shard_map/cond/branch_1_fun/jit(_where)/select_n | solution.py:215
  86.0 0.2 maximum_bitcast_fusion
  86.3 2.1 %copy.8 = bf16[6,8,4,2,24,128]{5,4,3,2,1,0:T(8,128)(2,1)} copy(bf16[6,8,4,2,24,128]{5,4,0,1,2,3:T(8,128)(2,1)S(1)} %maximum_bitcast_fusion) | data formatting | bytes 4718592 | tf_op jit(solution)/shard_map/cond/branch_1_fun/transpose | solution.py:216
  88.4 7.8 %branch_1_fun.1 = (bf16[1536,1536]{1,0:T(8,128)(2,1)}, bf16[1536,384]{1,0:T(8,128)(2,1)S(1)}, bf16[256,3840]{1,0:T(8,128)(2,1)S(1)}, bf16[6,384,128]{2,1,0:T(8,128)(2,1)}) custom-call(s32[1]{0:T(128)} %get-tuple-element.33.first_ref, s32[6,128]{1,0:T(8,128)S(1)} %get-tuple-element.26.rows_ref, bf16[6,1536,128]{2,1,0:T(8,128)(2,1)} %bitcast.328, ...), custom_call_target="tpu_custom_call" | custom-call | flops 301989888 | bytes 12582912 | tf_op jit(solution)/shard_map/cond/branch_1_fun/pallas_call | solution.py:217
  96.2 5.9 %all-to-all-done.3 = bf16[32,64,128]{2,1,0:T(8,128)(2,1)} async-done(((bf16[32,64,128]{2,1,0:T(8,128)(2,1)}), bf16[32,64,128]{2,1,0:T(8,128)(2,1)}, u32[]{:S(2)}, u32[]{:S(2)}) %all-to-all-start.3) | async-done | bytes 524320 | tf_op jit(solution)/shard_map/cond/branch_1_fun/all_to_all | solution.py:166
  102.0 2.1 %collective-permute-start.1 = (bf16[32,64,128]{2,1,0:T(8,128)(2,1)}, bf16[32,64,128]{2,1,0:T(8,128)(2,1)}, u32[]{:S(2)}, u32[]{:S(2)}) collective-permute-start(bf16[32,64,128]{2,1,0:T(8,128)(2,1)} %all-to-all-done.3), channel_id=1, source_target_pairs={{0,1},{1,0},{2,3},{3,2},{4,5},{5,4},{6,7},{7,6},{8,9},{9,8},{10,11... | collective-permute-start | bytes 1572872 | tf_op jit(solution)/shard_map/cond/branch_1_fun/ppermute | solution.py:230
  104.1 2.0 %collective-permute-done.1 = bf16[32,64,128]{2,1,0:T(8,128)(2,1)} collective-permute-done((bf16[32,64,128]{2,1,0:T(8,128)(2,1)}, bf16[32,64,128]{2,1,0:T(8,128)(2,1)}, u32[]{:S(2)}, u32[]{:S(2)}) %collective-permute-start.1) | collective-permute-done | bytes 524320 | tf_op jit(solution)/shard_map/cond/branch_1_fun/ppermute | solution.py:230
  106.2 7.5 %shard_map.48 = bf16[1536,384]{1,0:T(8,128)(2,1)} custom-call(s32[1]{0:T(128)} %bitcast.28.core_ref, bf16[2,768,384]{2,1,0:T(8,128)(2,1)} %all-reduce.2.cloned.1.call-done.content_hbm, bf16[32,64,128]{2,1,0:T(8,128)(2,1)} %get-tuple-element.56.mine_hbm, bf16[32,64,128]{2,1,0:T(8,128)(2,1)} %get-tuple-element.57.other_hbm, ...), custom_call_target="tpu_custom_call" | custom-call | flops 1811939328 | bytes 16777216 | tf_op jit(solution)/shard_map/pallas_call | solution.py:239
  (46 shorter events, 1.5 us)
Async XLA Ops:
  6.5 99.6 %all-reduce.2.cloned.1.call-start = ((), (), s32[]{:S(2)}) async-start(), calls=%async_computation.4 | async-start | bytes 2359296 | tf_op jit(solution)/shard_map/psum | solution.py:188
  11.4 1.0 copy-start
  11.4 1.0 copy-start.1
  13.9 22.9 %all-to-all-start = ((bf16[8,144,128]{2,1,0:T(8,128)(2,1)}), bf16[8,144,128]{2,1,0:T(8,128)(2,1)S(1)}, u32[]{:S(2)}, u32[]{:S(2)}) async-start(bf16[8,144,128]{2,1,0:T(8,128)(2,1)} %broadcast_in_dim.72), calls=%async_computation | async-start | bytes 589824 | tf_op jit(solution)/shard_map/cond/branch_1_fun/all_to_all | solution.py:166
  38.0 17.5 %all-to-all-start.1 = ((bf16[4,8,144,128]{3,2,1,0:T(8,128)(2,1)}), bf16[4,8,144,128]{3,2,1,0:T(8,128)(2,1)S(1)}, u32[]{:S(2)}, u32[]{:S(2)}) async-start(bf16[4,8,144,128]{3,2,1,0:T(8,128)(2,1)} %broadcast_in_dim.73), calls=%async_computation.1 | async-start | bytes 2359296 | tf_op jit(solution)/shard_map/cond/branch_1_fun/all_to_all | solution.py:166
  74.6 10.0 %collective-permute-start = (bf16[4,8,144,128]{3,2,1,0:T(8,128)(2,1)S(1)}, bf16[4,8,144,128]{3,2,1,0:T(8,128)(2,1)}, u32[]{:S(2)}, u32[]{:S(2)}) collective-permute-start(bf16[4,8,144,128]{3,2,1,0:T(8,128)(2,1)S(1)} %all-to-all-done.1), channel_id=1, source_target_pairs={{0,1},{1,0},{2,3},{3,2},{4,5},{5,4},{6,7},{7,6},{8,9},{9,8},{10,11... | collective-permute-start | bytes 3538952 | tf_op jit(solution)/shard_map/cond/branch_1_fun/ppermute | solution.py:211
  78.4 23.6 %all-to-all-start.3 = ((bf16[32,64,128]{2,1,0:T(8,128)(2,1)}), bf16[32,64,128]{2,1,0:T(8,128)(2,1)}, u32[]{:S(2)}, u32[]{:S(2)}) async-start(bf16[32,64,128]{2,1,0:T(8,128)(2,1)} %broadcast_in_dim.77), calls=%async_computation.3 | async-start | bytes 1048576 | tf_op jit(solution)/shard_map/cond/branch_1_fun/all_to_all | solution.py:166
  102.0 4.1 %collective-permute-start.1 = (bf16[32,64,128]{2,1,0:T(8,128)(2,1)}, bf16[32,64,128]{2,1,0:T(8,128)(2,1)}, u32[]{:S(2)}, u32[]{:S(2)}) collective-permute-start(bf16[32,64,128]{2,1,0:T(8,128)(2,1)} %all-to-all-done.3), channel_id=1, source_target_pairs={{0,1},{1,0},{2,3},{3,2},{4,5},{5,4},{6,7},{7,6},{8,9},{9,8},{10,11... | collective-permute-start | bytes 1572872 | tf_op jit(solution)/shard_map/cond/branch_1_fun/ppermute | solution.py:230
Sparse Core Ops, SparseCore 0:
  11.5 86.3 all-reduce.1

commit v6 on v5

--- a/solution.py
+++ b/solution.py
@@ -47,9 +47,11 @@
     return ids, out, found < 0.5
 
 
-def share_kernel(first_ref, rows_ref, matrix_ref, share_ref, hot):
+def share_kernel(first_ref, rows_ref, matrix_hbm, share_hbm, matrix, hot, share, sems):
+    load = pltpu.make_async_copy(matrix_hbm, matrix, sems.at[0])
+    load.start()
     first = first_ref[0]
-    local, width = matrix_ref.shape
+    local, width = matrix.shape
     fresh = []
     for k in range(STEPS):
         ids, _, new = masks(k, rows_ref)
@@ -58,26 +60,35 @@
         where = ids[NB:] - first
         for c in range(0, local, NB):
             hot[at:at + NB, c:c + NB] = jnp.where(iota((NB, NB), 1) + c == where, 1.0, 0.0).astype(BF)
-    for c in range(0, width, NB):
-        row = jnp.dot(hot[...], matrix_ref[:, c:c + NB], preferred_element_type=F32)
-        for k in range(STEPS):
-            at = k * NB
-            top = matrix_ref[at:at + NB, c:c + NB].astype(F32)
-            share_ref[0, at:at + NB, c:c + NB] = jnp.where(fresh[k][:NB] & (first == 0), top, 0.0).astype(BF)
-            share_ref[1, at:at + NB, c:c + NB] = jnp.where(fresh[k][NB:], row[at:at + NB], 0.0).astype(BF)
-
-
-def rows_kernel(first_ref, rows_ref, panels_ref, matrix_ref, inverses_ref, factor_ref, kept_ref, select_ref, parts_ref):
+    load.wait()
+    for k in range(STEPS):
+        at = k * NB
+        for c in range(0, width, NB):
+            top = matrix[at:at + NB, c:c + NB].astype(F32)
+            share[0, at:at + NB, c:c + NB] = jnp.where(fresh[k][:NB] & (first == 0), top, 0.0).astype(BF)
+    stores = [pltpu.make_async_copy(share.at[0], share_hbm.at[0], sems.at[0])]
+    stores[0].start()
+    for k in range(0, STEPS, 2):
+        at = k * NB
+        row = jnp.dot(hot[at:at + 2 * NB, :], matrix[...], preferred_element_type=F32)
+        for i in range(2):
+            for c in range(0, width, NB):
+                here = slice(at + i * NB, at + (i + 1) * NB)
+                new = jnp.where(fresh[k + i][NB:], row[i * NB:(i + 1) * NB, c:c + NB], 0.0)
+                share[1, here, c:c + NB] = new.astype(BF)
+        both = pl.ds(at, 2 * NB)
+        stores.append(pltpu.make_async_copy(share.at[1, both], share_hbm.at[1, both], sems.at[1 + k // 2]))
+        stores[-1].start()
+    for store in stores:
+        store.wait()
+
+
+def rows_kernel(first_ref, rows_ref, panels_ref, matrix_ref, factor_ref, kept_ref, select_ref):
     for k in range(1, STEPS):
         for j, same, live in masks(k, rows_ref)[1]:
             at = start_of(k) + 2 * NB * j
             select_ref[:, at:at + NB] = same.astype(BF)
             select_ref[:, at + NB:at + 2 * NB] = (-live).astype(BF)
-    for k in range(STEPS):
-        rest = inverses_ref[k]
-        for i in range(3):
-            parts_ref[k, i * NB:(i + 1) * NB, :] = rest.astype(BF)
-            rest = rest - rest.astype(BF).astype(F32)
     ones = jnp.ones((NB, NB), BF)
     height = 2 * NB
 
@@ -104,15 +115,15 @@
     lax.fori_loop(0, matrix_ref.shape[0] // height, one, 0)
 
 
-def solve_kernel(core_ref, content_hbm, mine_hbm, other_hbm, parts_hbm, select_hbm, factor_hbm, kept_hbm, out_hbm,
-                 content, low, parts, coef, factor, kept, state, out, sems, out_sems):
+def solve_kernel(core_ref, content_hbm, mine_hbm, other_hbm, inverses_hbm, select_hbm, factor_hbm, kept_hbm, out_hbm,
+                 content, low, inverses, parts, coef, factor, kept, state, out, sems, out_sems):
     core = core_ref[0]
     height = out.shape[0] // BLOCKS
     copies = [
         pltpu.make_async_copy(src, dst, sems.at[i])
         for i, (src, dst) in enumerate((
+            (inverses_hbm, inverses),
             (content_hbm, content),
-            (parts_hbm, parts),
             (mine_hbm, low.at[core]),
             (other_hbm, low.at[1 - core]),
             (select_hbm, coef),
@@ -122,8 +133,13 @@
     ]
     for copy in copies:
         copy.start()
-    for copy in copies[:2]:
-        copy.wait()
+    copies[0].wait()
+    for k in range(STEPS):
+        rest = inverses[k]
+        for i in range(3):
+            parts[k, i * NB:(i + 1) * NB, :] = rest.astype(BF)
+            rest = rest - rest.astype(BF).astype(F32)
+    copies[1].wait()
     each = CHUNK
     for k in range(STEPS):
         x = content[:, k * NB:(k + 1) * NB, :].reshape(2 * NB, -1).astype(F32)
@@ -171,42 +187,51 @@
     local, width = matrix.shape
     held = panels.shape[1]
     y, core = lax.axis_index("y"), lax.axis_index("c")
-    zx = lax.axis_index(("z", "x"))
+    z, x = lax.axis_index("z"), lax.axis_index("x")
     first = y * local
     swap = [(0, 1), (1, 0)]
     first1 = first.reshape(1).astype(jnp.int32)
     core1 = core.reshape(1).astype(jnp.int32)
 
+    column = jnp.broadcast_to(panels.reshape(1, STEPS * held, NB), (nz, STEPS * held, NB))
+
     share = pl.pallas_call(
         share_kernel,
         out_shape=jax.ShapeDtypeStruct((2, TOP, width), BF),
-        in_specs=[SM, VM, VM],
-        out_specs=VM,
-        scratch_shapes=[pltpu.VMEM((TOP, local), BF)],
+        in_specs=[SM, VM, ANY],
+        out_specs=ANY,
+        scratch_shapes=[
+            pltpu.VMEM((local, width), BF),
+            pltpu.VMEM((TOP, local), BF),
+            pltpu.VMEM((2, TOP, width), BF),
+            pltpu.SemaphoreType.DMA((4,)),
+        ],
         cost_estimate=cost(2 * TOP * local * width, 4 << 20),
     )(first1, pivots, matrix)
     content = lax.psum(share, "y")
-    panels, pivots, _ = lax.optimization_barrier((panels, pivots, share))
-
-    def gather(panels, pivots):
-        mine = spread(panels.reshape(STEPS * held, NB), "z", nz)
-        mine = spread(mine, "x", nx)
+    column, pivots, _ = lax.optimization_barrier((column, pivots, share))
+
+    def gather(column, pivots):
+        column = lax.all_to_all(column, "z", 0, 0, tiled=True)
 
         idx = []
         for k, j in PAIRS:
             for rows in (pivots[k], k * NB + jnp.arange(NB, dtype=jnp.int32)):
                 here = rows - first
                 pb = here // held
-                at = ((pb // nc % nx * nz + pb // nc // nx) * STEPS + j) * held + here % held
-                idx.append(jnp.where((here >= 0) & (here < local) & (pb % nc == core), at, -1))
+                at = (pb // (nx * nc) * STEPS + j) * held + here % held
+                owned = (here >= 0) & (here < local) & (pb % (nx * nc) == x * nc + core)
+                idx.append(jnp.where(owned, at, -1))
         chunk = -(-len(idx) * NB // (nzx * nc) // CHUNK) * CHUNK
         idx = jnp.concatenate(idx + [jnp.full((chunk * nzx * nc - len(idx) * NB,), -1, jnp.int32)])
-        idx = lax.dynamic_slice(idx.reshape(nc, nzx, chunk), (0, zx, 0), (nc, 1, chunk)).reshape(nc * chunk)
-        part = jnp.take(mine.reshape(-1, NB), jnp.maximum(idx, 0), axis=0)
-        part = jnp.where((idx >= 0)[:, None], part, jnp.zeros((), BF)).reshape(1, nc, chunk, NB)
-        part = jnp.broadcast_to(part, (ny, nc, chunk, NB)).reshape(ny * nc, chunk, NB)
-        part = lax.all_to_all(part, ("y", "c"), 0, 0, tiled=True).astype(F32).sum(0).astype(BF)
-
+        idx = lax.dynamic_slice(idx.reshape(nc, nz, nx * chunk), (0, z, 0), (nc, 1, nx * chunk)).reshape(nc * nx * chunk)
+        part = jnp.take(column.reshape(-1, NB), jnp.maximum(idx, 0), axis=0)
+        part = jnp.where((idx >= 0)[:, None], part, jnp.zeros((), BF)).reshape(nc * nx, chunk, NB)
+        part = lax.all_to_all(part, ("c", "x"), 0, 0, tiled=True).astype(F32).sum(0).astype(BF)
+        part = spread(part, "y", ny).reshape(ny, chunk, NB).astype(F32).sum(0).astype(BF)
+
+        blocks = [column] + [lax.ppermute(column, "x", [((i + s) % nx, i) for i in range(nx)]) for s in range(1, nx)]
+        mine = lax.dynamic_slice_in_dim(jnp.stack(blocks + blocks), (nx - x) % nx, nx)
         part, mine = lax.optimization_barrier((part, mine))
         other = lax.ppermute(mine, "c", swap)
         low_mine = spread(part, ("z", "x"), nzx)
@@ -214,25 +239,24 @@
         both = [a.reshape(nx, nz, STEPS, held, NB) for a in (mine, other)]
         both = jnp.stack([jnp.where(core == 0, both[0], both[1]), jnp.where(core == 0, both[1], both[0])])
         full = both.transpose(3, 2, 1, 0, 4, 5).reshape(STEPS, local, NB)
-        factor, kept, select, parts = pl.pallas_call(
+        factor, kept, select = pl.pallas_call(
             rows_kernel,
             out_shape=(
                 jax.ShapeDtypeStruct((local, 2 * TOP), BF),
                 jax.ShapeDtypeStruct((local, width), BF),
                 jax.ShapeDtypeStruct((2 * NB, start_of(STEPS)), BF),
-                jax.ShapeDtypeStruct((STEPS, 3 * NB, NB), BF),
             ),
-            in_specs=[SM, VM, VM, VM, VM],
-            out_specs=(VM, VM, VM, VM),
+            in_specs=[SM, VM, VM, VM],
+            out_specs=(VM, VM, VM),
             cost_estimate=cost(2 * TOP * local * NB, 12 << 20),
-        )(first1, pivots, full, matrix, inverses)
-        low_mine, factor, kept, select, parts = lax.optimization_barrier((low_mine, factor, kept, select, parts))
-        return low_mine, lax.ppermute(low_mine, "c", swap), factor, kept, select, parts
-
-    def nothing(panels, pivots):
-        return tuple(jnp.zeros(o.shape, o.dtype) for o in jax.eval_shape(gather, panels, pivots))
-
-    low_mine, low_other, factor, kept, select, parts = lax.cond(y < ny, gather, nothing, panels, pivots)
+        )(first1, pivots, full, matrix)
+        low_mine, factor, kept, select = lax.optimization_barrier((low_mine, factor, kept, select))
+        return low_mine, lax.ppermute(low_mine, "c", swap), factor, kept, select
+
+    def nothing(column, pivots):
+        return tuple(jnp.zeros(o.shape, o.dtype) for o in jax.eval_shape(gather, column, pivots))
+
+    low_mine, low_other, factor, kept, select = lax.cond(y < ny, gather, nothing, column, pivots)
 
     chunk = low_mine.size // (nzx * NB)
     low_shape = (nzx * chunk // CHUNK, CHUNK, NB)
@@ -244,7 +268,8 @@
         scratch_shapes=[
             pltpu.VMEM((2, TOP, width), BF),
             pltpu.VMEM((2,) + low_shape, BF),
-            pltpu.VMEM(parts.shape, BF),
+            pltpu.VMEM(inverses.shape, F32),
+            pltpu.VMEM((STEPS, 3 * NB, NB), BF),
             pltpu.VMEM(select.shape, BF),
             pltpu.VMEM(factor.shape, BF),
             pltpu.VMEM((local, width), BF),
@@ -254,7 +279,7 @@
             pltpu.SemaphoreType.DMA((BLOCKS,)),
         ],
         cost_estimate=cost(4 * TOP * local * width, 16 << 20),
-    )(core1, content, low_mine.reshape(low_shape), low_other.reshape(low_shape), parts, select, factor, kept)
+    )(core1, content, low_mine.reshape(low_shape), low_other.reshape(low_shape), inverses, select, factor, kept)
 
 
 def solution(mesh):

time: 123 us -> 117 us (0.951)
  blocking collectives: 18.2 us -> 0 us
  starting transfers between devices: 26.2 us -> 42.6 us
  waiting for transfers between devices: 31.7 us -> 22.4 us
  local copies, waits for them, and re-layouts: 7.67 us -> 13.3 us
    all_to_all x3 -> x2, waiting for transfers between devices: 29.7 us -> 8.96 us  [spread(): lax.all_to_all(jnp.broadcast_to(x[None], (parts,) + x.shape), axes, 0, 0,...]
    all_to_all x1 -> x0, blocking collectives: 18.2 us -> none  [gather(): lax.all_to_all(part, ('y', 'c'), 0, 0, tiled=True).astype(F32).sum(0)]
    all_to_all x0 -> x2, starting transfers between devices: none -> 16 us  [the longest x1 10.3 us: gather(): column = lax.all_to_all(column, 'z', 0, 0, tiled=True)]
    all_to_all x0 -> x2, waiting for transfers between devices: none -> 11.4 us  [the longest x1 11.4 us: gather(): column = lax.all_to_all(column, 'z', 0, 0, tiled=True)]
    ppermute x1 -> x4, starting transfers between devices: 2.09 us -> 11.5 us  [the longest x3 9.46 us: gather(): lax.ppermute(column, 'x', [((i + s) % nx, i) for i in range(nx)])]
    all_to_all x3 -> x2, starting transfers between devices: 21.2 us -> 13.1 us  [spread(): lax.all_to_all(jnp.broadcast_to(x[None], (parts,) + x.shape), axes, 0, 0,...]
    cond x1 -> x7, local copies, waits for them, and re-layouts: 0.01 us -> 5.16 us
    another operation x0 -> x2, local copies, waits for them, and re-layouts: none -> 2.82 us  [the longest x1 2.09 us: gather(): jnp.stack([jnp.where(core == 0, both[0], both[1]), jnp.where(core == 0, b...]
  transfers between devices with their start and end apart: 6 -> 10, of which waited for: 4 -> 4; matrix products, arithmetic and copies ran while one was open for 8% -> 14% of each run, Pallas kernels for 6% -> 7%
where the time goes in v6:
time: 117 us; the launch traced here: 115 us
  starting transfers between devices  42.6 us (36%)
  waiting for transfers between devices  22.4 us (19%)
  Pallas kernels  19.4 us (17%)
  between operations  13.4 us (11%)
  local copies, waits for them, and re-layouts  13.3 us (11%)
  other arithmetic  3.57 us (3%)
    all_to_all x2, starting transfers between devices, spread(): lax.all_to_all(jnp.broadcast_to(x[None], (parts,) + x.shape), axes, 0, 0,...  13.1 us
    all_to_all x1, waiting for transfers between devices, gather(): column = lax.all_to_all(column, 'z', 0, 0, tiled=True)  11.4 us
    all_to_all x1, starting transfers between devices, gather(): column = lax.all_to_all(column, 'z', 0, 0, tiled=True)  10.3 us
    ppermute x3, starting transfers between devices, gather(): lax.ppermute(column, 'x', [((i + s) % nx, i) for i in range(nx)])  9.46 us
    all_to_all x2, waiting for transfers between devices, spread(): lax.all_to_all(jnp.broadcast_to(x[None], (parts,) + x.shape), axes, 0, 0,...  8.96 us
    pallas_call x1, Pallas kernels, gather(): pl.pallas_call(rows_kernel, out_shape=(jax.ShapeDtypeStruct((local, 2 * T...  7.72 us
    pallas_call x1, Pallas kernels, per_device(): pl.pallas_call(solve_kernel, out_shape=jax.ShapeDtypeStruct((local, width...  7.47 us
    all_to_all x1, starting transfers between devices, gather(): lax.all_to_all(part, ('c', 'x'), 0, 0, tiled=True).astype(F32).sum(0)  5.69 us
  transfers between devices with their start and end apart: 10, of which 4 were waited for; matrix products, arithmetic and copies ran while one was open for 14% of the time, Pallas kernels for 7%

profile of v6, /device:TPU:6, one launch (start us, length us, event | category | flops | bytes accessed | tf_op | source)
XLA Modules:
  0.0 114.8 jit_solution(6143751592049082248)
XLA Ops:
  6.5 4.2 %shard_map.46 = bf16[2,768,384]{2,1,0:T(8,128)(2,1)} custom-call(s32[1]{0:T(128)} %bitcast.33.first_ref, s32[6,128]{1,0:T(8,128)} %rows_ref.1, bf16[1536,384]{1,0:T(8,128)(2,1)} %matrix_hbm.1), custom_call_target="tpu_custom_call" | custom-call | flops 905969664 | bytes 4194304 | tf_op jit(solution)/shard_map/pallas_call | solution.py:198
  10.8 0.8 broadcast_in_dim.74
  11.6 88.9 %conditional.1 = (bf16[32,64,128]{2,1,0:T(8,128)(2,1)}, bf16[32,64,128]{2,1,0:T(8,128)(2,1)}, bf16[1536,1536]{1,0:T(8,128)(2,1)}, bf16[1536,384]{1,0:T(8,128)(2,1)S(1)}, bf16[256,3840]{1,0:T(8,128)(2,1)S(1)}) conditional(s32[]{:T(128)} %convert_element_type.2, () %tuple.16, (s32[6,128]{1,0:T(8,128)S(1)}, s32[]{:T(128)}, s32[]{:T(128)}, s32[]{:T(128)}, ...), branch_computations={%region_1.0_spmd, %region_2.5_spmd} | conditional | flops 304750112 | bytes 49001260 | solution.py:259
  11.6 10.3 %all-to-all-start = ((bf16[8,144,128]{2,1,0:T(8,128)(2,1)}), bf16[8,144,128]{2,1,0:T(8,128)(2,1)S(1)}, u32[]{:S(2)}, u32[]{:S(2)}) async-start(bf16[8,144,128]{2,1,0:T(8,128)(2,1)} %get-tuple-element.26), calls=%async_computation | async-start | bytes 589824 | tf_op jit(solution)/shard_map/cond/branch_1_fun/all_to_all | solution.py:215
  23.1 11.4 %all-to-all-done = bf16[8,144,128]{2,1,0:T(8,128)(2,1)S(1)} async-done(((bf16[8,144,128]{2,1,0:T(8,128)(2,1)}), bf16[8,144,128]{2,1,0:T(8,128)(2,1)S(1)}, u32[]{:S(2)}, u32[]{:S(2)}) %all-to-all-start) | async-done | bytes 294944 | tf_op jit(solution)/shard_map/cond/branch_1_fun/all_to_all | solution.py:215
  34.5 1.3 %gather_fusion = bf16[512,128]{1,0:T(8,128)(2,1)S(1)} fusion(bf16[1152,128]{1,0:T(8,128)(2,1)S(1)} %bitcast.336, s32[1024]{0:T(1024)S(1)} %pad_clamp_fusion), kind=kCustom, calls=%fused_computation | custom fusion | bytes 264192 | tf_op jit(solution)/shard_map/cond/branch_1_fun/jit(_take)/gather | solution.py:228
  35.8 2.7 %collective-permute-start = (bf16[8,144,128]{2,1,0:T(8,128)(2,1)S(1)}, bf16[8,144,128]{2,1,0:T(8,128)(2,1)S(1)}, u32[]{:S(2)}, u32[]{:S(2)}) collective-permute-start(bf16[8,144,128]{2,1,0:T(8,128)(2,1)S(1)} %all-to-all-done), channel_id=1, source_target_pairs={{2,0},{4,2},{6,4},{0,6},{3,1},{5,3},{7,5},{1,7},{10,8},{12,10},{14... | collective-permute-start | bytes 884744 | tf_op jit(solution)/shard_map/cond/branch_1_fun/ppermute | solution.py:233
  38.6 0.9 select_select_fusion
  39.4 5.7 %all-to-all-start.1 = ((bf16[8,64,128]{2,1,0:T(8,128)(2,1)}), bf16[8,64,128]{2,1,0:T(8,128)(2,1)S(1)}, u32[]{:S(2)}, u32[]{:S(2)}) async-start(bf16[8,64,128]{2,1,0:T(8,128)(2,1)} %select_select_fusion), calls=%async_computation.1 | async-start | bytes 262144 | tf_op jit(solution)/shard_map/cond/branch_1_fun/all_to_all | solution.py:230
  45.1 2.0 %collective-permute-start.2 = (bf16[8,144,128]{2,1,0:T(8,128)(2,1)S(1)}, bf16[8,144,128]{2,1,0:T(8,128)(2,1)S(1)}, u32[]{:S(2)}, u32[]{:S(2)}) collective-permute-start(bf16[8,144,128]{2,1,0:T(8,128)(2,1)S(1)} %all-to-all-done), channel_id=1, source_target_pairs={{6,0},{0,2},{2,4},{4,6},{7,1},{1,3},{3,5},{5,7},{14,8},{8,10},{10,... | collective-permute-start | bytes 884744 | tf_op jit(solution)/shard_map/cond/branch_1_fun/ppermute | solution.py:233
  47.1 4.7 %collective-permute-start.1 = (bf16[8,144,128]{2,1,0:T(8,128)(2,1)S(1)}, bf16[8,144,128]{2,1,0:T(8,128)(2,1)S(1)}, u32[]{:S(2)}, u32[]{:S(2)}) collective-permute-start(bf16[8,144,128]{2,1,0:T(8,128)(2,1)S(1)} %all-to-all-done), channel_id=1, source_target_pairs={{4,0},{6,2},{0,4},{2,6},{5,1},{7,3},{1,5},{3,7},{12,8},{14,10},{8,... | collective-permute-start | bytes 884744 | tf_op jit(solution)/shard_map/cond/branch_1_fun/ppermute | solution.py:233
  53.3 7.1 %all-to-all-start.2 = ((bf16[8,64,128]{2,1,0:T(8,128)(2,1)}), bf16[8,64,128]{2,1,0:T(8,128)(2,1)S(1)}, u32[]{:S(2)}, u32[]{:S(2)}) async-start(bf16[8,64,128]{2,1,0:T(8,128)(2,1)} %broadcast_in_dim.69), calls=%async_computation.2 | async-start | bytes 262144 | tf_op jit(solution)/shard_map/cond/branch_1_fun/all_to_all | solution.py:182
  65.6 1.3 %constant_dynamic-slice_fusion = bf16[4,8,144,128]{3,2,1,0:T(8,128)(2,1)S(1)} fusion(bf16[8,8,144,128]{3,2,1,0:T(8,128)(2,1)} %bitcast_dynamic-update-slice_fusion.1, s32[]{:T(128)S(6)} %select_n.407), kind=kLoop, calls=%fused_computation.144 | loop fusion | bytes 2359300 | tf_op jit(solution)/shard_map/cond/branch_1_fun/dynamic_slice | solution.py:234
  66.9 2.6 %all-to-all-done.2 = bf16[8,64,128]{2,1,0:T(8,128)(2,1)S(1)} async-done(((bf16[8,64,128]{2,1,0:T(8,128)(2,1)}), bf16[8,64,128]{2,1,0:T(8,128)(2,1)S(1)}, u32[]{:S(2)}, u32[]{:S(2)}) %all-to-all-start.2) | async-done | bytes 131104 | tf_op jit(solution)/shard_map/cond/branch_1_fun/all_to_all | solution.py:182
  69.5 1.9 %collective-permute-start.3 = (bf16[4,8,144,128]{3,2,1,0:T(8,128)(2,1)S(1)}, bf16[4,8,144,128]{3,2,1,0:T(8,128)(2,1)}, u32[]{:S(2)}, u32[]{:S(2)}) collective-permute-start(bf16[4,8,144,128]{3,2,1,0:T(8,128)(2,1)S(1)} %constant_dynamic-slice_fusion), channel_id=1, source_target_pairs={{0,1},{1,0},{2,3},{3,2},{4,5},{5,4},{6,7},{7,6},{8,9},{9,8},{10,11... | collective-permute-start | bytes 3538952 | tf_op jit(solution)/shard_map/cond/branch_1_fun/ppermute | solution.py:236
  71.4 1.0 broadcast_in_dim.70
  72.4 6.0 %all-to-all-start.3 = ((bf16[32,64,128]{2,1,0:T(8,128)(2,1)}), bf16[32,64,128]{2,1,0:T(8,128)(2,1)}, u32[]{:S(2)}, u32[]{:S(2)}) async-start(bf16[32,64,128]{2,1,0:T(8,128)(2,1)} %broadcast_in_dim.70), calls=%async_computation.3 | async-start | bytes 1048576 | tf_op jit(solution)/shard_map/cond/branch_1_fun/all_to_all | solution.py:182
  78.4 1.4 %broadcast_select_fusion.1 = (bf16[4,8,144,128]{3,2,1,0:T(8,128)(2,1)S(1)}, bf16[4,8,144,128]{3,2,1,0:T(8,128)(2,1)S(1)}) fusion(bf16[4,8,144,128]{3,2,1,0:T(8,128)(2,1)S(1)} %constant_dynamic-slice_fusion, bf16[4,8,144,128]{3,2,1,0:T(8,128)(2,1)} %collective-permute-done.3, pred[]{:T(512)S(6)} %eq.148), kind=kLoop, calls=%fused_computation.3 | loop fusion | flops 1179648 | bytes 4718593 | tf_op jit(solution)/shard_map/cond/branch_1_fun/jit(_where)/select_n | solution.py:240
  80.1 2.1 %copy.13 = bf16[2,4,8,6,24,128]{5,4,0,1,2,3:T(8,128)(2,1)} copy(bf16[2,4,8,6,24,128]{5,4,3,2,1,0:T(8,128)(2,1)S(1)} %pad_maximum_fusion) | data formatting | bytes 4718592 | tf_op jit(solution)/shard_map/cond/branch_1_fun/stack | solution.py:240
  82.2 7.7 %branch_1_fun.1 = (bf16[1536,1536]{1,0:T(8,128)(2,1)}, bf16[1536,384]{1,0:T(8,128)(2,1)S(1)}, bf16[256,3840]{1,0:T(8,128)(2,1)S(1)}) custom-call(s32[1]{0:T(128)} %get-tuple-element.28.first_ref, s32[6,128]{1,0:T(8,128)S(1)} %get-tuple-element.21.rows_ref, bf16[6,1536,128]{2,1,0:T(8,128)(2,1)} %bitcast.337, bf16[1536,384]{1,0:T(8,128)(2,1)} %get-tuple-element.30.matrix_ref), custom_call_target="tpu_custom_call" | custom-call | flops 301989888 | bytes 12582912 | tf_op jit(solution)/shard_map/cond/branch_1_fun/pallas_call | solution.py:242
  89.9 6.4 %all-to-all-done.3 = bf16[32,64,128]{2,1,0:T(8,128)(2,1)} async-done(((bf16[32,64,128]{2,1,0:T(8,128)(2,1)}), bf16[32,64,128]{2,1,0:T(8,128)(2,1)}, u32[]{:S(2)}, u32[]{:S(2)}) %all-to-all-start.3) | async-done | bytes 524320 | tf_op jit(solution)/shard_map/cond/branch_1_fun/all_to_all | solution.py:182
  96.3 2.1 %collective-permute-start.4 = (bf16[32,64,128]{2,1,0:T(8,128)(2,1)}, bf16[32,64,128]{2,1,0:T(8,128)(2,1)}, u32[]{:S(2)}, u32[]{:S(2)}) collective-permute-start(bf16[32,64,128]{2,1,0:T(8,128)(2,1)} %all-to-all-done.3), channel_id=1, source_target_pairs={{0,1},{1,0},{2,3},{3,2},{4,5},{5,4},{6,7},{7,6},{8,9},{9,8},{10,11... | collective-permute-start | bytes 1572872 | tf_op jit(solution)/shard_map/cond/branch_1_fun/ppermute | solution.py:254
  98.4 2.0 %collective-permute-done.4 = bf16[32,64,128]{2,1,0:T(8,128)(2,1)} collective-permute-done((bf16[32,64,128]{2,1,0:T(8,128)(2,1)}, bf16[32,64,128]{2,1,0:T(8,128)(2,1)}, u32[]{:S(2)}, u32[]{:S(2)}) %collective-permute-start.4) | collective-permute-done | bytes 524320 | tf_op jit(solution)/shard_map/cond/branch_1_fun/ppermute | solution.py:254
  100.5 7.5 %shard_map.47 = bf16[1536,384]{1,0:T(8,128)(2,1)} custom-call(s32[1]{0:T(128)} %bitcast.32.core_ref, bf16[2,768,384]{2,1,0:T(8,128)(2,1)} %all-reduce.2.cloned.1.call-done.content_hbm, bf16[32,64,128]{2,1,0:T(8,128)(2,1)} %get-tuple-element.47.mine_hbm, bf16[32,64,128]{2,1,0:T(8,128)(2,1)} %get-tuple-element.48.other_hbm, f32[6,128,128]{2,1,0:T(8,128)} %inverses_hbm.1, ...), custom_call_target="tpu_custom_call" | custom-call | flops 1811939328 | bytes 16777216 | tf_op jit(solution)/shard_map/pallas_call | solution.py:263
  (61 shorter events, 8.1 us)
Async XLA Ops:
  6.5 4.2 %copy-start = (bf16[6,24,128]{2,1,0:T(8,128)(2,1)S(1)}, bf16[6,24,128]{2,1,0:T(8,128)(2,1)}, u32[]{:S(2)}) copy-start(bf16[6,24,128]{2,1,0:T(8,128)(2,1)} %param.7) | copy-start | bytes 110596
  6.5 93.9 %all-reduce.2.cloned.1.call-start = ((), (), s32[]{:S(2)}) async-start(), calls=%async_computation.4 | async-start | bytes 2359296 | tf_op jit(solution)/shard_map/psum | solution.py:211
  6.5 5.0 %copy-start.1 = (s32[6,128]{1,0:T(8,128)S(1)}, s32[6,128]{1,0:T(8,128)}, u32[]{:S(2)}) copy-start(s32[6,128]{1,0:T(8,128)} %rows_ref.1) | copy-start | bytes 9220
  11.6 22.9 %all-to-all-start = ((bf16[8,144,128]{2,1,0:T(8,128)(2,1)}), bf16[8,144,128]{2,1,0:T(8,128)(2,1)S(1)}, u32[]{:S(2)}, u32[]{:S(2)}) async-start(bf16[8,144,128]{2,1,0:T(8,128)(2,1)} %get-tuple-element.26), calls=%async_computation | async-start | bytes 589824 | tf_op jit(solution)/shard_map/cond/branch_1_fun/all_to_all | solution.py:215
  35.8 24.6 %collective-permute-start = (bf16[8,144,128]{2,1,0:T(8,128)(2,1)S(1)}, bf16[8,144,128]{2,1,0:T(8,128)(2,1)S(1)}, u32[]{:S(2)}, u32[]{:S(2)}) collective-permute-start(bf16[8,144,128]{2,1,0:T(8,128)(2,1)S(1)} %all-to-all-done), channel_id=1, source_target_pairs={{2,0},{4,2},{6,4},{0,6},{3,1},{5,3},{7,5},{1,7},{10,8},{12,10},{14... | collective-permute-start | bytes 884744 | tf_op jit(solution)/shard_map/cond/branch_1_fun/ppermute | solution.py:233
  39.4 13.2 %all-to-all-start.1 = ((bf16[8,64,128]{2,1,0:T(8,128)(2,1)}), bf16[8,64,128]{2,1,0:T(8,128)(2,1)S(1)}, u32[]{:S(2)}, u32[]{:S(2)}) async-start(bf16[8,64,128]{2,1,0:T(8,128)(2,1)} %select_select_fusion), calls=%async_computation.1 | async-start | bytes 262144 | tf_op jit(solution)/shard_map/cond/branch_1_fun/all_to_all | solution.py:230
  45.1 16.8 %collective-permute-start.2 = (bf16[8,144,128]{2,1,0:T(8,128)(2,1)S(1)}, bf16[8,144,128]{2,1,0:T(8,128)(2,1)S(1)}, u32[]{:S(2)}, u32[]{:S(2)}) collective-permute-start(bf16[8,144,128]{2,1,0:T(8,128)(2,1)S(1)} %all-to-all-done), channel_id=1, source_target_pairs={{6,0},{0,2},{2,4},{4,6},{7,1},{1,3},{3,5},{5,7},{14,8},{8,10},{10,... | collective-permute-start | bytes 884744 | tf_op jit(solution)/shard_map/cond/branch_1_fun/ppermute | solution.py:233
  47.1 14.0 %collective-permute-start.1 = (bf16[8,144,128]{2,1,0:T(8,128)(2,1)S(1)}, bf16[8,144,128]{2,1,0:T(8,128)(2,1)S(1)}, u32[]{:S(2)}, u32[]{:S(2)}) collective-permute-start(bf16[8,144,128]{2,1,0:T(8,128)(2,1)S(1)} %all-to-all-done), channel_id=1, source_target_pairs={{4,0},{6,2},{0,4},{2,6},{5,1},{7,3},{1,5},{3,7},{12,8},{14,10},{8,... | collective-permute-start | bytes 884744 | tf_op jit(solution)/shard_map/cond/branch_1_fun/ppermute | solution.py:233
  53.3 16.2 %all-to-all-start.2 = ((bf16[8,64,128]{2,1,0:T(8,128)(2,1)}), bf16[8,64,128]{2,1,0:T(8,128)(2,1)S(1)}, u32[]{:S(2)}, u32[]{:S(2)}) async-start(bf16[8,64,128]{2,1,0:T(8,128)(2,1)} %broadcast_in_dim.69), calls=%async_computation.2 | async-start | bytes 262144 | tf_op jit(solution)/shard_map/cond/branch_1_fun/all_to_all | solution.py:182
  69.5 8.9 %collective-permute-start.3 = (bf16[4,8,144,128]{3,2,1,0:T(8,128)(2,1)S(1)}, bf16[4,8,144,128]{3,2,1,0:T(8,128)(2,1)}, u32[]{:S(2)}, u32[]{:S(2)}) collective-permute-start(bf16[4,8,144,128]{3,2,1,0:T(8,128)(2,1)S(1)} %constant_dynamic-slice_fusion), channel_id=1, source_target_pairs={{0,1},{1,0},{2,3},{3,2},{4,5},{5,4},{6,7},{7,6},{8,9},{9,8},{10,11... | collective-permute-start | bytes 3538952 | tf_op jit(solution)/shard_map/cond/branch_1_fun/ppermute | solution.py:236
  72.4 23.9 %all-to-all-start.3 = ((bf16[32,64,128]{2,1,0:T(8,128)(2,1)}), bf16[32,64,128]{2,1,0:T(8,128)(2,1)}, u32[]{:S(2)}, u32[]{:S(2)}) async-start(bf16[32,64,128]{2,1,0:T(8,128)(2,1)} %broadcast_in_dim.70), calls=%async_computation.3 | async-start | bytes 1048576 | tf_op jit(solution)/shard_map/cond/branch_1_fun/all_to_all | solution.py:182
  96.3 4.1 %collective-permute-start.4 = (bf16[32,64,128]{2,1,0:T(8,128)(2,1)}, bf16[32,64,128]{2,1,0:T(8,128)(2,1)}, u32[]{:S(2)}, u32[]{:S(2)}) collective-permute-start(bf16[32,64,128]{2,1,0:T(8,128)(2,1)} %all-to-all-done.3), channel_id=1, source_target_pairs={{0,1},{1,0},{2,3},{3,2},{4,5},{5,4},{6,7},{7,6},{8,9},{9,8},{10,11... | collective-permute-start | bytes 1572872 | tf_op jit(solution)/shard_map/cond/branch_1_fun/ppermute | solution.py:254
Sparse Core Ops, SparseCore 0:
  11.7 86.7 all-reduce.1

commit v7 on v6

--- a/solution.py
+++ b/solution.py
@@ -14,6 +14,7 @@
 PAIRS = [(k, j) for k in range(1, STEPS) for j in range(k)]
 CHUNK = 64
 BLOCKS = 3
+LONG = 1 << 36
 BF = jnp.bfloat16
 F32 = jnp.float32
 VM = pl.BlockSpec(memory_space=pltpu.VMEM)
@@ -33,18 +34,24 @@
     return jnp.broadcast_to(row.astype(F32), (NB, NB)).T.astype(jnp.int32)
 
 
-def masks(k, rows_ref):
-    ones = jnp.ones((NB, NB), BF)
+def matches(k, rows_ref):
     ids = jnp.concatenate([iota((NB, NB), 0) + k * NB, columns(rows_ref[k:k + 1, :])])
-    found = jnp.zeros((2 * NB, NB), F32)
+    return ids, [jnp.where(ids == rows_ref[j:j + 1, :], 1.0, 0.0).astype(F32) for j in range(k)]
+
+
+def any_lane(same):
+    return jnp.dot(same.astype(BF), jnp.ones((NB, NB), BF), preferred_element_type=F32)
+
+
+def last_match(same):
+    hits = [any_lane(s) for s in same]
+    found = jnp.zeros(same[0].shape, F32)
     out = []
-    for j in reversed(range(k)):
-        same = jnp.where(ids == rows_ref[j:j + 1, :], 1.0, 0.0).astype(F32)
+    for s, hit in zip(reversed(same), reversed(hits)):
         live = 1.0 - found
-        out.append((j, same * live, live))
-        hit = jnp.dot(same.astype(BF), ones, preferred_element_type=F32)
+        out.append((s * live, live))
         found = jnp.maximum(found, hit)
-    return ids, out, found < 0.5
+    return out[::-1], found < 0.5
 
 
 def share_kernel(first_ref, rows_ref, matrix_hbm, share_hbm, matrix, hot, share, sems):
@@ -54,8 +61,8 @@
     local, width = matrix.shape
     fresh = []
     for k in range(STEPS):
-        ids, _, new = masks(k, rows_ref)
-        fresh.append(new)
+        ids, same = matches(k, rows_ref)
+        fresh.append(any_lane(sum(same, jnp.zeros((2 * NB, NB), F32))) < 0.5)
         at = k * NB
         where = ids[NB:] - first
         for c in range(0, local, NB):
@@ -83,36 +90,51 @@
         store.wait()
 
 
-def rows_kernel(first_ref, rows_ref, panels_ref, matrix_ref, factor_ref, kept_ref, select_ref):
+def select_kernel(rows_ref, select_ref):
     for k in range(1, STEPS):
-        for j, same, live in masks(k, rows_ref)[1]:
+        for j, (last, live) in enumerate(last_match(matches(k, rows_ref)[1])[0]):
             at = start_of(k) + 2 * NB * j
-            select_ref[:, at:at + NB] = same.astype(BF)
+            select_ref[:, at:at + NB] = last.astype(BF)
             select_ref[:, at + NB:at + 2 * NB] = (-live).astype(BF)
-    ones = jnp.ones((NB, NB), BF)
+
+
+def mark_kernel(first_ref, rows_ref, matrix_ref, last_ref, live_ref, kept_ref):
     height = 2 * NB
 
     def one(step, carry):
         at = pl.multiple_of(step * height, height)
         ids = iota((height, NB), 0) + first_ref[0] + at
         is_top = ids < TOP
-        found = jnp.zeros((height, NB), F32)
-        for j in reversed(range(STEPS)):
-            same = jnp.where((ids == rows_ref[j:j + 1, :]) & ~is_top, 1.0, 0.0).astype(F32)
-            live = 1.0 - found
-            factor_ref[pl.ds(at, height), 2 * NB * j:2 * NB * j + NB] = (same * live).astype(BF)
-            diag = jnp.where(ids - NB * j == iota((height, NB), 1), 1.0, 0.0).astype(F32)
-            lower = -live * panels_ref[j, pl.ds(at, height), :].astype(F32)
-            factor_ref[pl.ds(at, height), 2 * NB * j + NB:2 * NB * (j + 1)] = jnp.where(is_top, diag, lower).astype(BF)
-            hit = jnp.dot(same.astype(BF), ones, preferred_element_type=F32)
-            found = jnp.maximum(found, hit)
-        fresh = (found < 0.5) & ~is_top
+        same = [jnp.where((ids == rows_ref[j:j + 1, :]) & ~is_top, 1.0, 0.0).astype(F32) for j in range(STEPS)]
+        state, fresh = last_match(same)
+        for j, (last, live) in enumerate(state):
+            last_ref[pl.ds(at, height), NB * j:NB * (j + 1)] = last.astype(BF)
+            live_ref[pl.ds(at, height), NB * j:NB * (j + 1)] = jnp.where(is_top, 0.0, -live).astype(BF)
+        fresh = fresh & ~is_top
         for c in range(0, matrix_ref.shape[1], NB):
             old = matrix_ref[pl.ds(at, height), c:c + NB].astype(F32)
             kept_ref[pl.ds(at, height), c:c + NB] = jnp.where(fresh, old, 0.0).astype(BF)
         return carry
 
     lax.fori_loop(0, matrix_ref.shape[0] // height, one, 0)
+
+
+def rows_kernel(first_ref, panels_ref, last_ref, live_ref, factor_ref):
+    height = 2 * NB
+
+    def one(step, carry):
+        at = pl.multiple_of(step * height, height)
+        block = pl.ds(at, height)
+        ids = iota((height, NB), 0) + first_ref[0] + at
+        for j in range(STEPS):
+            here = 2 * NB * j
+            factor_ref[block, here:here + NB] = last_ref[block, NB * j:NB * (j + 1)]
+            diag = jnp.where((ids - NB * j == iota((height, NB), 1)) & (ids < TOP), 1.0, 0.0).astype(BF)
+            lower = live_ref[block, NB * j:NB * (j + 1)] * panels_ref[j, block, :]
+            factor_ref[block, here + NB:here + 2 * NB] = lower + diag
+        return carry
+
+    lax.fori_loop(0, panels_ref.shape[1] // height, one, 0)
 
 
 def solve_kernel(core_ref, content_hbm, mine_hbm, other_hbm, inverses_hbm, select_hbm, factor_hbm, kept_hbm, out_hbm,
@@ -193,8 +215,6 @@
     first1 = first.reshape(1).astype(jnp.int32)
     core1 = core.reshape(1).astype(jnp.int32)
 
-    column = jnp.broadcast_to(panels.reshape(1, STEPS * held, NB), (nz, STEPS * held, NB))
-
     share = pl.pallas_call(
         share_kernel,
         out_shape=jax.ShapeDtypeStruct((2, TOP, width), BF),
@@ -209,10 +229,10 @@
         cost_estimate=cost(2 * TOP * local * width, 4 << 20),
     )(first1, pivots, matrix)
     content = lax.psum(share, "y")
-    column, pivots, _ = lax.optimization_barrier((column, pivots, share))
-
-    def gather(column, pivots):
-        column = lax.all_to_all(column, "z", 0, 0, tiled=True)
+    panels, pivots, _ = lax.optimization_barrier((panels, pivots, share))
+
+    def gather(panels, pivots):
+        column = spread(panels.reshape(STEPS * held, NB), "z", nz).reshape(nz, STEPS * held, NB)
 
         idx = []
         for k, j in PAIRS:
@@ -227,36 +247,50 @@
         idx = lax.dynamic_slice(idx.reshape(nc, nz, nx * chunk), (0, z, 0), (nc, 1, nx * chunk)).reshape(nc * nx * chunk)
         part = jnp.take(column.reshape(-1, NB), jnp.maximum(idx, 0), axis=0)
         part = jnp.where((idx >= 0)[:, None], part, jnp.zeros((), BF)).reshape(nc * nx, chunk, NB)
-        part = lax.all_to_all(part, ("c", "x"), 0, 0, tiled=True).astype(F32).sum(0).astype(BF)
+        part = lax.all_to_all(part, ("c", "x"), 0, 0, tiled=True)
+        part = part.astype(F32).sum(0).astype(BF)
         part = spread(part, "y", ny).reshape(ny, chunk, NB).astype(F32).sum(0).astype(BF)
 
         blocks = [column] + [lax.ppermute(column, "x", [((i + s) % nx, i) for i in range(nx)]) for s in range(1, nx)]
         mine = lax.dynamic_slice_in_dim(jnp.stack(blocks + blocks), (nx - x) % nx, nx)
-        part, mine = lax.optimization_barrier((part, mine))
+        part = jnp.broadcast_to(part[None], (nzx, chunk, NB))
+        part, mine, pivots = lax.optimization_barrier((part, mine, pivots))
         other = lax.ppermute(mine, "c", swap)
-        low_mine = spread(part, ("z", "x"), nzx)
+        select = pl.pallas_call(
+            select_kernel,
+            out_shape=jax.ShapeDtypeStruct((2 * NB, start_of(STEPS)), BF),
+            in_specs=[VM],
+            out_specs=VM,
+            cost_estimate=cost(LONG, 2 << 20),
+        )(pivots)
+        marked = pl.pallas_call(
+            mark_kernel,
+            out_shape=(jax.ShapeDtypeStruct((local, TOP), BF), jax.ShapeDtypeStruct((local, TOP), BF), jax.ShapeDtypeStruct((local, width), BF)),
+            in_specs=[SM, VM, VM],
+            out_specs=(VM, VM, VM),
+            cost_estimate=cost(LONG, 6 << 20),
+        )(first1, pivots, matrix)
+        other, select, *marked = lax.optimization_barrier((other, select, *marked))
+        low_mine = lax.all_to_all(part, ("z", "x"), 0, 0, tiled=True)
 
         both = [a.reshape(nx, nz, STEPS, held, NB) for a in (mine, other)]
         both = jnp.stack([jnp.where(core == 0, both[0], both[1]), jnp.where(core == 0, both[1], both[0])])
         full = both.transpose(3, 2, 1, 0, 4, 5).reshape(STEPS, local, NB)
-        factor, kept, select = pl.pallas_call(
+        factor = pl.pallas_call(
             rows_kernel,
-            out_shape=(
-                jax.ShapeDtypeStruct((local, 2 * TOP), BF),
-                jax.ShapeDtypeStruct((local, width), BF),
-                jax.ShapeDtypeStruct((2 * NB, start_of(STEPS)), BF),
-            ),
+            out_shape=jax.ShapeDtypeStruct((local, 2 * TOP), BF),
             in_specs=[SM, VM, VM, VM],
-            out_specs=(VM, VM, VM),
+            out_specs=VM,
             cost_estimate=cost(2 * TOP * local * NB, 12 << 20),
-        )(first1, pivots, full, matrix)
-        low_mine, factor, kept, select = lax.optimization_barrier((low_mine, factor, kept, select))
+        )(first1, full, *marked[:2])
+        kept = marked[2]
+        low_mine, factor = lax.optimization_barrier((low_mine, factor))
         return low_mine, lax.ppermute(low_mine, "c", swap), factor, kept, select
 
-    def nothing(column, pivots):
-        return tuple(jnp.zeros(o.shape, o.dtype) for o in jax.eval_shape(gather, column, pivots))
-
-    low_mine, low_other, factor, kept, select = lax.cond(y < ny, gather, nothing, column, pivots)
+    def nothing(panels, pivots):
+        return tuple(jnp.zeros(o.shape, o.dtype) for o in jax.eval_shape(gather, panels, pivots))
+
+    low_mine, low_other, factor, kept, select = lax.cond(y < ny, gather, nothing, panels, pivots)
 
     chunk = low_mine.size // (nzx * NB)
     low_shape = (nzx * chunk // CHUNK, CHUNK, NB)

time: 117 us -> 118 us (level)
  Pallas kernels: 19.4 us -> 26.4 us
  local copies, waits for them, and re-layouts: 13.3 us -> 6.31 us
  starting transfers between devices: 42.6 us -> 43.8 us
    all_to_all x2, waiting for transfers between devices: 11.4 us -> 0.01 us  [the longest x1 0.01 us: gather(): low_mine = lax.all_to_all(part, ('z', 'x'), 0, 0, tiled=True)]
    all_to_all x2, waiting for transfers between devices: 8.96 us -> 20.1 us  [spread(): lax.all_to_all(jnp.broadcast_to(x[None], (parts,) + x.shape), axes, 0, 0,...]
    pallas_call x1 -> x3, Pallas kernels: 7.72 us -> 14.1 us  [the longest x1 6.67 us: gather(): pl.pallas_call(rows_kernel, out_shape=jax.ShapeDtypeStruct((local, 2 * TO...]
    cond x7 -> x13, local copies, waits for them, and re-layouts: 5.16 us -> 0.28 us
    all_to_all x2, starting transfers between devices: 13.1 us -> 17.4 us  [spread(): lax.all_to_all(jnp.broadcast_to(x[None], (parts,) + x.shape), axes, 0, 0,...]
    all_to_all x2, starting transfers between devices: 16 us -> 12.3 us  [the longest x1 6.3 us: gather(): part = lax.all_to_all(part, ('c', 'x'), 0, 0, tiled=True)]
    another operation x1 -> x0, local copies, waits for them, and re-layouts: 2.09 us -> none  [gather(): jnp.stack([jnp.where(core == 0, both[0], both[1]), jnp.where(core == 0, b...]
    transpose x0 -> x1, local copies, waits for them, and re-layouts: none -> 2.05 us  [gather(): full = both.transpose(3, 2, 1, 0, 4, 5).reshape(STEPS, local, NB)]
  transfers between devices with their start and end apart: 10 -> 10, of which waited for: 4 -> 3; matrix products, arithmetic and copies ran while one was open for 14% -> 9% of each run, Pallas kernels for 7% -> 12%
where the time goes in v7:
time: 118 us; the launch traced here: 116 us
  starting transfers between devices  43.8 us (37%)
  Pallas kernels  26.4 us (22%)
  waiting for transfers between devices  21.8 us (18%)
  between operations  13.4 us (11%)
  local copies, waits for them, and re-layouts  6.31 us (5%)
  other arithmetic  4.08 us (3%)
    all_to_all x2, waiting for transfers between devices, spread(): lax.all_to_all(jnp.broadcast_to(x[None], (parts,) + x.shape), axes, 0, 0,...  20.1 us
    all_to_all x2, starting transfers between devices, spread(): lax.all_to_all(jnp.broadcast_to(x[None], (parts,) + x.shape), axes, 0, 0,...  17.4 us
    ppermute x3, starting transfers between devices, gather(): lax.ppermute(column, 'x', [((i + s) % nx, i) for i in range(nx)])  9.46 us
    pallas_call x1, Pallas kernels, per_device(): pl.pallas_call(solve_kernel, out_shape=jax.ShapeDtypeStruct((local, width...  8.14 us
    pallas_call x1, Pallas kernels, gather(): pl.pallas_call(rows_kernel, out_shape=jax.ShapeDtypeStruct((local, 2 * TO...  6.67 us
    all_to_all x1, starting transfers between devices, gather(): part = lax.all_to_all(part, ('c', 'x'), 0, 0, tiled=True)  6.3 us
    all_to_all x1, starting transfers between devices, gather(): low_mine = lax.all_to_all(part, ('z', 'x'), 0, 0, tiled=True)  5.99 us
    pallas_call x1, Pallas kernels, gather(): pl.pallas_call(mark_kernel, out_shape=(jax.ShapeDtypeStruct((local, TOP),...  5.4 us
  transfers between devices with their start and end apart: 10, of which 3 were waited for; matrix products, arithmetic and copies ran while one was open for 9% of the time, Pallas kernels for 12%

profile of v7, /device:TPU:6, one launch (start us, length us, event | category | flops | bytes accessed | tf_op | source)
XLA Modules:
  0.0 116.1 jit_solution(789984444917838435)
XLA Ops:
  6.5 4.2 %shard_map.46 = bf16[2,768,384]{2,1,0:T(8,128)(2,1)} custom-call(s32[1]{0:T(128)} %bitcast.33.first_ref, s32[6,128]{1,0:T(8,128)} %rows_ref.1, bf16[1536,384]{1,0:T(8,128)(2,1)} %matrix_hbm.1), custom_call_target="tpu_custom_call" | custom-call | flops 905969664 | bytes 4194304 | tf_op jit(solution)/shard_map/pallas_call | solution.py:218
  10.8 90.3 %conditional.1 = (bf16[32,64,128]{2,1,0:T(8,128)(2,1)}, bf16[32,64,128]{2,1,0:T(8,128)(2,1)}, bf16[1536,1536]{1,0:T(8,128)(2,1)}, bf16[1536,384]{1,0:T(8,128)(2,1)}, bf16[256,3840]{1,0:T(8,128)(2,1)}) conditional(s32[]{:T(128)} %convert_element_type.2, () %tuple.17, (s32[6,128]{1,0:T(8,128)S(1)}, s32[]{:T(128)}, s32[]{:T(128)}, s32[]{:T(128)}, ...), branch_computations={%region_1.0_spmd, %region_2.5_spmd} | conditional | flops 137743695872 | bytes 62464896 | solution.py:293
  11.6 10.3 %all-to-all-start = ((bf16[8,144,128]{2,1,0:T(8,128)(2,1)}), bf16[8,144,128]{2,1,0:T(8,128)(2,1)S(1)}, u32[]{:S(2)}, u32[]{:S(2)}) async-start(bf16[8,144,128]{2,1,0:T(8,128)(2,1)} %broadcast_in_dim.68), calls=%async_computation | async-start | bytes 589824 | tf_op jit(solution)/shard_map/cond/branch_1_fun/all_to_all | solution.py:204
  23.1 11.4 %all-to-all-done = bf16[8,144,128]{2,1,0:T(8,128)(2,1)S(1)} async-done(((bf16[8,144,128]{2,1,0:T(8,128)(2,1)}), bf16[8,144,128]{2,1,0:T(8,128)(2,1)S(1)}, u32[]{:S(2)}, u32[]{:S(2)}) %all-to-all-start) | async-done | bytes 294944 | tf_op jit(solution)/shard_map/cond/branch_1_fun/all_to_all | solution.py:204
  34.5 1.3 %gather_fusion = bf16[512,128]{1,0:T(8,128)(2,1)S(1)} fusion(bf16[1152,128]{1,0:T(8,128)(2,1)S(1)} %bitcast.336, s32[1024]{0:T(1024)S(1)} %pad_clamp_fusion), kind=kCustom, calls=%fused_computation | custom fusion | bytes 264192 | tf_op jit(solution)/shard_map/cond/branch_1_fun/jit(_take)/gather | solution.py:248
  35.8 2.7 %collective-permute-start = (bf16[8,144,128]{2,1,0:T(8,128)(2,1)S(1)}, bf16[8,144,128]{2,1,0:T(8,128)(2,1)S(1)}, u32[]{:S(2)}, u32[]{:S(2)}) collective-permute-start(bf16[8,144,128]{2,1,0:T(8,128)(2,1)S(1)} %all-to-all-done), channel_id=1, source_target_pairs={{2,0},{4,2},{6,4},{0,6},{3,1},{5,3},{7,5},{1,7},{10,8},{12,10},{14... | collective-permute-start | bytes 884744 | tf_op jit(solution)/shard_map/cond/branch_1_fun/ppermute | solution.py:254
  38.6 0.8 select_select_fusion
  39.4 6.3 %all-to-all-start.1 = ((bf16[8,64,128]{2,1,0:T(8,128)(2,1)}), bf16[8,64,128]{2,1,0:T(8,128)(2,1)}, u32[]{:S(2)}, u32[]{:S(2)}) async-start(bf16[8,64,128]{2,1,0:T(8,128)(2,1)} %select_select_fusion), calls=%async_computation.1 | async-start | bytes 262144 | tf_op jit(solution)/shard_map/cond/branch_1_fun/all_to_all | solution.py:250
  45.7 2.1 %collective-permute-start.2 = (bf16[8,144,128]{2,1,0:T(8,128)(2,1)S(1)}, bf16[8,144,128]{2,1,0:T(8,128)(2,1)S(1)}, u32[]{:S(2)}, u32[]{:S(2)}) collective-permute-start(bf16[8,144,128]{2,1,0:T(8,128)(2,1)S(1)} %all-to-all-done), channel_id=1, source_target_pairs={{6,0},{0,2},{2,4},{4,6},{7,1},{1,3},{3,5},{5,7},{14,8},{8,10},{10,... | collective-permute-start | bytes 884744 | tf_op jit(solution)/shard_map/cond/branch_1_fun/ppermute | solution.py:254
  47.8 4.7 %collective-permute-start.1 = (bf16[8,144,128]{2,1,0:T(8,128)(2,1)S(1)}, bf16[8,144,128]{2,1,0:T(8,128)(2,1)S(1)}, u32[]{:S(2)}, u32[]{:S(2)}) collective-permute-start(bf16[8,144,128]{2,1,0:T(8,128)(2,1)S(1)} %all-to-all-done), channel_id=1, source_target_pairs={{4,0},{6,2},{0,4},{2,6},{5,1},{7,3},{1,5},{3,7},{12,8},{14,10},{8,... | collective-permute-start | bytes 884744 | tf_op jit(solution)/shard_map/cond/branch_1_fun/ppermute | solution.py:254
  52.5 0.9 reduce_sum.22
  54.1 7.1 %all-to-all-start.2 = ((bf16[8,64,128]{2,1,0:T(8,128)(2,1)}), bf16[8,64,128]{2,1,0:T(8,128)(2,1)}, u32[]{:S(2)}, u32[]{:S(2)}) async-start(bf16[8,64,128]{2,1,0:T(8,128)(2,1)} %broadcast_in_dim.71), calls=%async_computation.2 | async-start | bytes 262144 | tf_op jit(solution)/shard_map/cond/branch_1_fun/all_to_all | solution.py:204
  61.7 8.7 %all-to-all-done.2 = bf16[8,64,128]{2,1,0:T(8,128)(2,1)} async-done(((bf16[8,64,128]{2,1,0:T(8,128)(2,1)}), bf16[8,64,128]{2,1,0:T(8,128)(2,1)}, u32[]{:S(2)}, u32[]{:S(2)}) %all-to-all-start.2) | async-done | bytes 131104 | tf_op jit(solution)/shard_map/cond/branch_1_fun/all_to_all | solution.py:204
  70.4 0.9 reduce_sum.23
  71.3 0.9 broadcast_in_dim.72
  72.2 6.0 %all-to-all-start.3 = ((bf16[32,64,128]{2,1,0:T(8,128)(2,1)}), bf16[32,64,128]{2,1,0:T(8,128)(2,1)}, u32[]{:S(2)}, u32[]{:S(2)}) async-start(bf16[32,64,128]{2,1,0:T(8,128)(2,1)} %broadcast_in_dim.72), calls=%async_computation.3 | async-start | bytes 1048576 | tf_op jit(solution)/shard_map/cond/branch_1_fun/all_to_all | solution.py:274
  78.2 2.1 %collective-permute-start.3 = (bf16[4,8,144,128]{3,2,1,0:T(8,128)(2,1)S(1)}, bf16[4,8,144,128]{3,2,1,0:T(8,128)(2,1)S(1)}, u32[]{:S(2)}, u32[]{:S(2)}) collective-permute-start(bf16[4,8,144,128]{3,2,1,0:T(8,128)(2,1)S(1)} %constant_dynamic-slice_fusion), channel_id=1, source_target_pairs={{0,1},{1,0},{2,3},{3,2},{4,5},{5,4},{6,7},{7,6},{8,9},{9,8},{10,11... | collective-permute-start | bytes 3538952 | tf_op jit(solution)/shard_map/cond/branch_1_fun/ppermute | solution.py:258
  80.3 2.0 %branch_1_fun.3 = bf16[256,3840]{1,0:T(8,128)(2,1)} custom-call(s32[6,128]{1,0:T(8,128)S(1)} %copy-done.3), custom_call_target="tpu_custom_call" | custom-call | flops 68719476736 | bytes 2097152 | tf_op jit(solution)/shard_map/cond/branch_1_fun/pallas_call | solution.py:259
  82.3 5.4 %branch_1_fun.4 = (bf16[1536,768]{1,0:T(8,128)(2,1)}, bf16[1536,768]{1,0:T(8,128)(2,1)}, bf16[1536,384]{1,0:T(8,128)(2,1)}) custom-call(s32[1]{0:T(128)} %get-tuple-element.28.first_ref, s32[6,128]{1,0:T(8,128)S(1)} %copy-done.3, bf16[1536,384]{1,0:T(8,128)(2,1)S(1)} %copy-done.4), custom_call_target="tpu_custom_call" | custom-call | flops 68719476736 | bytes 6291456 | tf_op jit(solution)/shard_map/cond/branch_1_fun/pallas_call | solution.py:266
  88.1 2.0 %copy.7 = bf16[6,8,4,2,24,128]{5,4,3,2,1,0:T(8,128)(2,1)} copy(bf16[6,8,4,2,24,128]{5,4,0,1,2,3:T(8,128)(2,1)S(1)} %maximum_bitcast_fusion) | data formatting | bytes 4718592 | tf_op jit(solution)/shard_map/cond/branch_1_fun/transpose | solution.py:278
  90.2 6.7 %branch_1_fun.5 = bf16[1536,1536]{1,0:T(8,128)(2,1)} custom-call(s32[1]{0:T(128)} %get-tuple-element.28.first_ref, bf16[6,1536,128]{2,1,0:T(8,128)(2,1)} %bitcast.337, bf16[1536,768]{1,0:T(8,128)(2,1)} %get-tuple-element.36.last_ref, bf16[1536,768]{1,0:T(8,128)(2,1)} %get-tuple-element.37.live_ref), custom_call_target="tpu_custom_call" | custom-call | flops 301989888 | bytes 12582912 | tf_op jit(solution)/shard_map/cond/branch_1_fun/pallas_call | solution.py:279
  96.8 2.6 %collective-permute-start.4 = (bf16[32,64,128]{2,1,0:T(8,128)(2,1)}, bf16[32,64,128]{2,1,0:T(8,128)(2,1)}, u32[]{:S(2)}, u32[]{:S(2)}) collective-permute-start(bf16[32,64,128]{2,1,0:T(8,128)(2,1)} %all-to-all-done.3), channel_id=1, source_target_pairs={{0,1},{1,0},{2,3},{3,2},{4,5},{5,4},{6,7},{7,6},{8,9},{9,8},{10,11... | collective-permute-start | bytes 1572872 | tf_op jit(solution)/shard_map/cond/branch_1_fun/ppermute | solution.py:288
  99.4 1.7 %collective-permute-done.4 = bf16[32,64,128]{2,1,0:T(8,128)(2,1)} collective-permute-done((bf16[32,64,128]{2,1,0:T(8,128)(2,1)}, bf16[32,64,128]{2,1,0:T(8,128)(2,1)}, u32[]{:S(2)}, u32[]{:S(2)}) %collective-permute-start.4) | collective-permute-done | bytes 524320 | tf_op jit(solution)/shard_map/cond/branch_1_fun/ppermute | solution.py:288
  101.1 8.1 %shard_map.47 = bf16[1536,384]{1,0:T(8,128)(2,1)} custom-call(s32[1]{0:T(128)} %bitcast.32.core_ref, bf16[2,768,384]{2,1,0:T(8,128)(2,1)} %all-reduce.2.cloned.1.call-done.content_hbm, bf16[32,64,128]{2,1,0:T(8,128)(2,1)} %get-tuple-element.51.mine_hbm, bf16[32,64,128]{2,1,0:T(8,128)(2,1)} %get-tuple-element.52.other_hbm, f32[6,128,128]{2,1,0:T(8,128)} %inverses_hbm.1, ...), custom_call_target="tpu_custom_call" | custom-call | flops 1811939328 | bytes 16777216 | tf_op jit(solution)/shard_map/pallas_call | solution.py:297
  (69 shorter events, 3.4 us)
Async XLA Ops:
  6.5 4.3 %copy-start.1 = (s32[6,128]{1,0:T(8,128)S(1)}, s32[6,128]{1,0:T(8,128)}, u32[]{:S(2)}) copy-start(s32[6,128]{1,0:T(8,128)} %rows_ref.1) | copy-start | bytes 9220
  6.5 4.3 %copy-start = (bf16[6,24,128]{2,1,0:T(8,128)(2,1)S(1)}, bf16[6,24,128]{2,1,0:T(8,128)(2,1)}, u32[]{:S(2)}) copy-start(bf16[6,24,128]{2,1,0:T(8,128)(2,1)} %param.7) | copy-start | bytes 110596
  6.5 94.5 %all-reduce.2.cloned.1.call-start = ((), (), s32[]{:S(2)}) async-start(), calls=%async_computation.4 | async-start | bytes 2359296 | tf_op jit(solution)/shard_map/psum | solution.py:231
  10.8 12.1 %copy-start.2 = (s32[6,128]{1,0:T(8,128)}, s32[6,128]{1,0:T(8,128)S(1)}, u32[]{:S(2)}) copy-start(s32[6,128]{1,0:T(8,128)S(1)} %get-tuple-element.30.rows_ref) | copy-start | bytes 9220 | tf_op jit(solution)/shard_map/cond
  11.6 22.9 %all-to-all-start = ((bf16[8,144,128]{2,1,0:T(8,128)(2,1)}), bf16[8,144,128]{2,1,0:T(8,128)(2,1)S(1)}, u32[]{:S(2)}, u32[]{:S(2)}) async-start(bf16[8,144,128]{2,1,0:T(8,128)(2,1)} %broadcast_in_dim.68), calls=%async_computation | async-start | bytes 589824 | tf_op jit(solution)/shard_map/cond/branch_1_fun/all_to_all | solution.py:204
  35.8 25.4 %collective-permute-start = (bf16[8,144,128]{2,1,0:T(8,128)(2,1)S(1)}, bf16[8,144,128]{2,1,0:T(8,128)(2,1)S(1)}, u32[]{:S(2)}, u32[]{:S(2)}) collective-permute-start(bf16[8,144,128]{2,1,0:T(8,128)(2,1)S(1)} %all-to-all-done), channel_id=1, source_target_pairs={{2,0},{4,2},{6,4},{0,6},{3,1},{5,3},{7,5},{1,7},{10,8},{12,10},{14... | collective-permute-start | bytes 884744 | tf_op jit(solution)/shard_map/cond/branch_1_fun/ppermute | solution.py:254
  39.4 13.1 %all-to-all-start.1 = ((bf16[8,64,128]{2,1,0:T(8,128)(2,1)}), bf16[8,64,128]{2,1,0:T(8,128)(2,1)}, u32[]{:S(2)}, u32[]{:S(2)}) async-start(bf16[8,64,128]{2,1,0:T(8,128)(2,1)} %select_select_fusion), calls=%async_computation.1 | async-start | bytes 262144 | tf_op jit(solution)/shard_map/cond/branch_1_fun/all_to_all | solution.py:250
  45.7 15.6 %collective-permute-start.2 = (bf16[8,144,128]{2,1,0:T(8,128)(2,1)S(1)}, bf16[8,144,128]{2,1,0:T(8,128)(2,1)S(1)}, u32[]{:S(2)}, u32[]{:S(2)}) collective-permute-start(bf16[8,144,128]{2,1,0:T(8,128)(2,1)S(1)} %all-to-all-done), channel_id=1, source_target_pairs={{6,0},{0,2},{2,4},{4,6},{7,1},{1,3},{3,5},{5,7},{14,8},{8,10},{10,... | collective-permute-start | bytes 884744 | tf_op jit(solution)/shard_map/cond/branch_1_fun/ppermute | solution.py:254
  47.8 13.5 %collective-permute-start.1 = (bf16[8,144,128]{2,1,0:T(8,128)(2,1)S(1)}, bf16[8,144,128]{2,1,0:T(8,128)(2,1)S(1)}, u32[]{:S(2)}, u32[]{:S(2)}) collective-permute-start(bf16[8,144,128]{2,1,0:T(8,128)(2,1)S(1)} %all-to-all-done), channel_id=1, source_target_pairs={{4,0},{6,2},{0,4},{2,6},{5,1},{7,3},{1,5},{3,7},{12,8},{14,10},{8,... | collective-permute-start | bytes 884744 | tf_op jit(solution)/shard_map/cond/branch_1_fun/ppermute | solution.py:254
  54.1 16.3 %all-to-all-start.2 = ((bf16[8,64,128]{2,1,0:T(8,128)(2,1)}), bf16[8,64,128]{2,1,0:T(8,128)(2,1)}, u32[]{:S(2)}, u32[]{:S(2)}) async-start(bf16[8,64,128]{2,1,0:T(8,128)(2,1)} %broadcast_in_dim.71), calls=%async_computation.2 | async-start | bytes 262144 | tf_op jit(solution)/shard_map/cond/branch_1_fun/all_to_all | solution.py:204
  61.5 18.8 %copy-start.3 = (s32[6,128]{1,0:T(8,128)S(1)}, s32[6,128]{1,0:T(8,128)}, u32[]{:S(2)}) copy-start(s32[6,128]{1,0:T(8,128)} %copy-done.2) | copy-start | bytes 9220 | tf_op jit(solution)/shard_map/cond
  72.2 24.6 %all-to-all-start.3 = ((bf16[32,64,128]{2,1,0:T(8,128)(2,1)}), bf16[32,64,128]{2,1,0:T(8,128)(2,1)}, u32[]{:S(2)}, u32[]{:S(2)}) async-start(bf16[32,64,128]{2,1,0:T(8,128)(2,1)} %broadcast_in_dim.72), calls=%async_computation.3 | async-start | bytes 1048576 | tf_op jit(solution)/shard_map/cond/branch_1_fun/all_to_all | solution.py:274
  78.2 4.1 %copy-start.4 = (bf16[1536,384]{1,0:T(8,128)(2,1)S(1)}, bf16[1536,384]{1,0:T(8,128)(2,1)}, u32[]{:S(2)}) copy-start(bf16[1536,384]{1,0:T(8,128)(2,1)} %get-tuple-element.31.matrix_ref) | copy-start | bytes 3538948 | tf_op jit(solution)/shard_map/cond
  78.2 9.5 %collective-permute-start.3 = (bf16[4,8,144,128]{3,2,1,0:T(8,128)(2,1)S(1)}, bf16[4,8,144,128]{3,2,1,0:T(8,128)(2,1)S(1)}, u32[]{:S(2)}, u32[]{:S(2)}) collective-permute-start(bf16[4,8,144,128]{3,2,1,0:T(8,128)(2,1)S(1)} %constant_dynamic-slice_fusion), channel_id=1, source_target_pairs={{0,1},{1,0},{2,3},{3,2},{4,5},{5,4},{6,7},{7,6},{8,9},{9,8},{10,11... | collective-permute-start | bytes 3538952 | tf_op jit(solution)/shard_map/cond/branch_1_fun/ppermute | solution.py:258
  96.8 4.2 %collective-permute-start.4 = (bf16[32,64,128]{2,1,0:T(8,128)(2,1)}, bf16[32,64,128]{2,1,0:T(8,128)(2,1)}, u32[]{:S(2)}, u32[]{:S(2)}) collective-permute-start(bf16[32,64,128]{2,1,0:T(8,128)(2,1)} %all-to-all-done.3), channel_id=1, source_target_pairs={{0,1},{1,0},{2,3},{3,2},{4,5},{5,4},{6,7},{7,6},{8,9},{9,8},{10,11... | collective-permute-start | bytes 1572872 | tf_op jit(solution)/shard_map/cond/branch_1_fun/ppermute | solution.py:288
Sparse Core Ops, SparseCore 0:
  10.9 86.4 all-reduce.1

commit v8 on v7

--- a/solution.py
+++ b/solution.py
@@ -119,7 +119,7 @@
     lax.fori_loop(0, matrix_ref.shape[0] // height, one, 0)
 
 
-def rows_kernel(first_ref, panels_ref, last_ref, live_ref, factor_ref):
+def rows_kernel(first_ref, panels_ref, live_ref, lower_ref):
     height = 2 * NB
 
     def one(step, carry):
@@ -127,18 +127,16 @@
         block = pl.ds(at, height)
         ids = iota((height, NB), 0) + first_ref[0] + at
         for j in range(STEPS):
-            here = 2 * NB * j
-            factor_ref[block, here:here + NB] = last_ref[block, NB * j:NB * (j + 1)]
+            here = slice(NB * j, NB * (j + 1))
             diag = jnp.where((ids - NB * j == iota((height, NB), 1)) & (ids < TOP), 1.0, 0.0).astype(BF)
-            lower = live_ref[block, NB * j:NB * (j + 1)] * panels_ref[j, block, :]
-            factor_ref[block, here + NB:here + 2 * NB] = lower + diag
+            lower_ref[block, here] = live_ref[block, here] * panels_ref[j, block, :] + diag
         return carry
 
     lax.fori_loop(0, panels_ref.shape[1] // height, one, 0)
 
 
-def solve_kernel(core_ref, content_hbm, mine_hbm, other_hbm, inverses_hbm, select_hbm, factor_hbm, kept_hbm, out_hbm,
-                 content, low, inverses, parts, coef, factor, kept, state, out, sems, out_sems):
+def solve_kernel(core_ref, content_hbm, mine_hbm, other_hbm, inverses_hbm, select_hbm, last_hbm, lower_hbm, kept_hbm, out_hbm,
+                 content, low, inverses, parts, coef, last, lower, kept, state, moved, upper, out, sems, out_sems):
     core = core_ref[0]
     height = out.shape[0] // BLOCKS
     copies = [
@@ -149,7 +147,8 @@
             (mine_hbm, low.at[core]),
             (other_hbm, low.at[1 - core]),
             (select_hbm, coef),
-            (factor_hbm, factor),
+            (last_hbm, last),
+            (lower_hbm, lower),
             (kept_hbm, kept),
         ))
     ]
@@ -181,14 +180,18 @@
             x = x + jnp.dot(coef[:, at:at + 2 * NB * k], state[:2 * NB * k, :], preferred_element_type=F32)
         y = x.astype(BF)
         state[2 * NB * k:2 * NB * k + NB, :] = y[:NB]
+        moved[k * NB:(k + 1) * NB, :] = y[:NB]
         u = jnp.dot(parts[k], y[NB:], preferred_element_type=F32)
-        state[2 * NB * k + NB:2 * NB * (k + 1), :] = (u[:NB] + (u[NB:2 * NB] + u[2 * NB:])).astype(BF)
+        u = (u[:NB] + (u[NB:2 * NB] + u[2 * NB:])).astype(BF)
+        state[2 * NB * k + NB:2 * NB * (k + 1), :] = u
+        upper[k * NB:(k + 1) * NB, :] = u
     for copy in copies[5:]:
         copy.wait()
     writes = []
     for b in range(BLOCKS):
         at = b * height
-        new = jnp.dot(factor[at:at + height, :], state[...], preferred_element_type=F32)
+        new = jnp.dot(last[at:at + height, :], moved[...], preferred_element_type=F32)
+        new = new + jnp.dot(lower[at:at + height, :], upper[...], preferred_element_type=F32)
         out[at:at + height, :] = (kept[at:at + height, :].astype(F32) + new).astype(BF)
         writes.append(pltpu.make_async_copy(out.at[at:at + height], out_hbm.at[at:at + height], out_sems.at[b]))
         writes[-1].start()
@@ -249,7 +252,17 @@
         part = jnp.where((idx >= 0)[:, None], part, jnp.zeros((), BF)).reshape(nc * nx, chunk, NB)
         part = lax.all_to_all(part, ("c", "x"), 0, 0, tiled=True)
         part = part.astype(F32).sum(0).astype(BF)
-        part = spread(part, "y", ny).reshape(ny, chunk, NB).astype(F32).sum(0).astype(BF)
+        part, pivots = lax.optimization_barrier((part, pivots))
+        part = spread(part, "y", ny)
+        marked = pl.pallas_call(
+            mark_kernel,
+            out_shape=(jax.ShapeDtypeStruct((local, TOP), BF), jax.ShapeDtypeStruct((local, TOP), BF), jax.ShapeDtypeStruct((local, width), BF)),
+            in_specs=[SM, VM, VM],
+            out_specs=(VM, VM, VM),
+            cost_estimate=cost(4 * TOP * local * NB, 6 << 20),
+        )(first1, pivots, matrix)
+        part, *marked = lax.optimization_barrier((part, *marked))
+        part = part.reshape(ny, chunk, NB).astype(F32).sum(0).astype(BF)
 
         blocks = [column] + [lax.ppermute(column, "x", [((i + s) % nx, i) for i in range(nx)]) for s in range(1, nx)]
         mine = lax.dynamic_slice_in_dim(jnp.stack(blocks + blocks), (nx - x) % nx, nx)
@@ -263,41 +276,33 @@
             out_specs=VM,
             cost_estimate=cost(LONG, 2 << 20),
         )(pivots)
-        marked = pl.pallas_call(
-            mark_kernel,
-            out_shape=(jax.ShapeDtypeStruct((local, TOP), BF), jax.ShapeDtypeStruct((local, TOP), BF), jax.ShapeDtypeStruct((local, width), BF)),
-            in_specs=[SM, VM, VM],
-            out_specs=(VM, VM, VM),
-            cost_estimate=cost(LONG, 6 << 20),
-        )(first1, pivots, matrix)
-        other, select, *marked = lax.optimization_barrier((other, select, *marked))
+        other, select = lax.optimization_barrier((other, select))
         low_mine = lax.all_to_all(part, ("z", "x"), 0, 0, tiled=True)
 
         both = [a.reshape(nx, nz, STEPS, held, NB) for a in (mine, other)]
         both = jnp.stack([jnp.where(core == 0, both[0], both[1]), jnp.where(core == 0, both[1], both[0])])
         full = both.transpose(3, 2, 1, 0, 4, 5).reshape(STEPS, local, NB)
-        factor = pl.pallas_call(
+        lower = pl.pallas_call(
             rows_kernel,
-            out_shape=jax.ShapeDtypeStruct((local, 2 * TOP), BF),
-            in_specs=[SM, VM, VM, VM],
+            out_shape=jax.ShapeDtypeStruct((local, TOP), BF),
+            in_specs=[SM, VM, VM],
             out_specs=VM,
             cost_estimate=cost(2 * TOP * local * NB, 12 << 20),
-        )(first1, full, *marked[:2])
-        kept = marked[2]
-        low_mine, factor = lax.optimization_barrier((low_mine, factor))
-        return low_mine, lax.ppermute(low_mine, "c", swap), factor, kept, select
+        )(first1, full, marked[1])
+        low_mine, lower = lax.optimization_barrier((low_mine, lower))
+        return low_mine, lax.ppermute(low_mine, "c", swap), marked[0], lower, marked[2], select
 
     def nothing(panels, pivots):
         return tuple(jnp.zeros(o.shape, o.dtype) for o in jax.eval_shape(gather, panels, pivots))
 
-    low_mine, low_other, factor, kept, select = lax.cond(y < ny, gather, nothing, panels, pivots)
+    low_mine, low_other, last, lower, kept, select = lax.cond(y < ny, gather, nothing, panels, pivots)
 
     chunk = low_mine.size // (nzx * NB)
     low_shape = (nzx * chunk // CHUNK, CHUNK, NB)
     return pl.pallas_call(
         solve_kernel,
         out_shape=jax.ShapeDtypeStruct((local, width), BF),
-        in_specs=[SM] + [ANY] * 7,
+        in_specs=[SM] + [ANY] * 8,
         out_specs=ANY,
         scratch_shapes=[
             pltpu.VMEM((2, TOP, width), BF),
@@ -305,15 +310,18 @@
             pltpu.VMEM(inverses.shape, F32),
             pltpu.VMEM((STEPS, 3 * NB, NB), BF),
             pltpu.VMEM(select.shape, BF),
-            pltpu.VMEM(factor.shape, BF),
+            pltpu.VMEM(last.shape, BF),
+            pltpu.VMEM(lower.shape, BF),
             pltpu.VMEM((local, width), BF),
             pltpu.VMEM((2 * TOP, width), BF),
+            pltpu.VMEM((TOP, width), BF),
+            pltpu.VMEM((TOP, width), BF),
             pltpu.VMEM((local, width), BF),
-            pltpu.SemaphoreType.DMA((7,)),
+            pltpu.SemaphoreType.DMA((8,)),
             pltpu.SemaphoreType.DMA((BLOCKS,)),
         ],
         cost_estimate=cost(4 * TOP * local * width, 16 << 20),
-    )(core1, content, low_mine.reshape(low_shape), low_other.reshape(low_shape), inverses, select, factor, kept)
+    )(core1, content, low_mine.reshape(low_shape), low_other.reshape(low_shape), inverses, select, last, lower, kept)
 
 
 def solution(mesh):

time: 118 us -> 115 us (0.975)
  Pallas kernels: 26.4 us -> 24.4 us
  starting transfers between devices: 43.8 us -> 42.3 us
    all_to_all x2, waiting for transfers between devices: 20.1 us -> 13.5 us  [spread(): lax.all_to_all(jnp.broadcast_to(x[None], (parts,) + x.shape), axes, 0, 0,...]
    all_to_all x1, waiting for transfers between devices: 0.01 us -> 4.68 us  [gather(): low_mine = lax.all_to_all(part, ('z', 'x'), 0, 0, tiled=True)]
    pallas_call x1, Pallas kernels: 6.67 us -> 3.47 us  [gather(): pl.pallas_call(rows_kernel, out_shape=jax.ShapeDtypeStruct((local, TOP),...]
    all_to_all x1, starting transfers between devices: 6.3 us -> 4.78 us  [gather(): part = lax.all_to_all(part, ('c', 'x'), 0, 0, tiled=True)]
    all_to_all x1, starting transfers between devices: 5.99 us -> 7.43 us  [gather(): low_mine = lax.all_to_all(part, ('z', 'x'), 0, 0, tiled=True)]
    pallas_call x1, Pallas kernels: 5.4 us -> 6.61 us  [gather(): pl.pallas_call(mark_kernel, out_shape=(jax.ShapeDtypeStruct((local, TOP),...]
  transfers between devices with their start and end apart: 10 -> 10, of which waited for: 3 -> 6; matrix products, arithmetic and copies ran while one was open for 9% -> 9% of each run, Pallas kernels for 12% -> 11%
where the time goes in v8:
time: 115 us; the launch traced here: 112 us
  starting transfers between devices  42.3 us (37%)
  Pallas kernels  24.4 us (21%)
  waiting for transfers between devices  21.6 us (19%)
  between operations  13.4 us (12%)
  local copies, waits for them, and re-layouts  6.37 us (6%)
  other arithmetic  4.08 us (4%)
    all_to_all x2, starting transfers between devices, spread(): lax.all_to_all(jnp.broadcast_to(x[None], (parts,) + x.shape), axes, 0, 0,...  17.4 us
    all_to_all x2, waiting for transfers between devices, spread(): lax.all_to_all(jnp.broadcast_to(x[None], (parts,) + x.shape), axes, 0, 0,...  13.5 us
    ppermute x3, starting transfers between devices, gather(): lax.ppermute(column, 'x', [((i + s) % nx, i) for i in range(nx)])  8.65 us
    pallas_call x1, Pallas kernels, per_device(): pl.pallas_call(solve_kernel, out_shape=jax.ShapeDtypeStruct((local, width...  8.16 us
    all_to_all x1, starting transfers between devices, gather(): low_mine = lax.all_to_all(part, ('z', 'x'), 0, 0, tiled=True)  7.43 us
    pallas_call x1, Pallas kernels, gather(): pl.pallas_call(mark_kernel, out_shape=(jax.ShapeDtypeStruct((local, TOP),...  6.61 us
    all_to_all x1, starting transfers between devices, gather(): part = lax.all_to_all(part, ('c', 'x'), 0, 0, tiled=True)  4.78 us
    all_to_all x1, waiting for transfers between devices, gather(): low_mine = lax.all_to_all(part, ('z', 'x'), 0, 0, tiled=True)  4.68 us
  transfers between devices with their start and end apart: 10, of which 6 were waited for; matrix products, arithmetic and copies ran while one was open for 9% of the time, Pallas kernels for 11%

profile of v8, /device:TPU:6, one launch (start us, length us, event | category | flops | bytes accessed | tf_op | source)
XLA Modules:
  0.0 112.5 jit_solution(14764703605982096984)
XLA Ops:
  6.5 4.2 %shard_map.46 = bf16[2,768,384]{2,1,0:T(8,128)(2,1)} custom-call(s32[1]{0:T(128)} %bitcast.33.first_ref, s32[6,128]{1,0:T(8,128)} %rows_ref.1, bf16[1536,384]{1,0:T(8,128)(2,1)} %matrix_hbm.1), custom_call_target="tpu_custom_call" | custom-call | flops 905969664 | bytes 4194304 | tf_op jit(solution)/shard_map/pallas_call | solution.py:221
  10.8 86.1 %conditional.1 = (bf16[32,64,128]{2,1,0:T(8,128)(2,1)}, bf16[32,64,128]{2,1,0:T(8,128)(2,1)}, bf16[1536,768]{1,0:T(8,128)(2,1)}, bf16[1536,768]{1,0:T(8,128)(2,1...) conditional(s32[]{:T(128)} %convert_element_type.2, () %tuple.19, (s32[6,128]{1,0:T(8,128)S(1)}, ...), branch_computations={%region_1.0_spmd, %region_2.5_spmd} | conditional | flops 69628207104 | bytes 57746280 | solution.py:298
  11.6 10.3 %all-to-all-start = ((bf16[8,144,128]{2,1,0:T(8,128)(2,1)}), bf16[8,144,128]{2,1,0:T(8,128)(2,1)S(1)}, u32[]{:S(2)}, u32[]{:S(2)}) async-start(bf16[8,144,128]{2,1,0:T(8,128)(2,1)} %broadcast_in_dim.68), calls=%async_computation | async-start | bytes 589824 | tf_op jit(solution)/shard_map/cond/branch_1_fun/all_to_all | solution.py:207
  23.1 11.4 %all-to-all-done = bf16[8,144,128]{2,1,0:T(8,128)(2,1)S(1)} async-done(((bf16[8,144,128]{2,1,0:T(8,128)(2,1)}), bf16[8,144,128]{2,1,0:T(8,128)(2,1)S(1)}, u32[]{:S(2)}, u32[]{:S(2)}) %all-to-all-start) | async-done | bytes 294944 | tf_op jit(solution)/shard_map/cond/branch_1_fun/all_to_all | solution.py:207
  34.5 1.3 %gather_fusion = bf16[512,128]{1,0:T(8,128)(2,1)S(1)} fusion(bf16[1152,128]{1,0:T(8,128)(2,1)S(1)} %bitcast.336, s32[1024]{0:T(1024)S(1)} %pad_clamp_fusion), kind=kCustom, calls=%fused_computation | custom fusion | bytes 264192 | tf_op jit(solution)/shard_map/cond/branch_1_fun/jit(_take)/gather | solution.py:251
  36.7 4.8 %all-to-all-start.1 = ((bf16[8,64,128]{2,1,0:T(8,128)(2,1)}), bf16[8,64,128]{2,1,0:T(8,128)(2,1)}, u32[]{:S(2)}, u32[]{:S(2)}) async-start(bf16[8,64,128]{2,1,0:T(8,128)(2,1)} %select_select_fusion), calls=%async_computation.1 | async-start | bytes 262144 | tf_op jit(solution)/shard_map/cond/branch_1_fun/all_to_all | solution.py:253
  41.5 1.9 %collective-permute-start.2 = (bf16[8,144,128]{2,1,0:T(8,128)(2,1)S(1)}, bf16[8,144,128]{2,1,0:T(8,128)(2,1)S(1)}, u32[]{:S(2)}, u32[]{:S(2)}) collective-permute-start(bf16[8,144,128]{2,1,0:T(8,128)(2,1)S(1)} %all-to-all-done), channel_id=1, source_target_pairs={{6,0},{0,2},{2,4},{4,6},{7,1},{1,3},{3,5},{5,7},{14,8},{8,10},{10,... | collective-permute-start | bytes 884744 | tf_op jit(solution)/shard_map/cond/branch_1_fun/ppermute | solution.py:267
  43.4 4.8 %collective-permute-start.1 = (bf16[8,144,128]{2,1,0:T(8,128)(2,1)S(1)}, bf16[8,144,128]{2,1,0:T(8,128)(2,1)S(1)}, u32[]{:S(2)}, u32[]{:S(2)}) collective-permute-start(bf16[8,144,128]{2,1,0:T(8,128)(2,1)S(1)} %all-to-all-done), channel_id=1, source_target_pairs={{4,0},{6,2},{0,4},{2,6},{5,1},{7,3},{1,5},{3,7},{12,8},{14,10},{8,... | collective-permute-start | bytes 884744 | tf_op jit(solution)/shard_map/cond/branch_1_fun/ppermute | solution.py:267
  48.2 1.9 %collective-permute-start = (bf16[8,144,128]{2,1,0:T(8,128)(2,1)S(1)}, bf16[8,144,128]{2,1,0:T(8,128)(2,1)S(1)}, u32[]{:S(2)}, u32[]{:S(2)}) collective-permute-start(bf16[8,144,128]{2,1,0:T(8,128)(2,1)S(1)} %all-to-all-done), channel_id=1, source_target_pairs={{2,0},{4,2},{6,4},{0,6},{3,1},{5,3},{7,5},{1,7},{10,8},{12,10},{14... | collective-permute-start | bytes 884744 | tf_op jit(solution)/shard_map/cond/branch_1_fun/ppermute | solution.py:267
  50.2 0.9 reduce_sum.22
  51.8 7.1 %all-to-all-start.2 = ((bf16[8,64,128]{2,1,0:T(8,128)(2,1)}), bf16[8,64,128]{2,1,0:T(8,128)(2,1)}, u32[]{:S(2)}, u32[]{:S(2)}) async-start(bf16[8,64,128]{2,1,0:T(8,128)(2,1)} %broadcast_in_dim.71), calls=%async_computation.2 | async-start | bytes 262144 | tf_op jit(solution)/shard_map/cond/branch_1_fun/all_to_all | solution.py:207
  58.9 6.6 %branch_1_fun.3 = (bf16[1536,768]{1,0:T(8,128)(2,1)}, bf16[1536,768]{1,0:T(8,128)(2,1)}, bf16[1536,384]{1,0:T(8,128)(2,1)}) custom-call(s32[1]{0:T(128)} %get-tuple-element.28.first_ref, s32[6,128]{1,0:T(8,128)} %copy-done.2, bf16[1536,384]{1,0:T(8,128)(2,1)} %get-tuple-element.30.matrix_ref), custom_call_target="tpu_custom_call" | custom-call | flops 603979776 | bytes 6291456 | tf_op jit(solution)/shard_map/cond/branch_1_fun/pallas_call | solution.py:257
  66.0 2.1 %all-to-all-done.2 = bf16[8,64,128]{2,1,0:T(8,128)(2,1)} async-done(((bf16[8,64,128]{2,1,0:T(8,128)(2,1)}), bf16[8,64,128]{2,1,0:T(8,128)(2,1)}, u32[]{:S(2)}, u32[]{:S(2)}) %all-to-all-start.2) | async-done | bytes 131104 | tf_op jit(solution)/shard_map/cond/branch_1_fun/all_to_all | solution.py:207
  68.1 0.9 reduce_sum.23
  69.0 0.9 broadcast_in_dim.72
  69.9 7.4 %all-to-all-start.3 = ((bf16[32,64,128]{2,1,0:T(8,128)(2,1)}), bf16[32,64,128]{2,1,0:T(8,128)(2,1)}, u32[]{:S(2)}, u32[]{:S(2)}) async-start(bf16[32,64,128]{2,1,0:T(8,128)(2,1)} %broadcast_in_dim.72), calls=%async_computation.3 | async-start | bytes 1048576 | tf_op jit(solution)/shard_map/cond/branch_1_fun/all_to_all | solution.py:280
  77.4 1.9 %collective-permute-start.3 = (bf16[4,8,144,128]{3,2,1,0:T(8,128)(2,1)S(1)}, bf16[4,8,144,128]{3,2,1,0:T(8,128)(2,1)S(1)}, u32[]{:S(2)}, u32[]{:S(2)}) collective-permute-start(bf16[4,8,144,128]{3,2,1,0:T(8,128)(2,1)S(1)} %constant_dynamic-slice_fusion), channel_id=1, source_target_pairs={{0,1},{1,0},{2,3},{3,2},{4,5},{5,4},{6,7},{7,6},{8,9},{9,8},{10,11... | collective-permute-start | bytes 3538952 | tf_op jit(solution)/shard_map/cond/branch_1_fun/ppermute | solution.py:271
  79.3 2.0 %branch_1_fun.4 = bf16[256,3840]{1,0:T(8,128)(2,1)} custom-call(s32[6,128]{1,0:T(8,128)S(1)} %copy-done.3), custom_call_target="tpu_custom_call" | custom-call | flops 68719476736 | bytes 2097152 | tf_op jit(solution)/shard_map/cond/branch_1_fun/pallas_call | solution.py:272
  82.5 2.1 %copy.6 = bf16[6,8,4,2,24,128]{5,4,3,2,1,0:T(8,128)(2,1)} copy(bf16[6,8,4,2,24,128]{5,4,0,1,2,3:T(8,128)(2,1)S(1)} %maximum_bitcast_fusion) | data formatting | bytes 4718592 | tf_op jit(solution)/shard_map/cond/branch_1_fun/transpose | solution.py:284
  84.6 3.5 %branch_1_fun.5 = bf16[1536,768]{1,0:T(8,128)(2,1)S(1)} custom-call(s32[1]{0:T(128)} %get-tuple-element.28.first_ref, bf16[6,1536,128]{2,1,0:T(8,128)(2,1)} %bitcast.337, bf16[1536,768]{1,0:T(8,128)(2,1)} %get-tuple-element.39.live_ref), custom_call_target="tpu_custom_call" | custom-call | flops 301989888 | bytes 12582912 | tf_op jit(solution)/shard_map/cond/branch_1_fun/pallas_call | solution.py:285
  88.1 4.7 %all-to-all-done.3 = bf16[32,64,128]{2,1,0:T(8,128)(2,1)} async-done(((bf16[32,64,128]{2,1,0:T(8,128)(2,1)}), bf16[32,64,128]{2,1,0:T(8,128)(2,1)}, u32[]{:S(2)}, u32[]{:S(2)}) %all-to-all-start.3) | async-done | bytes 524320 | tf_op jit(solution)/shard_map/cond/branch_1_fun/all_to_all | solution.py:280
  92.7 2.1 %collective-permute-start.4 = (bf16[32,64,128]{2,1,0:T(8,128)(2,1)}, bf16[32,64,128]{2,1,0:T(8,128)(2,1)}, u32[]{:S(2)}, u32[]{:S(2)}) collective-permute-start(bf16[32,64,128]{2,1,0:T(8,128)(2,1)} %all-to-all-done.3), channel_id=1, source_target_pairs={{0,1},{1,0},{2,3},{3,2},{4,5},{5,4},{6,7},{7,6},{8,9},{9,8},{10,11... | collective-permute-start | bytes 1572872 | tf_op jit(solution)/shard_map/cond/branch_1_fun/ppermute | solution.py:293
  94.8 2.0 %collective-permute-done.4 = bf16[32,64,128]{2,1,0:T(8,128)(2,1)} collective-permute-done((bf16[32,64,128]{2,1,0:T(8,128)(2,1)}, bf16[32,64,128]{2,1,0:T(8,128)(2,1)}, u32[]{:S(2)}, u32[]{:S(2)}) %collective-permute-start.4) | collective-permute-done | bytes 524320 | tf_op jit(solution)/shard_map/cond/branch_1_fun/ppermute | solution.py:293
  97.5 8.2 %shard_map.47 = bf16[1536,384]{1,0:T(8,128)(2,1)} custom-call(s32[1]{0:T(128)} %bitcast.32.core_ref, bf16[2,768,384]{2,1,0:T(8,128)(2,1)} %all-reduce.2.cloned.1.call-done.content_hbm, bf16[32,64,128]{2,1,0:T(8,128)(2,1)} %get-tuple-element.55.mine_hbm, bf16[32,64,128]{2,1,0:T(8,128)(2,1)} %get-tuple-element.56.other_hbm, f32[6,128,128]{2,1,0:T(8,128)} %inverses_hbm.1, ...), custom_call_target="tpu_custom_call" | custom-call | flops 1811939328 | bytes 16777216 | tf_op jit(solution)/shard_map/pallas_call | solution.py:302
  (67 shorter events, 5.7 us)
Async XLA Ops:
  6.5 4.3 %copy-start.1 = (s32[6,128]{1,0:T(8,128)S(1)}, s32[6,128]{1,0:T(8,128)}, u32[]{:S(2)}) copy-start(s32[6,128]{1,0:T(8,128)} %rows_ref.1) | copy-start | bytes 9220
  6.5 4.3 %copy-start = (bf16[6,24,128]{2,1,0:T(8,128)(2,1)S(1)}, bf16[6,24,128]{2,1,0:T(8,128)(2,1)}, u32[]{:S(2)}) copy-start(bf16[6,24,128]{2,1,0:T(8,128)(2,1)} %param.7) | copy-start | bytes 110596
  6.5 90.9 %all-reduce.2.cloned.1.call-start = ((), (), s32[]{:S(2)}) async-start(), calls=%async_computation.4 | async-start | bytes 2359296 | tf_op jit(solution)/shard_map/psum | solution.py:234
  10.8 37.4 %copy-start.2 = (s32[6,128]{1,0:T(8,128)}, s32[6,128]{1,0:T(8,128)S(1)}, u32[]{:S(2)}) copy-start(s32[6,128]{1,0:T(8,128)S(1)} %get-tuple-element.37.rows_ref) | copy-start | bytes 9220 | tf_op jit(solution)/shard_map/cond
  11.6 22.9 %all-to-all-start = ((bf16[8,144,128]{2,1,0:T(8,128)(2,1)}), bf16[8,144,128]{2,1,0:T(8,128)(2,1)S(1)}, u32[]{:S(2)}, u32[]{:S(2)}) async-start(bf16[8,144,128]{2,1,0:T(8,128)(2,1)} %broadcast_in_dim.68), calls=%async_computation | async-start | bytes 589824 | tf_op jit(solution)/shard_map/cond/branch_1_fun/all_to_all | solution.py:207
  36.7 13.5 %all-to-all-start.1 = ((bf16[8,64,128]{2,1,0:T(8,128)(2,1)}), bf16[8,64,128]{2,1,0:T(8,128)(2,1)}, u32[]{:S(2)}, u32[]{:S(2)}) async-start(bf16[8,64,128]{2,1,0:T(8,128)(2,1)} %select_select_fusion), calls=%async_computation.1 | async-start | bytes 262144 | tf_op jit(solution)/shard_map/cond/branch_1_fun/all_to_all | solution.py:253
  41.5 24.2 %collective-permute-start.2 = (bf16[8,144,128]{2,1,0:T(8,128)(2,1)S(1)}, bf16[8,144,128]{2,1,0:T(8,128)(2,1)S(1)}, u32[]{:S(2)}, u32[]{:S(2)}) collective-permute-start(bf16[8,144,128]{2,1,0:T(8,128)(2,1)S(1)} %all-to-all-done), channel_id=1, source_target_pairs={{6,0},{0,2},{2,4},{4,6},{7,1},{1,3},{3,5},{5,7},{14,8},{8,10},{10,... | collective-permute-start | bytes 884744 | tf_op jit(solution)/shard_map/cond/branch_1_fun/ppermute | solution.py:267
  43.4 22.2 %collective-permute-start.1 = (bf16[8,144,128]{2,1,0:T(8,128)(2,1)S(1)}, bf16[8,144,128]{2,1,0:T(8,128)(2,1)S(1)}, u32[]{:S(2)}, u32[]{:S(2)}) collective-permute-start(bf16[8,144,128]{2,1,0:T(8,128)(2,1)S(1)} %all-to-all-done), channel_id=1, source_target_pairs={{4,0},{6,2},{0,4},{2,6},{5,1},{7,3},{1,5},{3,7},{12,8},{14,10},{8,... | collective-permute-start | bytes 884744 | tf_op jit(solution)/shard_map/cond/branch_1_fun/ppermute | solution.py:267
  48.2 17.3 %collective-permute-start = (bf16[8,144,128]{2,1,0:T(8,128)(2,1)S(1)}, bf16[8,144,128]{2,1,0:T(8,128)(2,1)S(1)}, u32[]{:S(2)}, u32[]{:S(2)}) collective-permute-start(bf16[8,144,128]{2,1,0:T(8,128)(2,1)S(1)} %all-to-all-done), channel_id=1, source_target_pairs={{2,0},{4,2},{6,4},{0,6},{3,1},{5,3},{7,5},{1,7},{10,8},{12,10},{14... | collective-permute-start | bytes 884744 | tf_op jit(solution)/shard_map/cond/branch_1_fun/ppermute | solution.py:267
  51.8 16.3 %all-to-all-start.2 = ((bf16[8,64,128]{2,1,0:T(8,128)(2,1)}), bf16[8,64,128]{2,1,0:T(8,128)(2,1)}, u32[]{:S(2)}, u32[]{:S(2)}) async-start(bf16[8,64,128]{2,1,0:T(8,128)(2,1)} %broadcast_in_dim.71), calls=%async_computation.2 | async-start | bytes 262144 | tf_op jit(solution)/shard_map/cond/branch_1_fun/all_to_all | solution.py:207
  65.8 13.5 %copy-start.3 = (s32[6,128]{1,0:T(8,128)S(1)}, s32[6,128]{1,0:T(8,128)}, u32[]{:S(2)}) copy-start(s32[6,128]{1,0:T(8,128)} %copy-done.2) | copy-start | bytes 9220 | tf_op jit(solution)/shard_map/cond
  69.9 22.8 %all-to-all-start.3 = ((bf16[32,64,128]{2,1,0:T(8,128)(2,1)}), bf16[32,64,128]{2,1,0:T(8,128)(2,1)}, u32[]{:S(2)}, u32[]{:S(2)}) async-start(bf16[32,64,128]{2,1,0:T(8,128)(2,1)} %broadcast_in_dim.72), calls=%async_computation.3 | async-start | bytes 1048576 | tf_op jit(solution)/shard_map/cond/branch_1_fun/all_to_all | solution.py:280
  77.4 4.7 %collective-permute-start.3 = (bf16[4,8,144,128]{3,2,1,0:T(8,128)(2,1)S(1)}, bf16[4,8,144,128]{3,2,1,0:T(8,128)(2,1)S(1)}, u32[]{:S(2)}, u32[]{:S(2)}) collective-permute-start(bf16[4,8,144,128]{3,2,1,0:T(8,128)(2,1)S(1)} %constant_dynamic-slice_fusion), channel_id=1, source_target_pairs={{0,1},{1,0},{2,3},{3,2},{4,5},{5,4},{6,7},{7,6},{8,9},{9,8},{10,11... | collective-permute-start | bytes 3538952 | tf_op jit(solution)/shard_map/cond/branch_1_fun/ppermute | solution.py:271
  92.7 4.1 %collective-permute-start.4 = (bf16[32,64,128]{2,1,0:T(8,128)(2,1)}, bf16[32,64,128]{2,1,0:T(8,128)(2,1)}, u32[]{:S(2)}, u32[]{:S(2)}) collective-permute-start(bf16[32,64,128]{2,1,0:T(8,128)(2,1)} %all-to-all-done.3), channel_id=1, source_target_pairs={{0,1},{1,0},{2,3},{3,2},{4,5},{5,4},{6,7},{7,6},{8,9},{9,8},{10,11... | collective-permute-start | bytes 1572872 | tf_op jit(solution)/shard_map/cond/branch_1_fun/ppermute | solution.py:293
Sparse Core Ops, SparseCore 0:
  10.9 86.5 all-reduce.1

commit v9 on v8

--- a/solution.py
+++ b/solution.py
@@ -99,24 +99,17 @@
 
 
 def mark_kernel(first_ref, rows_ref, matrix_ref, last_ref, live_ref, kept_ref):
-    height = 2 * NB
-
-    def one(step, carry):
-        at = pl.multiple_of(step * height, height)
-        ids = iota((height, NB), 0) + first_ref[0] + at
-        is_top = ids < TOP
-        same = [jnp.where((ids == rows_ref[j:j + 1, :]) & ~is_top, 1.0, 0.0).astype(F32) for j in range(STEPS)]
-        state, fresh = last_match(same)
-        for j, (last, live) in enumerate(state):
-            last_ref[pl.ds(at, height), NB * j:NB * (j + 1)] = last.astype(BF)
-            live_ref[pl.ds(at, height), NB * j:NB * (j + 1)] = jnp.where(is_top, 0.0, -live).astype(BF)
-        fresh = fresh & ~is_top
-        for c in range(0, matrix_ref.shape[1], NB):
-            old = matrix_ref[pl.ds(at, height), c:c + NB].astype(F32)
-            kept_ref[pl.ds(at, height), c:c + NB] = jnp.where(fresh, old, 0.0).astype(BF)
-        return carry
-
-    lax.fori_loop(0, matrix_ref.shape[0] // height, one, 0)
+    height = matrix_ref.shape[0]
+    ids = iota((height, NB), 0) + first_ref[0] + pl.program_id(0) * height
+    is_top = ids < TOP
+    same = [jnp.where((ids == rows_ref[j:j + 1, :]) & ~is_top, 1.0, 0.0).astype(F32) for j in range(STEPS)]
+    state, fresh = last_match(same)
+    for j, (last, live) in enumerate(state):
+        last_ref[:, NB * j:NB * (j + 1)] = last.astype(BF)
+        live_ref[:, NB * j:NB * (j + 1)] = jnp.where(is_top, 0.0, -live).astype(BF)
+    fresh = fresh & ~is_top
+    for c in range(0, matrix_ref.shape[1], NB):
+        kept_ref[:, c:c + NB] = jnp.where(fresh, matrix_ref[:, c:c + NB].astype(F32), 0.0).astype(BF)
 
 
 def rows_kernel(first_ref, panels_ref, live_ref, lower_ref):
@@ -252,19 +245,22 @@
         part = jnp.where((idx >= 0)[:, None], part, jnp.zeros((), BF)).reshape(nc * nx, chunk, NB)
         part = lax.all_to_all(part, ("c", "x"), 0, 0, tiled=True)
         part = part.astype(F32).sum(0).astype(BF)
-        part, pivots = lax.optimization_barrier((part, pivots))
+        part, pivots, late = lax.optimization_barrier((part, pivots, column))
         part = spread(part, "y", ny)
         marked = pl.pallas_call(
             mark_kernel,
             out_shape=(jax.ShapeDtypeStruct((local, TOP), BF), jax.ShapeDtypeStruct((local, TOP), BF), jax.ShapeDtypeStruct((local, width), BF)),
-            in_specs=[SM, VM, VM],
-            out_specs=(VM, VM, VM),
+            grid=(local // (2 * NB),),
+            in_specs=[SM, pl.BlockSpec((STEPS, NB), lambda i: (0, 0)), pl.BlockSpec((2 * NB, width), lambda i: (i, 0))],
+            out_specs=tuple(pl.BlockSpec((2 * NB, n), lambda i: (i, 0)) for n in (TOP, TOP, width)),
             cost_estimate=cost(4 * TOP * local * NB, 6 << 20),
         )(first1, pivots, matrix)
         part, *marked = lax.optimization_barrier((part, *marked))
         part = part.reshape(ny, chunk, NB).astype(F32).sum(0).astype(BF)
 
-        blocks = [column] + [lax.ppermute(column, "x", [((i + s) % nx, i) for i in range(nx)]) for s in range(1, nx)]
+        blocks = [column] + [
+            lax.ppermute(late if s % 2 else column, "x", [((i + s) % nx, i) for i in range(nx)]) for s in range(1, nx)
+        ]
         mine = lax.dynamic_slice_in_dim(jnp.stack(blocks + blocks), (nx - x) % nx, nx)
         part = jnp.broadcast_to(part[None], (nzx, chunk, NB))
         part, mine, pivots = lax.optimization_barrier((part, mine, pivots))

time: 115 us -> 115 us (level); the launches traced: 112 us -> 114 us
  waiting for transfers between devices: 21.6 us -> 23.5 us
    psum x1, waiting for transfers between devices: 0.57 us -> 4.32 us  [per_device(): content = lax.psum(share, 'y')]
    all_to_all x2, waiting for transfers between devices: 13.5 us -> 11.4 us  [spread(): lax.all_to_all(jnp.broadcast_to(x[None], (parts,) + x.shape), axes, 0, 0,...]
    ppermute x3, starting transfers between devices: 8.65 us -> 10.4 us  [gather(): lax.ppermute(late if s % 2 else column, 'x', [((i + s) % nx, i) for i in...]
    all_to_all x1, starting transfers between devices: 7.43 us -> 5.83 us  [gather(): low_mine = lax.all_to_all(part, ('z', 'x'), 0, 0, tiled=True)]
  transfers between devices with their start and end apart: 10 -> 10, of which waited for: 6 -> 6; matrix products, arithmetic and copies ran while one was open for 9% -> 8% of each run, Pallas kernels for 11% -> 11%
where the time goes in v9:
time: 115 us; the launch traced here: 114 us
  starting transfers between devices  42.4 us (37%)
  Pallas kernels  24.9 us (22%)
  waiting for transfers between devices  23.5 us (20%)
  between operations  13.4 us (12%)
  local copies, waits for them, and re-layouts  6.33 us (6%)
  other arithmetic  3.16 us (3%)
    all_to_all x2, starting transfers between devices, spread(): lax.all_to_all(jnp.broadcast_to(x[None], (parts,) + x.shape), axes, 0, 0,...  17.4 us
    all_to_all x2, waiting for transfers between devices, spread(): lax.all_to_all(jnp.broadcast_to(x[None], (parts,) + x.shape), axes, 0, 0,...  11.4 us
    ppermute x3, starting transfers between devices, gather(): lax.ppermute(late if s % 2 else column, 'x', [((i + s) % nx, i) for i in...  10.4 us
    pallas_call x1, Pallas kernels, per_device(): pl.pallas_call(solve_kernel, out_shape=jax.ShapeDtypeStruct((local, width...  8.15 us
    pallas_call x1, Pallas kernels, gather(): pl.pallas_call(mark_kernel, out_shape=(jax.ShapeDtypeStruct((local, TOP),...  6.49 us
    all_to_all x1, starting transfers between devices, gather(): low_mine = lax.all_to_all(part, ('z', 'x'), 0, 0, tiled=True)  5.83 us
    all_to_all x1, waiting for transfers between devices, gather(): low_mine = lax.all_to_all(part, ('z', 'x'), 0, 0, tiled=True)  4.88 us
    all_to_all x1, starting transfers between devices, gather(): part = lax.all_to_all(part, ('c', 'x'), 0, 0, tiled=True)  4.78 us
  transfers between devices with their start and end apart: 10, of which 6 were waited for; matrix products, arithmetic and copies ran while one was open for 8% of the time, Pallas kernels for 11%

profile of v9, /device:TPU:6, one launch (start us, length us, event | category | flops | bytes accessed | tf_op | source)
XLA Modules:
  0.0 114.1 jit_solution(7052249969883410054)
XLA Ops:
  6.5 4.2 %shard_map.46 = bf16[2,768,384]{2,1,0:T(8,128)(2,1)} custom-call(s32[1]{0:T(128)} %bitcast.33.first_ref, s32[6,128]{1,0:T(8,128)} %rows_ref.1, bf16[1536,384]{1,0:T(8,128)(2,1)} %matrix_hbm.1), custom_call_target="tpu_custom_call" | custom-call | flops 905969664 | bytes 4194304 | tf_op jit(solution)/shard_map/pallas_call | solution.py:214
  10.8 83.9 %conditional.1 = (bf16[32,64,128]{2,1,0:T(8,128)(2,1)}, bf16[32,64,128]{2,1,0:T(8,128)(2,1)}, bf16[1536,768]{1,0:T(8,128)(2,1)}, bf16[1536,768]{1,0:T(8,128)(2,1...) conditional(s32[]{:T(128)} %convert_element_type.2, () %tuple.19, (s32[6,128]{1,0:T(8,128)S(1)}, ...), branch_computations={%region_1.0_spmd, %region_2.5_spmd} | conditional | flops 69628207104 | bytes 57733964 | solution.py:294
  11.6 10.3 %all-to-all-start = ((bf16[8,144,128]{2,1,0:T(8,128)(2,1)}), bf16[8,144,128]{2,1,0:T(8,128)(2,1)S(1)}, u32[]{:S(2)}, u32[]{:S(2)}) async-start(bf16[8,144,128]{2,1,0:T(8,128)(2,1)} %broadcast_in_dim.68), calls=%async_computation | async-start | bytes 589824 | tf_op jit(solution)/shard_map/cond/branch_1_fun/all_to_all | solution.py:200
  23.1 11.4 %all-to-all-done = bf16[8,144,128]{2,1,0:T(8,128)(2,1)S(1)} async-done(((bf16[8,144,128]{2,1,0:T(8,128)(2,1)}), bf16[8,144,128]{2,1,0:T(8,128)(2,1)S(1)}, u32[]{:S(2)}, u32[]{:S(2)}) %all-to-all-start) | async-done | bytes 294944 | tf_op jit(solution)/shard_map/cond/branch_1_fun/all_to_all | solution.py:200
  34.5 1.3 %gather_fusion = bf16[512,128]{1,0:T(8,128)(2,1)S(1)} fusion(bf16[1152,128]{1,0:T(8,128)(2,1)S(1)} %bitcast.336, s32[1024]{0:T(1024)S(1)} %pad_clamp_fusion), kind=kCustom, calls=%fused_computation | custom fusion | bytes 264192 | tf_op jit(solution)/shard_map/cond/branch_1_fun/jit(_take)/gather | solution.py:244
  35.8 0.8 select_select_fusion
  36.6 4.8 %all-to-all-start.1 = ((bf16[8,64,128]{2,1,0:T(8,128)(2,1)}), bf16[8,64,128]{2,1,0:T(8,128)(2,1)S(1)}, u32[]{:S(2)}, u32[]{:S(2)}) async-start(bf16[8,64,128]{2,1,0:T(8,128)(2,1)} %select_select_fusion), calls=%async_computation.1 | async-start | bytes 262144 | tf_op jit(solution)/shard_map/cond/branch_1_fun/all_to_all | solution.py:246
  41.4 3.4 %collective-permute-start.1 = (bf16[8,144,128]{2,1,0:T(8,128)(2,1)S(1)}, bf16[8,144,128]{2,1,0:T(8,128)(2,1)S(1)}, u32[]{:S(2)}, u32[]{:S(2)}) collective-permute-start(bf16[8,144,128]{2,1,0:T(8,128)(2,1)S(1)} %all-to-all-done), channel_id=1, source_target_pairs={{4,0},{6,2},{0,4},{2,6},{5,1},{7,3},{1,5},{3,7},{12,8},{14,10},{8,... | collective-permute-start | bytes 884744 | tf_op jit(solution)/shard_map/cond/branch_1_fun/ppermute | solution.py:262
  46.2 7.1 %all-to-all-start.2 = ((bf16[8,64,128]{2,1,0:T(8,128)(2,1)}), bf16[8,64,128]{2,1,0:T(8,128)(2,1)}, u32[]{:S(2)}, u32[]{:S(2)}) async-start(bf16[8,64,128]{2,1,0:T(8,128)(2,1)} %broadcast_in_dim.71), calls=%async_computation.2 | async-start | bytes 262144 | tf_op jit(solution)/shard_map/cond/branch_1_fun/all_to_all | solution.py:200
  53.3 1.9 %collective-permute-start = (bf16[8,144,128]{2,1,0:T(8,128)(2,1)S(1)}, bf16[8,144,128]{2,1,0:T(8,128)(2,1)S(1)}, u32[]{:S(2)}, u32[]{:S(2)}) collective-permute-start(bf16[8,144,128]{2,1,0:T(8,128)(2,1)S(1)} %all-to-all-done), channel_id=1, source_target_pairs={{2,0},{4,2},{6,4},{0,6},{3,1},{5,3},{7,5},{1,7},{10,8},{12,10},{14... | collective-permute-start | bytes 884744 | tf_op jit(solution)/shard_map/cond/branch_1_fun/ppermute | solution.py:262
  55.2 5.1 %collective-permute-start.2 = (bf16[8,144,128]{2,1,0:T(8,128)(2,1)S(1)}, bf16[8,144,128]{2,1,0:T(8,128)(2,1)S(1)}, u32[]{:S(2)}, u32[]{:S(2)}) collective-permute-start(bf16[8,144,128]{2,1,0:T(8,128)(2,1)S(1)} %all-to-all-done), channel_id=1, source_target_pairs={{6,0},{0,2},{2,4},{4,6},{7,1},{1,3},{3,5},{5,7},{14,8},{8,10},{10,... | collective-permute-start | bytes 884744 | tf_op jit(solution)/shard_map/cond/branch_1_fun/ppermute | solution.py:262
  60.4 6.5 %branch_1_fun.3 = (bf16[1536,768]{1,0:T(8,128)(2,1)}, bf16[1536,768]{1,0:T(8,128)(2,1)}, bf16[1536,384]{1,0:T(8,128)(2,1)}) custom-call(s32[1]{0:T(128)} %get-tuple-element.28.first_ref, s32[6,128]{1,0:T(8,128)S(1)} %get-tuple-element.38.rows_ref, bf16[1536,384]{1,0:T(8,128)(2,1)} %get-tuple-element.30.matrix_ref), custom_call_target="tpu_custom_call" | custom-call | flops 603979776 | bytes 6291456 | tf_op jit(solution)/shard_map/cond/branch_1_fun/pallas_call | solution.py:250
  66.9 0.9 reduce_sum.23
  68.3 0.9 broadcast_in_dim.72
  69.2 5.8 %all-to-all-start.3 = ((bf16[32,64,128]{2,1,0:T(8,128)(2,1)}), bf16[32,64,128]{2,1,0:T(8,128)(2,1)}, u32[]{:S(2)}, u32[]{:S(2)}) async-start(bf16[32,64,128]{2,1,0:T(8,128)(2,1)} %broadcast_in_dim.72), calls=%async_computation.3 | async-start | bytes 1048576 | tf_op jit(solution)/shard_map/cond/branch_1_fun/all_to_all | solution.py:276
  75.0 1.9 %collective-permute-start.3 = (bf16[4,8,144,128]{3,2,1,0:T(8,128)(2,1)S(1)}, bf16[4,8,144,128]{3,2,1,0:T(8,128)(2,1)S(1)}, u32[]{:S(2)}, u32[]{:S(2)}) collective-permute-start(bf16[4,8,144,128]{3,2,1,0:T(8,128)(2,1)S(1)} %constant_dynamic-slice_fusion), channel_id=1, source_target_pairs={{0,1},{1,0},{2,3},{3,2},{4,5},{5,4},{6,7},{7,6},{8,9},{9,8},{10,11... | collective-permute-start | bytes 3538952 | tf_op jit(solution)/shard_map/cond/branch_1_fun/ppermute | solution.py:267
  76.9 2.6 %branch_1_fun.4 = bf16[256,3840]{1,0:T(8,128)(2,1)} custom-call(s32[6,128]{1,0:T(8,128)} %copy-done.2), custom_call_target="tpu_custom_call" | custom-call | flops 68719476736 | bytes 2097152 | tf_op jit(solution)/shard_map/cond/branch_1_fun/pallas_call | solution.py:268
  80.1 2.1 %copy.6 = bf16[6,8,4,2,24,128]{5,4,3,2,1,0:T(8,128)(2,1)} copy(bf16[6,8,4,2,24,128]{5,4,0,1,2,3:T(8,128)(2,1)S(1)} %maximum_bitcast_fusion) | data formatting | bytes 4718592 | tf_op jit(solution)/shard_map/cond/branch_1_fun/transpose | solution.py:280
  82.2 3.5 %branch_1_fun.5 = bf16[1536,768]{1,0:T(8,128)(2,1)S(1)} custom-call(s32[1]{0:T(128)} %get-tuple-element.28.first_ref, bf16[6,1536,128]{2,1,0:T(8,128)(2,1)} %bitcast.337, bf16[1536,768]{1,0:T(8,128)(2,1)} %get-tuple-element.40.live_ref), custom_call_target="tpu_custom_call" | custom-call | flops 301989888 | bytes 12582912 | tf_op jit(solution)/shard_map/cond/branch_1_fun/pallas_call | solution.py:281
  85.7 4.9 %all-to-all-done.3 = bf16[32,64,128]{2,1,0:T(8,128)(2,1)} async-done(((bf16[32,64,128]{2,1,0:T(8,128)(2,1)}), bf16[32,64,128]{2,1,0:T(8,128)(2,1)}, u32[]{:S(2)}, u32[]{:S(2)}) %all-to-all-start.3) | async-done | bytes 524320 | tf_op jit(solution)/shard_map/cond/branch_1_fun/all_to_all | solution.py:276
  90.6 2.1 %collective-permute-start.4 = (bf16[32,64,128]{2,1,0:T(8,128)(2,1)}, bf16[32,64,128]{2,1,0:T(8,128)(2,1)}, u32[]{:S(2)}, u32[]{:S(2)}) collective-permute-start(bf16[32,64,128]{2,1,0:T(8,128)(2,1)} %all-to-all-done.3), channel_id=1, source_target_pairs={{0,1},{1,0},{2,3},{3,2},{4,5},{5,4},{6,7},{7,6},{8,9},{9,8},{10,11... | collective-permute-start | bytes 1572872 | tf_op jit(solution)/shard_map/cond/branch_1_fun/ppermute | solution.py:289
  92.7 2.0 %collective-permute-done.4 = bf16[32,64,128]{2,1,0:T(8,128)(2,1)} collective-permute-done((bf16[32,64,128]{2,1,0:T(8,128)(2,1)}, bf16[32,64,128]{2,1,0:T(8,128)(2,1)}, u32[]{:S(2)}, u32[]{:S(2)}) %collective-permute-start.4) | collective-permute-done | bytes 524320 | tf_op jit(solution)/shard_map/cond/branch_1_fun/ppermute | solution.py:289
  94.7 4.3 %all-reduce.2.cloned.1.call-done.content_hbm = bf16[2,768,384]{2,1,0:T(8,128)(2,1)} async-done(((bf16[2,768,384]{2,1,0:T(8,128)(2,1)}), bf16[2,768,384]{2,1,0:T(8,128)(2,1)}) %all-reduce.2.cloned.1.call-update) | async-done | bytes 1179664 | tf_op jit(solution)/shard_map/psum | solution.py:227
  99.0 8.2 %shard_map.47 = bf16[1536,384]{1,0:T(8,128)(2,1)} custom-call(s32[1]{0:T(128)} %bitcast.32.core_ref, bf16[2,768,384]{2,1,0:T(8,128)(2,1)} %all-reduce.2.cloned.1.call-done.content_hbm, bf16[32,64,128]{2,1,0:T(8,128)(2,1)} %get-tuple-element.56.mine_hbm, bf16[32,64,128]{2,1,0:T(8,128)(2,1)} %get-tuple-element.57.other_hbm, f32[6,128,128]{2,1,0:T(8,128)} %inverses_hbm.1, ...), custom_call_target="tpu_custom_call" | custom-call | flops 1811939328 | bytes 16777216 | tf_op jit(solution)/shard_map/pallas_call | solution.py:298
  (65 shorter events, 4.3 us)
Async XLA Ops:
  6.5 4.3 %copy-start.1 = (s32[6,128]{1,0:T(8,128)S(1)}, s32[6,128]{1,0:T(8,128)}, u32[]{:S(2)}) copy-start(s32[6,128]{1,0:T(8,128)} %rows_ref.1) | copy-start | bytes 9220
  6.5 4.3 %copy-start = (bf16[6,24,128]{2,1,0:T(8,128)(2,1)S(1)}, bf16[6,24,128]{2,1,0:T(8,128)(2,1)}, u32[]{:S(2)}) copy-start(bf16[6,24,128]{2,1,0:T(8,128)(2,1)} %param.7) | copy-start | bytes 110596
  6.5 92.5 %all-reduce.2.cloned.1.call-start = ((), (), s32[]{:S(2)}) async-start(), calls=%async_computation.4 | async-start | bytes 2359296 | tf_op jit(solution)/shard_map/psum | solution.py:227
  10.8 56.1 %copy-start.2 = (s32[6,128]{1,0:T(8,128)}, s32[6,128]{1,0:T(8,128)S(1)}, u32[]{:S(2)}) copy-start(s32[6,128]{1,0:T(8,128)S(1)} %get-tuple-element.38.rows_ref) | copy-start | bytes 9220 | tf_op jit(solution)/shard_map/cond
  11.6 22.9 %all-to-all-start = ((bf16[8,144,128]{2,1,0:T(8,128)(2,1)}), bf16[8,144,128]{2,1,0:T(8,128)(2,1)S(1)}, u32[]{:S(2)}, u32[]{:S(2)}) async-start(bf16[8,144,128]{2,1,0:T(8,128)(2,1)} %broadcast_in_dim.68), calls=%async_computation | async-start | bytes 589824 | tf_op jit(solution)/shard_map/cond/branch_1_fun/all_to_all | solution.py:200
  36.6 8.8 %all-to-all-start.1 = ((bf16[8,64,128]{2,1,0:T(8,128)(2,1)}), bf16[8,64,128]{2,1,0:T(8,128)(2,1)S(1)}, u32[]{:S(2)}, u32[]{:S(2)}) async-start(bf16[8,64,128]{2,1,0:T(8,128)(2,1)} %select_select_fusion), calls=%async_computation.1 | async-start | bytes 262144 | tf_op jit(solution)/shard_map/cond/branch_1_fun/all_to_all | solution.py:246
  41.4 26.4 %collective-permute-start.1 = (bf16[8,144,128]{2,1,0:T(8,128)(2,1)S(1)}, bf16[8,144,128]{2,1,0:T(8,128)(2,1)S(1)}, u32[]{:S(2)}, u32[]{:S(2)}) collective-permute-start(bf16[8,144,128]{2,1,0:T(8,128)(2,1)S(1)} %all-to-all-done), channel_id=1, source_target_pairs={{4,0},{6,2},{0,4},{2,6},{5,1},{7,3},{1,5},{3,7},{12,8},{14,10},{8,... | collective-permute-start | bytes 884744 | tf_op jit(solution)/shard_map/cond/branch_1_fun/ppermute | solution.py:262
  46.2 20.7 %all-to-all-start.2 = ((bf16[8,64,128]{2,1,0:T(8,128)(2,1)}), bf16[8,64,128]{2,1,0:T(8,128)(2,1)}, u32[]{:S(2)}, u32[]{:S(2)}) async-start(bf16[8,64,128]{2,1,0:T(8,128)(2,1)} %broadcast_in_dim.71), calls=%async_computation.2 | async-start | bytes 262144 | tf_op jit(solution)/shard_map/cond/branch_1_fun/all_to_all | solution.py:200
  53.3 14.5 %collective-permute-start = (bf16[8,144,128]{2,1,0:T(8,128)(2,1)S(1)}, bf16[8,144,128]{2,1,0:T(8,128)(2,1)S(1)}, u32[]{:S(2)}, u32[]{:S(2)}) collective-permute-start(bf16[8,144,128]{2,1,0:T(8,128)(2,1)S(1)} %all-to-all-done), channel_id=1, source_target_pairs={{2,0},{4,2},{6,4},{0,6},{3,1},{5,3},{7,5},{1,7},{10,8},{12,10},{14... | collective-permute-start | bytes 884744 | tf_op jit(solution)/shard_map/cond/branch_1_fun/ppermute | solution.py:262
  55.2 12.7 %collective-permute-start.2 = (bf16[8,144,128]{2,1,0:T(8,128)(2,1)S(1)}, bf16[8,144,128]{2,1,0:T(8,128)(2,1)S(1)}, u32[]{:S(2)}, u32[]{:S(2)}) collective-permute-start(bf16[8,144,128]{2,1,0:T(8,128)(2,1)S(1)} %all-to-all-done), channel_id=1, source_target_pairs={{6,0},{0,2},{2,4},{4,6},{7,1},{1,3},{3,5},{5,7},{14,8},{8,10},{10,... | collective-permute-start | bytes 884744 | tf_op jit(solution)/shard_map/cond/branch_1_fun/ppermute | solution.py:262
  69.2 21.4 %all-to-all-start.3 = ((bf16[32,64,128]{2,1,0:T(8,128)(2,1)}), bf16[32,64,128]{2,1,0:T(8,128)(2,1)}, u32[]{:S(2)}, u32[]{:S(2)}) async-start(bf16[32,64,128]{2,1,0:T(8,128)(2,1)} %broadcast_in_dim.72), calls=%async_computation.3 | async-start | bytes 1048576 | tf_op jit(solution)/shard_map/cond/branch_1_fun/all_to_all | solution.py:276
  75.0 4.7 %collective-permute-start.3 = (bf16[4,8,144,128]{3,2,1,0:T(8,128)(2,1)S(1)}, bf16[4,8,144,128]{3,2,1,0:T(8,128)(2,1)S(1)}, u32[]{:S(2)}, u32[]{:S(2)}) collective-permute-start(bf16[4,8,144,128]{3,2,1,0:T(8,128)(2,1)S(1)} %constant_dynamic-slice_fusion), channel_id=1, source_target_pairs={{0,1},{1,0},{2,3},{3,2},{4,5},{5,4},{6,7},{7,6},{8,9},{9,8},{10,11... | collective-permute-start | bytes 3538952 | tf_op jit(solution)/shard_map/cond/branch_1_fun/ppermute | solution.py:267
  90.6 4.1 %collective-permute-start.4 = (bf16[32,64,128]{2,1,0:T(8,128)(2,1)}, bf16[32,64,128]{2,1,0:T(8,128)(2,1)}, u32[]{:S(2)}, u32[]{:S(2)}) collective-permute-start(bf16[32,64,128]{2,1,0:T(8,128)(2,1)} %all-to-all-done.3), channel_id=1, source_target_pairs={{0,1},{1,0},{2,3},{3,2},{4,5},{5,4},{6,7},{7,6},{8,9},{9,8},{10,11... | collective-permute-start | bytes 1572872 | tf_op jit(solution)/shard_map/cond/branch_1_fun/ppermute | solution.py:289
Sparse Core Ops, SparseCore 0:
  10.9 88.0 all-reduce.1

commit v10 on v8

--- a/solution.py
+++ b/solution.py
@@ -136,7 +136,7 @@
 
 
 def solve_kernel(core_ref, content_hbm, mine_hbm, other_hbm, inverses_hbm, select_hbm, last_hbm, lower_hbm, kept_hbm, out_hbm,
-                 content, low, inverses, parts, coef, last, lower, kept, state, moved, upper, out, sems, out_sems):
+                 content, low, inverses, parts, coef, factor, kept, state, final, out, sems, out_sems):
     core = core_ref[0]
     height = out.shape[0] // BLOCKS
     copies = [
@@ -147,8 +147,8 @@
             (mine_hbm, low.at[core]),
             (other_hbm, low.at[1 - core]),
             (select_hbm, coef),
-            (last_hbm, last),
-            (lower_hbm, lower),
+            (last_hbm, factor.at[:, :TOP]),
+            (lower_hbm, factor.at[:, TOP:]),
             (kept_hbm, kept),
         ))
     ]
@@ -180,18 +180,17 @@
             x = x + jnp.dot(coef[:, at:at + 2 * NB * k], state[:2 * NB * k, :], preferred_element_type=F32)
         y = x.astype(BF)
         state[2 * NB * k:2 * NB * k + NB, :] = y[:NB]
-        moved[k * NB:(k + 1) * NB, :] = y[:NB]
+        final[k * NB:(k + 1) * NB, :] = y[:NB]
         u = jnp.dot(parts[k], y[NB:], preferred_element_type=F32)
         u = (u[:NB] + (u[NB:2 * NB] + u[2 * NB:])).astype(BF)
         state[2 * NB * k + NB:2 * NB * (k + 1), :] = u
-        upper[k * NB:(k + 1) * NB, :] = u
+        final[TOP + k * NB:TOP + (k + 1) * NB, :] = u
     for copy in copies[5:]:
         copy.wait()
     writes = []
     for b in range(BLOCKS):
         at = b * height
-        new = jnp.dot(last[at:at + height, :], moved[...], preferred_element_type=F32)
-        new = new + jnp.dot(lower[at:at + height, :], upper[...], preferred_element_type=F32)
+        new = jnp.dot(factor[at:at + height, :], final[...], preferred_element_type=F32)
         out[at:at + height, :] = (kept[at:at + height, :].astype(F32) + new).astype(BF)
         writes.append(pltpu.make_async_copy(out.at[at:at + height], out_hbm.at[at:at + height], out_sems.at[b]))
         writes[-1].start()
@@ -310,12 +309,10 @@
             pltpu.VMEM(inverses.shape, F32),
             pltpu.VMEM((STEPS, 3 * NB, NB), BF),
             pltpu.VMEM(select.shape, BF),
-            pltpu.VMEM(last.shape, BF),
-            pltpu.VMEM(lower.shape, BF),
+            pltpu.VMEM((local, 2 * TOP), BF),
             pltpu.VMEM((local, width), BF),
             pltpu.VMEM((2 * TOP, width), BF),
-            pltpu.VMEM((TOP, width), BF),
-            pltpu.VMEM((TOP, width), BF),
+            pltpu.VMEM((2 * TOP, width), BF),
             pltpu.VMEM((local, width), BF),
             pltpu.SemaphoreType.DMA((8,)),
             pltpu.SemaphoreType.DMA((BLOCKS,)),

time: 115 us -> 115 us (level)
  no operation moved by 1% of the time
where the time goes in v10:
time: 115 us; the launch traced here: 112 us
  starting transfers between devices  42.3 us (37%)
  Pallas kernels  24.4 us (21%)
  waiting for transfers between devices  21.6 us (19%)
  between operations  13.4 us (12%)
  local copies, waits for them, and re-layouts  6.37 us (6%)
  other arithmetic  4.08 us (4%)
    all_to_all x2, starting transfers between devices, spread(): lax.all_to_all(jnp.broadcast_to(x[None], (parts,) + x.shape), axes, 0, 0,...  17.4 us
    all_to_all x2, waiting for transfers between devices, spread(): lax.all_to_all(jnp.broadcast_to(x[None], (parts,) + x.shape), axes, 0, 0,...  13.5 us
    ppermute x3, starting transfers between devices, gather(): lax.ppermute(column, 'x', [((i + s) % nx, i) for i in range(nx)])  8.65 us
    pallas_call x1, Pallas kernels, per_device(): pl.pallas_call(solve_kernel, out_shape=jax.ShapeDtypeStruct((local, width...  8.16 us
    all_to_all x1, starting transfers between devices, gather(): low_mine = lax.all_to_all(part, ('z', 'x'), 0, 0, tiled=True)  7.43 us
    pallas_call x1, Pallas kernels, gather(): pl.pallas_call(mark_kernel, out_shape=(jax.ShapeDtypeStruct((local, TOP),...  6.61 us
    all_to_all x1, starting transfers between devices, gather(): part = lax.all_to_all(part, ('c', 'x'), 0, 0, tiled=True)  4.78 us
    all_to_all x1, waiting for transfers between devices, gather(): low_mine = lax.all_to_all(part, ('z', 'x'), 0, 0, tiled=True)  4.68 us
  transfers between devices with their start and end apart: 10, of which 6 were waited for; matrix products, arithmetic and copies ran while one was open for 9% of the time, Pallas kernels for 11%

profile of v10, /device:TPU:6, one launch (start us, length us, event | category | flops | bytes accessed | tf_op | source)
XLA Modules:
  0.0 112.5 jit_solution(14718603627850031824)
XLA Ops:
  6.5 4.2 %shard_map.46 = bf16[2,768,384]{2,1,0:T(8,128)(2,1)} custom-call(s32[1]{0:T(128)} %bitcast.33.first_ref, s32[6,128]{1,0:T(8,128)} %rows_ref.1, bf16[1536,384]{1,0:T(8,128)(2,1)} %matrix_hbm.1), custom_call_target="tpu_custom_call" | custom-call | flops 905969664 | bytes 4194304 | tf_op jit(solution)/shard_map/pallas_call | solution.py:220
  10.8 86.1 %conditional.1 = (bf16[32,64,128]{2,1,0:T(8,128)(2,1)}, bf16[32,64,128]{2,1,0:T(8,128)(2,1)}, bf16[1536,768]{1,0:T(8,128)(2,1)}, bf16[1536,768]{1,0:T(8,128)(2,1...) conditional(s32[]{:T(128)} %convert_element_type.2, () %tuple.19, (s32[6,128]{1,0:T(8,128)S(1)}, ...), branch_computations={%region_1.0_spmd, %region_2.5_spmd} | conditional | flops 69628207104 | bytes 57746280 | solution.py:297
  11.6 10.3 %all-to-all-start = ((bf16[8,144,128]{2,1,0:T(8,128)(2,1)}), bf16[8,144,128]{2,1,0:T(8,128)(2,1)S(1)}, u32[]{:S(2)}, u32[]{:S(2)}) async-start(bf16[8,144,128]{2,1,0:T(8,128)(2,1)} %broadcast_in_dim.68), calls=%async_computation | async-start | bytes 589824 | tf_op jit(solution)/shard_map/cond/branch_1_fun/all_to_all | solution.py:206
  23.1 11.4 %all-to-all-done = bf16[8,144,128]{2,1,0:T(8,128)(2,1)S(1)} async-done(((bf16[8,144,128]{2,1,0:T(8,128)(2,1)}), bf16[8,144,128]{2,1,0:T(8,128)(2,1)S(1)}, u32[]{:S(2)}, u32[]{:S(2)}) %all-to-all-start) | async-done | bytes 294944 | tf_op jit(solution)/shard_map/cond/branch_1_fun/all_to_all | solution.py:206
  34.5 1.3 %gather_fusion = bf16[512,128]{1,0:T(8,128)(2,1)S(1)} fusion(bf16[1152,128]{1,0:T(8,128)(2,1)S(1)} %bitcast.336, s32[1024]{0:T(1024)S(1)} %pad_clamp_fusion), kind=kCustom, calls=%fused_computation | custom fusion | bytes 264192 | tf_op jit(solution)/shard_map/cond/branch_1_fun/jit(_take)/gather | solution.py:250
  36.7 4.8 %all-to-all-start.1 = ((bf16[8,64,128]{2,1,0:T(8,128)(2,1)}), bf16[8,64,128]{2,1,0:T(8,128)(2,1)}, u32[]{:S(2)}, u32[]{:S(2)}) async-start(bf16[8,64,128]{2,1,0:T(8,128)(2,1)} %select_select_fusion), calls=%async_computation.1 | async-start | bytes 262144 | tf_op jit(solution)/shard_map/cond/branch_1_fun/all_to_all | solution.py:252
  41.5 1.9 %collective-permute-start.2 = (bf16[8,144,128]{2,1,0:T(8,128)(2,1)S(1)}, bf16[8,144,128]{2,1,0:T(8,128)(2,1)S(1)}, u32[]{:S(2)}, u32[]{:S(2)}) collective-permute-start(bf16[8,144,128]{2,1,0:T(8,128)(2,1)S(1)} %all-to-all-done), channel_id=1, source_target_pairs={{6,0},{0,2},{2,4},{4,6},{7,1},{1,3},{3,5},{5,7},{14,8},{8,10},{10,... | collective-permute-start | bytes 884744 | tf_op jit(solution)/shard_map/cond/branch_1_fun/ppermute | solution.py:266
  43.4 4.8 %collective-permute-start.1 = (bf16[8,144,128]{2,1,0:T(8,128)(2,1)S(1)}, bf16[8,144,128]{2,1,0:T(8,128)(2,1)S(1)}, u32[]{:S(2)}, u32[]{:S(2)}) collective-permute-start(bf16[8,144,128]{2,1,0:T(8,128)(2,1)S(1)} %all-to-all-done), channel_id=1, source_target_pairs={{4,0},{6,2},{0,4},{2,6},{5,1},{7,3},{1,5},{3,7},{12,8},{14,10},{8,... | collective-permute-start | bytes 884744 | tf_op jit(solution)/shard_map/cond/branch_1_fun/ppermute | solution.py:266
  48.2 1.9 %collective-permute-start = (bf16[8,144,128]{2,1,0:T(8,128)(2,1)S(1)}, bf16[8,144,128]{2,1,0:T(8,128)(2,1)S(1)}, u32[]{:S(2)}, u32[]{:S(2)}) collective-permute-start(bf16[8,144,128]{2,1,0:T(8,128)(2,1)S(1)} %all-to-all-done), channel_id=1, source_target_pairs={{2,0},{4,2},{6,4},{0,6},{3,1},{5,3},{7,5},{1,7},{10,8},{12,10},{14... | collective-permute-start | bytes 884744 | tf_op jit(solution)/shard_map/cond/branch_1_fun/ppermute | solution.py:266
  50.2 0.9 reduce_sum.22
  51.8 7.1 %all-to-all-start.2 = ((bf16[8,64,128]{2,1,0:T(8,128)(2,1)}), bf16[8,64,128]{2,1,0:T(8,128)(2,1)}, u32[]{:S(2)}, u32[]{:S(2)}) async-start(bf16[8,64,128]{2,1,0:T(8,128)(2,1)} %broadcast_in_dim.71), calls=%async_computation.2 | async-start | bytes 262144 | tf_op jit(solution)/shard_map/cond/branch_1_fun/all_to_all | solution.py:206
  58.9 6.6 %branch_1_fun.3 = (bf16[1536,768]{1,0:T(8,128)(2,1)}, bf16[1536,768]{1,0:T(8,128)(2,1)}, bf16[1536,384]{1,0:T(8,128)(2,1)}) custom-call(s32[1]{0:T(128)} %get-tuple-element.28.first_ref, s32[6,128]{1,0:T(8,128)} %copy-done.2, bf16[1536,384]{1,0:T(8,128)(2,1)} %get-tuple-element.30.matrix_ref), custom_call_target="tpu_custom_call" | custom-call | flops 603979776 | bytes 6291456 | tf_op jit(solution)/shard_map/cond/branch_1_fun/pallas_call | solution.py:256
  66.0 2.1 %all-to-all-done.2 = bf16[8,64,128]{2,1,0:T(8,128)(2,1)} async-done(((bf16[8,64,128]{2,1,0:T(8,128)(2,1)}), bf16[8,64,128]{2,1,0:T(8,128)(2,1)}, u32[]{:S(2)}, u32[]{:S(2)}) %all-to-all-start.2) | async-done | bytes 131104 | tf_op jit(solution)/shard_map/cond/branch_1_fun/all_to_all | solution.py:206
  68.1 0.9 reduce_sum.23
  69.0 0.9 broadcast_in_dim.72
  69.9 7.4 %all-to-all-start.3 = ((bf16[32,64,128]{2,1,0:T(8,128)(2,1)}), bf16[32,64,128]{2,1,0:T(8,128)(2,1)}, u32[]{:S(2)}, u32[]{:S(2)}) async-start(bf16[32,64,128]{2,1,0:T(8,128)(2,1)} %broadcast_in_dim.72), calls=%async_computation.3 | async-start | bytes 1048576 | tf_op jit(solution)/shard_map/cond/branch_1_fun/all_to_all | solution.py:279
  77.4 1.9 %collective-permute-start.3 = (bf16[4,8,144,128]{3,2,1,0:T(8,128)(2,1)S(1)}, bf16[4,8,144,128]{3,2,1,0:T(8,128)(2,1)S(1)}, u32[]{:S(2)}, u32[]{:S(2)}) collective-permute-start(bf16[4,8,144,128]{3,2,1,0:T(8,128)(2,1)S(1)} %constant_dynamic-slice_fusion), channel_id=1, source_target_pairs={{0,1},{1,0},{2,3},{3,2},{4,5},{5,4},{6,7},{7,6},{8,9},{9,8},{10,11... | collective-permute-start | bytes 3538952 | tf_op jit(solution)/shard_map/cond/branch_1_fun/ppermute | solution.py:270
  79.3 2.0 %branch_1_fun.4 = bf16[256,3840]{1,0:T(8,128)(2,1)} custom-call(s32[6,128]{1,0:T(8,128)S(1)} %copy-done.3), custom_call_target="tpu_custom_call" | custom-call | flops 68719476736 | bytes 2097152 | tf_op jit(solution)/shard_map/cond/branch_1_fun/pallas_call | solution.py:271
  82.5 2.1 %copy.6 = bf16[6,8,4,2,24,128]{5,4,3,2,1,0:T(8,128)(2,1)} copy(bf16[6,8,4,2,24,128]{5,4,0,1,2,3:T(8,128)(2,1)S(1)} %maximum_bitcast_fusion) | data formatting | bytes 4718592 | tf_op jit(solution)/shard_map/cond/branch_1_fun/transpose | solution.py:283
  84.6 3.5 %branch_1_fun.5 = bf16[1536,768]{1,0:T(8,128)(2,1)S(1)} custom-call(s32[1]{0:T(128)} %get-tuple-element.28.first_ref, bf16[6,1536,128]{2,1,0:T(8,128)(2,1)} %bitcast.337, bf16[1536,768]{1,0:T(8,128)(2,1)} %get-tuple-element.39.live_ref), custom_call_target="tpu_custom_call" | custom-call | flops 301989888 | bytes 12582912 | tf_op jit(solution)/shard_map/cond/branch_1_fun/pallas_call | solution.py:284
  88.1 4.7 %all-to-all-done.3 = bf16[32,64,128]{2,1,0:T(8,128)(2,1)} async-done(((bf16[32,64,128]{2,1,0:T(8,128)(2,1)}), bf16[32,64,128]{2,1,0:T(8,128)(2,1)}, u32[]{:S(2)}, u32[]{:S(2)}) %all-to-all-start.3) | async-done | bytes 524320 | tf_op jit(solution)/shard_map/cond/branch_1_fun/all_to_all | solution.py:279
  92.7 2.1 %collective-permute-start.4 = (bf16[32,64,128]{2,1,0:T(8,128)(2,1)}, bf16[32,64,128]{2,1,0:T(8,128)(2,1)}, u32[]{:S(2)}, u32[]{:S(2)}) collective-permute-start(bf16[32,64,128]{2,1,0:T(8,128)(2,1)} %all-to-all-done.3), channel_id=1, source_target_pairs={{0,1},{1,0},{2,3},{3,2},{4,5},{5,4},{6,7},{7,6},{8,9},{9,8},{10,11... | collective-permute-start | bytes 1572872 | tf_op jit(solution)/shard_map/cond/branch_1_fun/ppermute | solution.py:292
  94.8 2.0 %collective-permute-done.4 = bf16[32,64,128]{2,1,0:T(8,128)(2,1)} collective-permute-done((bf16[32,64,128]{2,1,0:T(8,128)(2,1)}, bf16[32,64,128]{2,1,0:T(8,128)(2,1)}, u32[]{:S(2)}, u32[]{:S(2)}) %collective-permute-start.4) | collective-permute-done | bytes 524320 | tf_op jit(solution)/shard_map/cond/branch_1_fun/ppermute | solution.py:292
  97.5 8.2 %shard_map.47 = bf16[1536,384]{1,0:T(8,128)(2,1)} custom-call(s32[1]{0:T(128)} %bitcast.32.core_ref, bf16[2,768,384]{2,1,0:T(8,128)(2,1)} %all-reduce.2.cloned.1.call-done.content_hbm, bf16[32,64,128]{2,1,0:T(8,128)(2,1)} %get-tuple-element.55.mine_hbm, bf16[32,64,128]{2,1,0:T(8,128)(2,1)} %get-tuple-element.56.other_hbm, f32[6,128,128]{2,1,0:T(8,128)} %inverses_hbm.1, ...), custom_call_target="tpu_custom_call" | custom-call | flops 1811939328 | bytes 16777216 | tf_op jit(solution)/shard_map/pallas_call | solution.py:301
  (67 shorter events, 5.7 us)
Async XLA Ops:
  6.5 4.3 %copy-start.1 = (s32[6,128]{1,0:T(8,128)S(1)}, s32[6,128]{1,0:T(8,128)}, u32[]{:S(2)}) copy-start(s32[6,128]{1,0:T(8,128)} %rows_ref.1) | copy-start | bytes 9220
  6.5 4.3 %copy-start = (bf16[6,24,128]{2,1,0:T(8,128)(2,1)S(1)}, bf16[6,24,128]{2,1,0:T(8,128)(2,1)}, u32[]{:S(2)}) copy-start(bf16[6,24,128]{2,1,0:T(8,128)(2,1)} %param.7) | copy-start | bytes 110596
  6.5 90.9 %all-reduce.2.cloned.1.call-start = ((), (), s32[]{:S(2)}) async-start(), calls=%async_computation.4 | async-start | bytes 2359296 | tf_op jit(solution)/shard_map/psum | solution.py:233
  10.8 37.4 %copy-start.2 = (s32[6,128]{1,0:T(8,128)}, s32[6,128]{1,0:T(8,128)S(1)}, u32[]{:S(2)}) copy-start(s32[6,128]{1,0:T(8,128)S(1)} %get-tuple-element.37.rows_ref) | copy-start | bytes 9220 | tf_op jit(solution)/shard_map/cond
  11.6 22.9 %all-to-all-start = ((bf16[8,144,128]{2,1,0:T(8,128)(2,1)}), bf16[8,144,128]{2,1,0:T(8,128)(2,1)S(1)}, u32[]{:S(2)}, u32[]{:S(2)}) async-start(bf16[8,144,128]{2,1,0:T(8,128)(2,1)} %broadcast_in_dim.68), calls=%async_computation | async-start | bytes 589824 | tf_op jit(solution)/shard_map/cond/branch_1_fun/all_to_all | solution.py:206
  36.7 13.5 %all-to-all-start.1 = ((bf16[8,64,128]{2,1,0:T(8,128)(2,1)}), bf16[8,64,128]{2,1,0:T(8,128)(2,1)}, u32[]{:S(2)}, u32[]{:S(2)}) async-start(bf16[8,64,128]{2,1,0:T(8,128)(2,1)} %select_select_fusion), calls=%async_computation.1 | async-start | bytes 262144 | tf_op jit(solution)/shard_map/cond/branch_1_fun/all_to_all | solution.py:252
  41.5 24.2 %collective-permute-start.2 = (bf16[8,144,128]{2,1,0:T(8,128)(2,1)S(1)}, bf16[8,144,128]{2,1,0:T(8,128)(2,1)S(1)}, u32[]{:S(2)}, u32[]{:S(2)}) collective-permute-start(bf16[8,144,128]{2,1,0:T(8,128)(2,1)S(1)} %all-to-all-done), channel_id=1, source_target_pairs={{6,0},{0,2},{2,4},{4,6},{7,1},{1,3},{3,5},{5,7},{14,8},{8,10},{10,... | collective-permute-start | bytes 884744 | tf_op jit(solution)/shard_map/cond/branch_1_fun/ppermute | solution.py:266
  43.4 22.2 %collective-permute-start.1 = (bf16[8,144,128]{2,1,0:T(8,128)(2,1)S(1)}, bf16[8,144,128]{2,1,0:T(8,128)(2,1)S(1)}, u32[]{:S(2)}, u32[]{:S(2)}) collective-permute-start(bf16[8,144,128]{2,1,0:T(8,128)(2,1)S(1)} %all-to-all-done), channel_id=1, source_target_pairs={{4,0},{6,2},{0,4},{2,6},{5,1},{7,3},{1,5},{3,7},{12,8},{14,10},{8,... | collective-permute-start | bytes 884744 | tf_op jit(solution)/shard_map/cond/branch_1_fun/ppermute | solution.py:266
  48.2 17.3 %collective-permute-start = (bf16[8,144,128]{2,1,0:T(8,128)(2,1)S(1)}, bf16[8,144,128]{2,1,0:T(8,128)(2,1)S(1)}, u32[]{:S(2)}, u32[]{:S(2)}) collective-permute-start(bf16[8,144,128]{2,1,0:T(8,128)(2,1)S(1)} %all-to-all-done), channel_id=1, source_target_pairs={{2,0},{4,2},{6,4},{0,6},{3,1},{5,3},{7,5},{1,7},{10,8},{12,10},{14... | collective-permute-start | bytes 884744 | tf_op jit(solution)/shard_map/cond/branch_1_fun/ppermute | solution.py:266
  51.8 16.3 %all-to-all-start.2 = ((bf16[8,64,128]{2,1,0:T(8,128)(2,1)}), bf16[8,64,128]{2,1,0:T(8,128)(2,1)}, u32[]{:S(2)}, u32[]{:S(2)}) async-start(bf16[8,64,128]{2,1,0:T(8,128)(2,1)} %broadcast_in_dim.71), calls=%async_computation.2 | async-start | bytes 262144 | tf_op jit(solution)/shard_map/cond/branch_1_fun/all_to_all | solution.py:206
  65.8 13.5 %copy-start.3 = (s32[6,128]{1,0:T(8,128)S(1)}, s32[6,128]{1,0:T(8,128)}, u32[]{:S(2)}) copy-start(s32[6,128]{1,0:T(8,128)} %copy-done.2) | copy-start | bytes 9220 | tf_op jit(solution)/shard_map/cond
  69.9 22.8 %all-to-all-start.3 = ((bf16[32,64,128]{2,1,0:T(8,128)(2,1)}), bf16[32,64,128]{2,1,0:T(8,128)(2,1)}, u32[]{:S(2)}, u32[]{:S(2)}) async-start(bf16[32,64,128]{2,1,0:T(8,128)(2,1)} %broadcast_in_dim.72), calls=%async_computation.3 | async-start | bytes 1048576 | tf_op jit(solution)/shard_map/cond/branch_1_fun/all_to_all | solution.py:279
  77.4 4.7 %collective-permute-start.3 = (bf16[4,8,144,128]{3,2,1,0:T(8,128)(2,1)S(1)}, bf16[4,8,144,128]{3,2,1,0:T(8,128)(2,1)S(1)}, u32[]{:S(2)}, u32[]{:S(2)}) collective-permute-start(bf16[4,8,144,128]{3,2,1,0:T(8,128)(2,1)S(1)} %constant_dynamic-slice_fusion), channel_id=1, source_target_pairs={{0,1},{1,0},{2,3},{3,2},{4,5},{5,4},{6,7},{7,6},{8,9},{9,8},{10,11... | collective-permute-start | bytes 3538952 | tf_op jit(solution)/shard_map/cond/branch_1_fun/ppermute | solution.py:270
  92.7 4.1 %collective-permute-start.4 = (bf16[32,64,128]{2,1,0:T(8,128)(2,1)}, bf16[32,64,128]{2,1,0:T(8,128)(2,1)}, u32[]{:S(2)}, u32[]{:S(2)}) collective-permute-start(bf16[32,64,128]{2,1,0:T(8,128)(2,1)} %all-to-all-done.3), channel_id=1, source_target_pairs={{0,1},{1,0},{2,3},{3,2},{4,5},{5,4},{6,7},{7,6},{8,9},{9,8},{10,11... | collective-permute-start | bytes 1572872 | tf_op jit(solution)/shard_map/cond/branch_1_fun/ppermute | solution.py:292
Sparse Core Ops, SparseCore 0:
  10.9 86.5 all-reduce.1

commit v11 on v10

--- a/solution.py
+++ b/solution.py
@@ -152,7 +152,7 @@
             (kept_hbm, kept),
         ))
     ]
-    for copy in copies:
+    for copy in copies[:5]:
         copy.start()
     copies[0].wait()
     for k in range(STEPS):
@@ -161,6 +161,8 @@
             parts[k, i * NB:(i + 1) * NB, :] = rest.astype(BF)
             rest = rest - rest.astype(BF).astype(F32)
     copies[1].wait()
+    for copy in copies[5:]:
+        copy.start()
     each = CHUNK
     for k in range(STEPS):
         x = content[:, k * NB:(k + 1) * NB, :].reshape(2 * NB, -1).astype(F32)

time: 115 us -> 115 us (level)
  no operation moved by 1% of the time
where the time goes in v11:
time: 115 us; the launch traced here: 112 us
  starting transfers between devices  42.3 us (37%)
  Pallas kernels  24.4 us (21%)
  waiting for transfers between devices  21.6 us (19%)
  between operations  13.4 us (12%)
  local copies, waits for them, and re-layouts  6.37 us (6%)
  other arithmetic  4.08 us (4%)
    all_to_all x2, starting transfers between devices, spread(): lax.all_to_all(jnp.broadcast_to(x[None], (parts,) + x.shape), axes, 0, 0,...  17.4 us
    all_to_all x2, waiting for transfers between devices, spread(): lax.all_to_all(jnp.broadcast_to(x[None], (parts,) + x.shape), axes, 0, 0,...  13.5 us
    ppermute x3, starting transfers between devices, gather(): lax.ppermute(column, 'x', [((i + s) % nx, i) for i in range(nx)])  8.65 us
    pallas_call x1, Pallas kernels, per_device(): pl.pallas_call(solve_kernel, out_shape=jax.ShapeDtypeStruct((local, width...  8.16 us
    all_to_all x1, starting transfers between devices, gather(): low_mine = lax.all_to_all(part, ('z', 'x'), 0, 0, tiled=True)  7.43 us
    pallas_call x1, Pallas kernels, gather(): pl.pallas_call(mark_kernel, out_shape=(jax.ShapeDtypeStruct((local, TOP),...  6.61 us
    all_to_all x1, starting transfers between devices, gather(): part = lax.all_to_all(part, ('c', 'x'), 0, 0, tiled=True)  4.78 us
    all_to_all x1, waiting for transfers between devices, gather(): low_mine = lax.all_to_all(part, ('z', 'x'), 0, 0, tiled=True)  4.68 us
  transfers between devices with their start and end apart: 10, of which 6 were waited for; matrix products, arithmetic and copies ran while one was open for 9% of the time, Pallas kernels for 11%

profile of v11, /device:TPU:6, one launch (start us, length us, event | category | flops | bytes accessed | tf_op | source)
XLA Modules:
  0.0 112.5 jit_solution(9588344893368142154)
XLA Ops:
  6.5 4.2 %shard_map.46 = bf16[2,768,384]{2,1,0:T(8,128)(2,1)} custom-call(s32[1]{0:T(128)} %bitcast.33.first_ref, s32[6,128]{1,0:T(8,128)} %rows_ref.1, bf16[1536,384]{1,0:T(8,128)(2,1)} %matrix_hbm.1), custom_call_target="tpu_custom_call" | custom-call | flops 905969664 | bytes 4194304 | tf_op jit(solution)/shard_map/pallas_call | solution.py:222
  10.8 86.1 %conditional.1 = (bf16[32,64,128]{2,1,0:T(8,128)(2,1)}, bf16[32,64,128]{2,1,0:T(8,128)(2,1)}, bf16[1536,768]{1,0:T(8,128)(2,1)}, bf16[1536,768]{1,0:T(8,128)(2,1...) conditional(s32[]{:T(128)} %convert_element_type.2, () %tuple.19, (s32[6,128]{1,0:T(8,128)S(1)}, ...), branch_computations={%region_1.0_spmd, %region_2.5_spmd} | conditional | flops 69628207104 | bytes 57746280 | solution.py:299
  11.6 10.3 %all-to-all-start = ((bf16[8,144,128]{2,1,0:T(8,128)(2,1)}), bf16[8,144,128]{2,1,0:T(8,128)(2,1)S(1)}, u32[]{:S(2)}, u32[]{:S(2)}) async-start(bf16[8,144,128]{2,1,0:T(8,128)(2,1)} %broadcast_in_dim.68), calls=%async_computation | async-start | bytes 589824 | tf_op jit(solution)/shard_map/cond/branch_1_fun/all_to_all | solution.py:208
  23.1 11.4 %all-to-all-done = bf16[8,144,128]{2,1,0:T(8,128)(2,1)S(1)} async-done(((bf16[8,144,128]{2,1,0:T(8,128)(2,1)}), bf16[8,144,128]{2,1,0:T(8,128)(2,1)S(1)}, u32[]{:S(2)}, u32[]{:S(2)}) %all-to-all-start) | async-done | bytes 294944 | tf_op jit(solution)/shard_map/cond/branch_1_fun/all_to_all | solution.py:208
  34.5 1.3 %gather_fusion = bf16[512,128]{1,0:T(8,128)(2,1)S(1)} fusion(bf16[1152,128]{1,0:T(8,128)(2,1)S(1)} %bitcast.336, s32[1024]{0:T(1024)S(1)} %pad_clamp_fusion), kind=kCustom, calls=%fused_computation | custom fusion | bytes 264192 | tf_op jit(solution)/shard_map/cond/branch_1_fun/jit(_take)/gather | solution.py:252
  36.7 4.8 %all-to-all-start.1 = ((bf16[8,64,128]{2,1,0:T(8,128)(2,1)}), bf16[8,64,128]{2,1,0:T(8,128)(2,1)}, u32[]{:S(2)}, u32[]{:S(2)}) async-start(bf16[8,64,128]{2,1,0:T(8,128)(2,1)} %select_select_fusion), calls=%async_computation.1 | async-start | bytes 262144 | tf_op jit(solution)/shard_map/cond/branch_1_fun/all_to_all | solution.py:254
  41.5 1.9 %collective-permute-start.2 = (bf16[8,144,128]{2,1,0:T(8,128)(2,1)S(1)}, bf16[8,144,128]{2,1,0:T(8,128)(2,1)S(1)}, u32[]{:S(2)}, u32[]{:S(2)}) collective-permute-start(bf16[8,144,128]{2,1,0:T(8,128)(2,1)S(1)} %all-to-all-done), channel_id=1, source_target_pairs={{6,0},{0,2},{2,4},{4,6},{7,1},{1,3},{3,5},{5,7},{14,8},{8,10},{10,... | collective-permute-start | bytes 884744 | tf_op jit(solution)/shard_map/cond/branch_1_fun/ppermute | solution.py:268
  43.4 4.8 %collective-permute-start.1 = (bf16[8,144,128]{2,1,0:T(8,128)(2,1)S(1)}, bf16[8,144,128]{2,1,0:T(8,128)(2,1)S(1)}, u32[]{:S(2)}, u32[]{:S(2)}) collective-permute-start(bf16[8,144,128]{2,1,0:T(8,128)(2,1)S(1)} %all-to-all-done), channel_id=1, source_target_pairs={{4,0},{6,2},{0,4},{2,6},{5,1},{7,3},{1,5},{3,7},{12,8},{14,10},{8,... | collective-permute-start | bytes 884744 | tf_op jit(solution)/shard_map/cond/branch_1_fun/ppermute | solution.py:268
  48.2 1.9 %collective-permute-start = (bf16[8,144,128]{2,1,0:T(8,128)(2,1)S(1)}, bf16[8,144,128]{2,1,0:T(8,128)(2,1)S(1)}, u32[]{:S(2)}, u32[]{:S(2)}) collective-permute-start(bf16[8,144,128]{2,1,0:T(8,128)(2,1)S(1)} %all-to-all-done), channel_id=1, source_target_pairs={{2,0},{4,2},{6,4},{0,6},{3,1},{5,3},{7,5},{1,7},{10,8},{12,10},{14... | collective-permute-start | bytes 884744 | tf_op jit(solution)/shard_map/cond/branch_1_fun/ppermute | solution.py:268
  50.2 0.9 reduce_sum.22
  51.8 7.1 %all-to-all-start.2 = ((bf16[8,64,128]{2,1,0:T(8,128)(2,1)}), bf16[8,64,128]{2,1,0:T(8,128)(2,1)}, u32[]{:S(2)}, u32[]{:S(2)}) async-start(bf16[8,64,128]{2,1,0:T(8,128)(2,1)} %broadcast_in_dim.71), calls=%async_computation.2 | async-start | bytes 262144 | tf_op jit(solution)/shard_map/cond/branch_1_fun/all_to_all | solution.py:208
  58.9 6.6 %branch_1_fun.3 = (bf16[1536,768]{1,0:T(8,128)(2,1)}, bf16[1536,768]{1,0:T(8,128)(2,1)}, bf16[1536,384]{1,0:T(8,128)(2,1)}) custom-call(s32[1]{0:T(128)} %get-tuple-element.28.first_ref, s32[6,128]{1,0:T(8,128)} %copy-done.2, bf16[1536,384]{1,0:T(8,128)(2,1)} %get-tuple-element.30.matrix_ref), custom_call_target="tpu_custom_call" | custom-call | flops 603979776 | bytes 6291456 | tf_op jit(solution)/shard_map/cond/branch_1_fun/pallas_call | solution.py:258
  66.0 2.1 %all-to-all-done.2 = bf16[8,64,128]{2,1,0:T(8,128)(2,1)} async-done(((bf16[8,64,128]{2,1,0:T(8,128)(2,1)}), bf16[8,64,128]{2,1,0:T(8,128)(2,1)}, u32[]{:S(2)}, u32[]{:S(2)}) %all-to-all-start.2) | async-done | bytes 131104 | tf_op jit(solution)/shard_map/cond/branch_1_fun/all_to_all | solution.py:208
  68.1 0.9 reduce_sum.23
  69.0 0.9 broadcast_in_dim.72
  69.9 7.4 %all-to-all-start.3 = ((bf16[32,64,128]{2,1,0:T(8,128)(2,1)}), bf16[32,64,128]{2,1,0:T(8,128)(2,1)}, u32[]{:S(2)}, u32[]{:S(2)}) async-start(bf16[32,64,128]{2,1,0:T(8,128)(2,1)} %broadcast_in_dim.72), calls=%async_computation.3 | async-start | bytes 1048576 | tf_op jit(solution)/shard_map/cond/branch_1_fun/all_to_all | solution.py:281
  77.4 1.9 %collective-permute-start.3 = (bf16[4,8,144,128]{3,2,1,0:T(8,128)(2,1)S(1)}, bf16[4,8,144,128]{3,2,1,0:T(8,128)(2,1)S(1)}, u32[]{:S(2)}, u32[]{:S(2)}) collective-permute-start(bf16[4,8,144,128]{3,2,1,0:T(8,128)(2,1)S(1)} %constant_dynamic-slice_fusion), channel_id=1, source_target_pairs={{0,1},{1,0},{2,3},{3,2},{4,5},{5,4},{6,7},{7,6},{8,9},{9,8},{10,11... | collective-permute-start | bytes 3538952 | tf_op jit(solution)/shard_map/cond/branch_1_fun/ppermute | solution.py:272
  79.3 2.0 %branch_1_fun.4 = bf16[256,3840]{1,0:T(8,128)(2,1)} custom-call(s32[6,128]{1,0:T(8,128)S(1)} %copy-done.3), custom_call_target="tpu_custom_call" | custom-call | flops 68719476736 | bytes 2097152 | tf_op jit(solution)/shard_map/cond/branch_1_fun/pallas_call | solution.py:273
  82.5 2.1 %copy.6 = bf16[6,8,4,2,24,128]{5,4,3,2,1,0:T(8,128)(2,1)} copy(bf16[6,8,4,2,24,128]{5,4,0,1,2,3:T(8,128)(2,1)S(1)} %maximum_bitcast_fusion) | data formatting | bytes 4718592 | tf_op jit(solution)/shard_map/cond/branch_1_fun/transpose | solution.py:285
  84.6 3.5 %branch_1_fun.5 = bf16[1536,768]{1,0:T(8,128)(2,1)S(1)} custom-call(s32[1]{0:T(128)} %get-tuple-element.28.first_ref, bf16[6,1536,128]{2,1,0:T(8,128)(2,1)} %bitcast.337, bf16[1536,768]{1,0:T(8,128)(2,1)} %get-tuple-element.39.live_ref), custom_call_target="tpu_custom_call" | custom-call | flops 301989888 | bytes 12582912 | tf_op jit(solution)/shard_map/cond/branch_1_fun/pallas_call | solution.py:286
  88.1 4.7 %all-to-all-done.3 = bf16[32,64,128]{2,1,0:T(8,128)(2,1)} async-done(((bf16[32,64,128]{2,1,0:T(8,128)(2,1)}), bf16[32,64,128]{2,1,0:T(8,128)(2,1)}, u32[]{:S(2)}, u32[]{:S(2)}) %all-to-all-start.3) | async-done | bytes 524320 | tf_op jit(solution)/shard_map/cond/branch_1_fun/all_to_all | solution.py:281
  92.7 2.1 %collective-permute-start.4 = (bf16[32,64,128]{2,1,0:T(8,128)(2,1)}, bf16[32,64,128]{2,1,0:T(8,128)(2,1)}, u32[]{:S(2)}, u32[]{:S(2)}) collective-permute-start(bf16[32,64,128]{2,1,0:T(8,128)(2,1)} %all-to-all-done.3), channel_id=1, source_target_pairs={{0,1},{1,0},{2,3},{3,2},{4,5},{5,4},{6,7},{7,6},{8,9},{9,8},{10,11... | collective-permute-start | bytes 1572872 | tf_op jit(solution)/shard_map/cond/branch_1_fun/ppermute | solution.py:294
  94.8 2.0 %collective-permute-done.4 = bf16[32,64,128]{2,1,0:T(8,128)(2,1)} collective-permute-done((bf16[32,64,128]{2,1,0:T(8,128)(2,1)}, bf16[32,64,128]{2,1,0:T(8,128)(2,1)}, u32[]{:S(2)}, u32[]{:S(2)}) %collective-permute-start.4) | collective-permute-done | bytes 524320 | tf_op jit(solution)/shard_map/cond/branch_1_fun/ppermute | solution.py:294
  97.5 8.2 %shard_map.47 = bf16[1536,384]{1,0:T(8,128)(2,1)} custom-call(s32[1]{0:T(128)} %bitcast.32.core_ref, bf16[2,768,384]{2,1,0:T(8,128)(2,1)} %all-reduce.2.cloned.1.call-done.content_hbm, bf16[32,64,128]{2,1,0:T(8,128)(2,1)} %get-tuple-element.55.mine_hbm, bf16[32,64,128]{2,1,0:T(8,128)(2,1)} %get-tuple-element.56.other_hbm, f32[6,128,128]{2,1,0:T(8,128)} %inverses_hbm.1, ...), custom_call_target="tpu_custom_call" | custom-call | flops 1811939328 | bytes 16777216 | tf_op jit(solution)/shard_map/pallas_call | solution.py:303
  (67 shorter events, 5.7 us)
Async XLA Ops:
  6.5 4.3 %copy-start.1 = (s32[6,128]{1,0:T(8,128)S(1)}, s32[6,128]{1,0:T(8,128)}, u32[]{:S(2)}) copy-start(s32[6,128]{1,0:T(8,128)} %rows_ref.1) | copy-start | bytes 9220
  6.5 4.3 %copy-start = (bf16[6,24,128]{2,1,0:T(8,128)(2,1)S(1)}, bf16[6,24,128]{2,1,0:T(8,128)(2,1)}, u32[]{:S(2)}) copy-start(bf16[6,24,128]{2,1,0:T(8,128)(2,1)} %param.7) | copy-start | bytes 110596
  6.5 90.9 %all-reduce.2.cloned.1.call-start = ((), (), s32[]{:S(2)}) async-start(), calls=%async_computation.4 | async-start | bytes 2359296 | tf_op jit(solution)/shard_map/psum | solution.py:235
  10.8 37.4 %copy-start.2 = (s32[6,128]{1,0:T(8,128)}, s32[6,128]{1,0:T(8,128)S(1)}, u32[]{:S(2)}) copy-start(s32[6,128]{1,0:T(8,128)S(1)} %get-tuple-element.37.rows_ref) | copy-start | bytes 9220 | tf_op jit(solution)/shard_map/cond
  11.6 22.9 %all-to-all-start = ((bf16[8,144,128]{2,1,0:T(8,128)(2,1)}), bf16[8,144,128]{2,1,0:T(8,128)(2,1)S(1)}, u32[]{:S(2)}, u32[]{:S(2)}) async-start(bf16[8,144,128]{2,1,0:T(8,128)(2,1)} %broadcast_in_dim.68), calls=%async_computation | async-start | bytes 589824 | tf_op jit(solution)/shard_map/cond/branch_1_fun/all_to_all | solution.py:208
  36.7 13.5 %all-to-all-start.1 = ((bf16[8,64,128]{2,1,0:T(8,128)(2,1)}), bf16[8,64,128]{2,1,0:T(8,128)(2,1)}, u32[]{:S(2)}, u32[]{:S(2)}) async-start(bf16[8,64,128]{2,1,0:T(8,128)(2,1)} %select_select_fusion), calls=%async_computation.1 | async-start | bytes 262144 | tf_op jit(solution)/shard_map/cond/branch_1_fun/all_to_all | solution.py:254
  41.5 24.2 %collective-permute-start.2 = (bf16[8,144,128]{2,1,0:T(8,128)(2,1)S(1)}, bf16[8,144,128]{2,1,0:T(8,128)(2,1)S(1)}, u32[]{:S(2)}, u32[]{:S(2)}) collective-permute-start(bf16[8,144,128]{2,1,0:T(8,128)(2,1)S(1)} %all-to-all-done), channel_id=1, source_target_pairs={{6,0},{0,2},{2,4},{4,6},{7,1},{1,3},{3,5},{5,7},{14,8},{8,10},{10,... | collective-permute-start | bytes 884744 | tf_op jit(solution)/shard_map/cond/branch_1_fun/ppermute | solution.py:268
  43.4 22.2 %collective-permute-start.1 = (bf16[8,144,128]{2,1,0:T(8,128)(2,1)S(1)}, bf16[8,144,128]{2,1,0:T(8,128)(2,1)S(1)}, u32[]{:S(2)}, u32[]{:S(2)}) collective-permute-start(bf16[8,144,128]{2,1,0:T(8,128)(2,1)S(1)} %all-to-all-done), channel_id=1, source_target_pairs={{4,0},{6,2},{0,4},{2,6},{5,1},{7,3},{1,5},{3,7},{12,8},{14,10},{8,... | collective-permute-start | bytes 884744 | tf_op jit(solution)/shard_map/cond/branch_1_fun/ppermute | solution.py:268
  48.2 17.3 %collective-permute-start = (bf16[8,144,128]{2,1,0:T(8,128)(2,1)S(1)}, bf16[8,144,128]{2,1,0:T(8,128)(2,1)S(1)}, u32[]{:S(2)}, u32[]{:S(2)}) collective-permute-start(bf16[8,144,128]{2,1,0:T(8,128)(2,1)S(1)} %all-to-all-done), channel_id=1, source_target_pairs={{2,0},{4,2},{6,4},{0,6},{3,1},{5,3},{7,5},{1,7},{10,8},{12,10},{14... | collective-permute-start | bytes 884744 | tf_op jit(solution)/shard_map/cond/branch_1_fun/ppermute | solution.py:268
  51.8 16.3 %all-to-all-start.2 = ((bf16[8,64,128]{2,1,0:T(8,128)(2,1)}), bf16[8,64,128]{2,1,0:T(8,128)(2,1)}, u32[]{:S(2)}, u32[]{:S(2)}) async-start(bf16[8,64,128]{2,1,0:T(8,128)(2,1)} %broadcast_in_dim.71), calls=%async_computation.2 | async-start | bytes 262144 | tf_op jit(solution)/shard_map/cond/branch_1_fun/all_to_all | solution.py:208
  65.8 13.5 %copy-start.3 = (s32[6,128]{1,0:T(8,128)S(1)}, s32[6,128]{1,0:T(8,128)}, u32[]{:S(2)}) copy-start(s32[6,128]{1,0:T(8,128)} %copy-done.2) | copy-start | bytes 9220 | tf_op jit(solution)/shard_map/cond
  69.9 22.8 %all-to-all-start.3 = ((bf16[32,64,128]{2,1,0:T(8,128)(2,1)}), bf16[32,64,128]{2,1,0:T(8,128)(2,1)}, u32[]{:S(2)}, u32[]{:S(2)}) async-start(bf16[32,64,128]{2,1,0:T(8,128)(2,1)} %broadcast_in_dim.72), calls=%async_computation.3 | async-start | bytes 1048576 | tf_op jit(solution)/shard_map/cond/branch_1_fun/all_to_all | solution.py:281
  77.4 4.7 %collective-permute-start.3 = (bf16[4,8,144,128]{3,2,1,0:T(8,128)(2,1)S(1)}, bf16[4,8,144,128]{3,2,1,0:T(8,128)(2,1)S(1)}, u32[]{:S(2)}, u32[]{:S(2)}) collective-permute-start(bf16[4,8,144,128]{3,2,1,0:T(8,128)(2,1)S(1)} %constant_dynamic-slice_fusion), channel_id=1, source_target_pairs={{0,1},{1,0},{2,3},{3,2},{4,5},{5,4},{6,7},{7,6},{8,9},{9,8},{10,11... | collective-permute-start | bytes 3538952 | tf_op jit(solution)/shard_map/cond/branch_1_fun/ppermute | solution.py:272
  92.7 4.1 %collective-permute-start.4 = (bf16[32,64,128]{2,1,0:T(8,128)(2,1)}, bf16[32,64,128]{2,1,0:T(8,128)(2,1)}, u32[]{:S(2)}, u32[]{:S(2)}) collective-permute-start(bf16[32,64,128]{2,1,0:T(8,128)(2,1)} %all-to-all-done.3), channel_id=1, source_target_pairs={{0,1},{1,0},{2,3},{3,2},{4,5},{5,4},{6,7},{7,6},{8,9},{9,8},{10,11... | collective-permute-start | bytes 1572872 | tf_op jit(solution)/shard_map/cond/branch_1_fun/ppermute | solution.py:294
Sparse Core Ops, SparseCore 0:
  10.9 86.5 all-reduce.1
